TPU v7x, 256 devices: a whole 4x4x8 slice. The times are simulated.
256 devices in a mesh: lon: 64 (over x, y_lo, z), lat: 4 (over y_hi, core).
Axes of the slice: x: 4, y: 4 (y_hi: 2, y_lo: 2; y = y_hi * 2 + y_lo), z: 8, core: 2. Of those that a mesh axis runs over, the one named last changes fastest.
Arguments:
- conditions: bfloat16 [80, 64, 8192], P(None, 'lat', 'lon'), may hold values from -6 to 6
- noisy_state: float32 [1, 80, 64, 8192], P(None, None, 'lat', 'lon'), may hold values from -6 to 6
- noise_level: float32 [1], replicated, may hold values from 0.25 to 1
- kernel_input: bfloat16 [9, 128, 80], replicated, may hold values from -0.21875 to 0.21875
- kernel_coarse: bfloat16 [9, 256, 128], replicated, may hold values from -0.1875 to 0.1875
- kernel_deeper: bfloat16 [9, 256, 256], replicated, may hold values from -0.125 to 0.125
- guide_weight: bfloat16 [128, 256], replicated, may hold values from -0.375 to 0.375
- time_scale: float32 [128], replicated, may hold values from -9 to 9
- time_shift: float32 [128], replicated, may hold values from -3 to 3
- kernel_noisy: bfloat16 [9, 128, 80], replicated, may hold values from -0.21875 to 0.21875
- kernel_block: bfloat16 [9, 128, 128], replicated, may hold values from -0.1875 to 0.1875
- kernel_branch: bfloat16 [9, 128, 128], replicated, may hold values from -0.1875 to 0.1875
- kernel_output: bfloat16 [9, 80, 128], replicated, may hold values from -0.1875 to 0.1875
Outputs:
- denoised: float32 [1, 80, 64, 8192], P(None, None, 'lat', 'lon')
All inputs are finite; a program needn't handle non-finite values.
Results may differ from a plain program's by a relative error of at most 0.0075.
Values may be sent and summed in bfloat16 or wider, within the bound.
No kernel may reach another device: no remote copies, remote signals or barrier semaphores. Data moves between devices by JAX's collectives and lax.ppermute only.
A program may use at most 64 MiB of HBM per device.

v0:
```python
import functools

import jax
import jax.numpy as jnp
from jax import lax
from jax.experimental import pallas as pl
from jax.experimental.pallas import tpu as pltpu
from jax.sharding import PartitionSpec as P

F32 = jnp.float32
BF16 = jnp.bfloat16
PITCH = 80
EDGE = 8
ROWS = 16
PAIRS = 64
CH = 80
DEEP = 9
THIN = 4
VMEM = pltpu.VMEM
AXES = ("lon", "lat")


def swap_pairs(mesh_shape, lat, lon):
    n_lon, n_lat = mesh_shape
    pairs = []
    for o in range(n_lon):
        for a in range(n_lat):
            b, p = a, o
            if lat:
                b = a ^ 1 if lat == "A" else a - 1 + 2 * (a % 2)
            if lon:
                p = (o ^ 1 if lon == "A" else o - 1 + 2 * (o % 2)) % n_lon
            if 0 <= b < n_lat:
                pairs.append((o * n_lat + a, p * n_lat + b))
    return pairs


def silu(v):
    h = v * 0.5
    return h + h * jnp.tanh(h)


def matmul_nt(x, w):
    return lax.dot_general(x, w, (((1,), (1,)), ((), ())), preferred_element_type=F32)


def prep_body(scal, cond, state, own_c, own_s, edge_a, edge_b, lat_a, lat_b, work):
    lon_even = scal[6] > 0.5
    lat_even = scal[7] > 0.5
    work[...] = cond[...].astype(F32)
    row = lax.broadcasted_iota(jnp.int32, (128, 128), 0)
    col = lax.broadcasted_iota(jnp.int32, (128, 128), 1)
    pick = (col == jnp.where(row < PAIRS, 2 * row, 2 * (row - PAIRS) + 1)).astype(BF16)
    blank = jnp.zeros((128 - CH, 128), BF16)
    slot = lax.broadcasted_iota(jnp.int32, (8, 128), 0)
    for i in range(ROWS):
        c_row = work[pl.ds(i, CH, stride=ROWS), :].astype(BF16)
        s_row = (scal[0] * state[pl.ds(i, CH, stride=ROWS), :]).astype(BF16)
        both = matmul_nt(pick, jnp.concatenate([c_row, blank, s_row, blank], 0))
        c_pair = jnp.concatenate([both[:PAIRS, :128], both[PAIRS:, :128]], 1)
        s_pair = jnp.concatenate([both[:PAIRS, 128:], both[PAIRS:, 128:]], 1)
        own_c[i] = c_pair.astype(BF16)
        own_s[i] = s_pair.astype(BF16)
        for half in range(2):
            lanes = slice(128 * half, 128 * half + 128)
            left = jnp.where(slot < 5, c_pair[:8, lanes], pltpu.roll(s_pair[:8, lanes], 5, 0))
            right = jnp.where(slot > 2, c_pair[-8:, lanes], pltpu.roll(s_pair[-8:, lanes], 3, 0))
            edge_a[i, :, lanes] = jnp.where(lon_even, right, left).astype(BF16)
            edge_b[i, :, lanes] = jnp.where(lon_even, left, right).astype(BF16)
    lane = lax.broadcasted_iota(jnp.int32, (PAIRS, 128), 1)
    free = 128 - CH
    for k in range(DEEP):
        for half in range(2):
            lanes = slice(128 * half, 128 * half + 128)
            rows = []
            for first, s_first in ((0, 0), (ROWS - DEEP, ROWS - THIN)):
                value = own_c[first + k, :, lanes].astype(F32)
                n = 2 * k + half
                if n < 4 * THIN:
                    r, h = divmod(n // 2, 2)
                    part = own_s[s_first + r, :, 128 * h : 128 * h + 128].astype(F32)
                    part = pltpu.roll(part, (CH - free * (n % 2)) % 128, 1)
                    value = jnp.where(lane < CH, value, part)
                rows.append(value)
            lat_a[k, :, lanes] = jnp.where(lat_even, rows[1], rows[0]).astype(BF16)
            lat_b[k, :, lanes] = jnp.where(lat_even, rows[0], rows[1]).astype(BF16)


def prep(scal, cond, state):
    vm = pl.BlockSpec(memory_space=VMEM)
    own = jax.ShapeDtypeStruct((ROWS, PAIRS, 256), BF16)
    edge = jax.ShapeDtypeStruct((ROWS, 8, 256), BF16)
    rows = jax.ShapeDtypeStruct((DEEP, PAIRS, 256), BF16)
    return pl.pallas_call(
        prep_body,
        out_shape=(own, own, edge, edge, rows, rows),
        in_specs=[pl.BlockSpec(memory_space=pltpu.SMEM), vm, vm],
        out_specs=[vm] * 6,
        scratch_shapes=[VMEM((CH * ROWS, 128), F32)],
        name="prep",
    )(scal, cond, state)


def pair_weights(w, di):
    k0, k1, k2 = w[3 * di], w[3 * di + 1], w[3 * di + 2]
    z = jnp.zeros_like(k0)
    c = jnp.concatenate
    return c([c([k1, k2], 1), c([k0, k1], 1), c([z, k0], 1), c([k2, z], 1)], 0)


def pair_conv(x, w, centre, rows):
    span = rows * PITCH
    taps = [x[(centre + d - 1) * PITCH : (centre + d - 1) * PITCH + span, :] for d in range(3)]
    weights = jnp.concatenate([pair_weights(w, d) for d in range(3)], 1)
    y = matmul_nt(jnp.concatenate(taps, 1), weights)
    even = y[:, 0:128] + pltpu.roll(y[:, 256:384], 1, 0)
    odd = y[:, 128:256] + pltpu.roll(y[:, 384:512], span - 1, 0)
    return even, odd


def half_conv(x, w, centre, rows):
    span = rows * PITCH
    c = jnp.concatenate
    taps = c([x[(centre + d - 1) * PITCH : (centre + d - 1) * PITCH + span, :] for d in range(3)], 1)
    weights = c([c([w[3 * d + b] for d in range(3)], 1) for b in range(3)], 0)
    y = matmul_nt(taps, weights)
    n = y.shape[1] // 3
    return y[:, n : 2 * n] + pltpu.roll(y[:, :n], 1, 0) + pltpu.roll(y[:, 2 * n :], span - 1, 0)


def net_body(
    scal, own_c, own_s, edge_a, edge_b, lat_a, lat_b, corner_a, corner_b, state,
    k_in, k_coarse, k_deeper, guide_w, scale, shift, k_noisy, k_block, k_branch, k_out,
    out, x_c, x_s, w_in, w_noisy, w_out, pooled, middle, guide, hidden, inner, mixed, turn,
):
    top = scal[4]
    bottom = scal[5]
    lon_even = scal[6] > 0.5
    lat_even = scal[7] > 0.5
    free = 128 - CH
    for tap in range(9):
        for src, dst in ((k_in, w_in), (k_noisy, w_noisy)):
            dst[tap, :, CH:] = jnp.zeros((128, free), BF16)
            dst[tap, :, :CH] = src[tap]
        w_out[tap, CH:, :] = jnp.zeros((free, 128), BF16)
        w_out[tap, :CH, :] = k_out[tap]

    slot = lax.broadcasted_iota(jnp.int32, (8, 256), 0)
    lane = lax.broadcasted_iota(jnp.int32, (1, 128), 1)

    def put(c_row, s_row, left, right, middle_c, middle_s):
        x_c[c_row * PITCH : c_row * PITCH + 8, :] = jnp.where(slot > 2, left, 0.0).astype(BF16)
        x_c[c_row * PITCH + 8 : c_row * PITCH + 72, :] = middle_c
        x_c[c_row * PITCH + 72 : c_row * PITCH + 80, :] = jnp.where(slot < 5, right, 0.0).astype(BF16)
        if s_row is not None:
            s_left = jnp.where(slot > 5, pltpu.roll(left, 5, 0), 0.0)
            s_right = jnp.where(slot < 2, pltpu.roll(right, 3, 0), 0.0)
            x_s[s_row * PITCH : s_row * PITCH + 8, :] = s_left.astype(BF16)
            x_s[s_row * PITCH + 8 : s_row * PITCH + 72, :] = middle_s
            x_s[s_row * PITCH + 72 : s_row * PITCH + 80, :] = s_right.astype(BF16)

    for i in range(ROWS):
        a, b = edge_a[i].astype(F32), edge_b[i].astype(F32)
        put(DEEP + i, THIN + i, jnp.where(lon_even, b, a), jnp.where(lon_even, a, b), own_c[i], own_s[i])
    for below in range(2):
        for k in range(DEEP):
            r = k - (DEEP - THIN) if not below else k
            s_row = r if not below else THIN + ROWS + k
            if not 0 <= r < THIN:
                s_row = None
            picks = []
            for half in range(2):
                lanes = slice(128 * half, 128 * half + 128)
                a, b = lat_a[k, :, lanes].astype(F32), lat_b[k, :, lanes].astype(F32)
                value = jnp.where(lat_even, a, b) if below else jnp.where(lat_even, b, a)
                picks.append(jnp.where(lane < CH, value, 0.0).astype(BF16))
            mid_s = None
            if s_row is not None:
                mids = []
                for h in range(2):
                    n = 2 * (2 * r + h)
                    parts = []
                    for m in (n, n + 1):
                        lanes = slice(128 * (m % 2), 128 * (m % 2) + 128)
                        a, b = lat_a[m // 2, :, lanes].astype(F32), lat_b[m // 2, :, lanes].astype(F32)
                        value = jnp.where(lat_even, a, b) if below else jnp.where(lat_even, b, a)
                        parts.append(pltpu.roll(value, (128 - CH + free * (m % 2)) % 128, 1))
                    mids.append(jnp.where(lane < free, parts[0], jnp.where(lane < CH, parts[1], 0.0)).astype(BF16))
                mid_s = jnp.concatenate(mids, 1)
            sides = []
            for side in range(2):
                pair = []
                for corner in (corner_a, corner_b):
                    pair.append(corner[side, k].astype(F32))
                sides.append(jnp.where(lat_even, pair[0], pair[1]) if below else jnp.where(lat_even, pair[1], pair[0]))
            row = DEEP + ROWS + k if below else k
            put(row, s_row, sides[0], sides[1], jnp.concatenate(picks, 1), mid_s)

    for ch in range(8):
        even, odd = pair_conv(x_c, w_in, 1 + 4 * ch, 4)
        both = silu(even).astype(BF16).astype(F32) + silu(odd).astype(BF16).astype(F32)
        both = both.reshape(2, 2, PITCH, 128)
        mean = (both[:, 0] + both[:, 1]) * 0.25
        if ch < 2 or ch > 5:
            mean = mean * (top if ch < 2 else bottom)
        pooled[2 * ch * PITCH : (2 * ch + 2) * PITCH, :] = mean.reshape(2 * PITCH, 128).astype(BF16)
    for ch in range(7):
        m = silu(half_conv(pooled, k_coarse, 1 + 2 * ch, 2))
        for q in range(2):
            row = 2 * ch + q
            v = m[q * PITCH : (q + 1) * PITCH]
            if row < 3 or row > 10:
                v = v * (top if row < 3 else bottom)
            middle[row * PITCH : (row + 1) * PITCH, :] = v.astype(BF16)
    embedded = scale[...] * scal[3] + shift[...]
    for ch in range(6):
        d = silu(half_conv(middle, k_deeper, 1 + 2 * ch, 2)).astype(BF16)
        guide[2 * ch * PITCH : (2 * ch + 2) * PITCH, :] = matmul_nt(d, guide_w[...]) + embedded
    for ch in range(11):
        even, odd = pair_conv(x_s, w_noisy, 1 + 2 * ch, 2)
        for q in range(2):
            row = 2 * ch + q
            g = guide[(row + 1) // 2 * PITCH : ((row + 1) // 2 + 1) * PITCH, :]
            for half, v in enumerate((even, odd)):
                v = silu(v[q * PITCH : (q + 1) * PITCH] + g)
                if row < 3 or row > 18:
                    v = v * (top if row < 3 else bottom)
                hidden[row * PITCH : (row + 1) * PITCH, 128 * half : 128 * half + 128] = v.astype(BF16)
    for ch in range(10):
        for half, v in enumerate(pair_conv(hidden, k_block, 1 + 2 * ch, 2)):
            v = silu(v)
            if ch in (0, 9):
                v = v * (top if ch == 0 else bottom)
            inner[2 * ch * PITCH : (2 * ch + 2) * PITCH, 128 * half : 128 * half + 128] = v.astype(BF16)
    for ch in range(9):
        h = hidden[(2 + 2 * ch) * PITCH : (4 + 2 * ch) * PITCH, :].astype(F32)
        for half, v in enumerate(pair_conv(inner, k_branch, 1 + 2 * ch, 2)):
            v = silu(v + h[:, 128 * half : 128 * half + 128])
            for q in range(2):
                row = 2 * ch + q
                u = v[q * PITCH : (q + 1) * PITCH]
                if row in (0, 17):
                    u = u * (top if row == 0 else bottom)
                mixed[row * PITCH : (row + 1) * PITCH, 128 * half : 128 * half + 128] = u.astype(BF16)
    for ch in range(8):
        even, odd = pair_conv(mixed, w_out, 1 + 2 * ch, 2)
        for q in range(2):
            row = 2 * ch + q
            at = q * PITCH + EDGE
            turn[row, pl.ds(0, PAIRS, stride=2), :] = even[at : at + PAIRS]
            turn[row, pl.ds(1, PAIRS, stride=2), :] = odd[at : at + PAIRS]
            head = turn[row].T[:CH]
            here = pl.ds(row, CH, stride=ROWS)
            out[here, :] = scal[1] * state[here, :] + scal[2] * head


def net(*args):
    vm = pl.BlockSpec(memory_space=VMEM)
    return pl.pallas_call(
        net_body,
        out_shape=jax.ShapeDtypeStruct((CH * ROWS, 128), F32),
        in_specs=[pl.BlockSpec(memory_space=pltpu.SMEM)] + [vm] * (len(args) - 1),
        out_specs=vm,
        scratch_shapes=[
            VMEM((34 * PITCH, 256), BF16),
            VMEM((24 * PITCH, 256), BF16),
            VMEM((9, 128, 128), BF16),
            VMEM((9, 128, 128), BF16),
            VMEM((9, 128, 128), BF16),
            VMEM((16 * PITCH, 128), BF16),
            VMEM((14 * PITCH, 256), BF16),
            VMEM((12 * PITCH, 128), F32),
            VMEM((22 * PITCH, 256), BF16),
            VMEM((20 * PITCH, 256), BF16),
            VMEM((18 * PITCH, 256), BF16),
            VMEM((ROWS, 128, 128), F32),
        ],
        compiler_params=pltpu.CompilerParams(vmem_limit_bytes=56 << 20),
        name="net",
    )(*args)


def on_device(
    mesh_shape,
    conditions,
    noisy_state,
    noise_level,
    kernel_input,
    kernel_coarse,
    kernel_deeper,
    guide_weight,
    time_scale,
    time_shift,
    kernel_noisy,
    kernel_block,
    kernel_branch,
    kernel_output,
):
    sigma = noise_level[0]
    variance = sigma * sigma + 0.25
    root = jnp.sqrt(variance)
    lon, lat = lax.axis_index("lon"), lax.axis_index("lat")
    flags = [lat > 0, lat < mesh_shape[1] - 1, lon % 2 == 0, lat % 2 == 0]
    scal = jnp.stack(
        [1.0 / root, 0.25 / variance, 0.5 * sigma / root, jnp.log(sigma) / 4.0] + [f.astype(F32) for f in flags]
    )
    cond = conditions.reshape(CH * ROWS, 128)
    state = noisy_state.reshape(CH * ROWS, 128)
    own_c, own_s, edge_a, edge_b, lat_a, lat_b = prep(scal, cond, state)
    permute = lambda value, a, o: lax.ppermute(value, AXES, swap_pairs(mesh_shape, a, o))
    edge_a = permute(edge_a, None, "A")
    edge_b = permute(edge_b, None, "B")
    lat_a = permute(lat_a, "A", None)
    lat_b = permute(lat_b, "B", None)
    lon_even, lat_even = scal[6] > 0.5, scal[7] > 0.5
    sides = jnp.stack([jnp.where(lon_even, edge_b, edge_a), jnp.where(lon_even, edge_a, edge_b)])
    first, last = sides[:, :DEEP], sides[:, ROWS - DEEP :]
    corner_a = permute(jnp.where(lat_even, last, first), "A", None)
    corner_b = permute(jnp.where(lat_even, first, last), "B", None)
    out = net(
        scal, own_c, own_s, edge_a, edge_b, lat_a, lat_b, corner_a, corner_b, state,
        kernel_input, kernel_coarse, kernel_deeper, guide_weight, time_scale[None], time_shift[None],
        kernel_noisy, kernel_block, kernel_branch, kernel_output,
    )
    return out.reshape(noisy_state.shape)


def solution(mesh):
    tile = P(None, "lat", "lon")
    member = P(None, None, "lat", "lon")
    return jax.shard_map(
        functools.partial(on_device, (mesh.shape["lon"], mesh.shape["lat"])),
        mesh=mesh,
        in_specs=(tile, member) + (P(),) * 11,
        out_specs=member,
        check_vma=False,
    )
```

profile of v0, /device:TPU:1, one launch (start us, length us, event | category | flops | bytes accessed | tf_op | source)
XLA Modules:
  0.0 49.9 jit_solution(1796923730973097355)
XLA Ops:
  0.0 0.0 copy-start.4
  0.0 0.0 copy-start.5
  0.9 0.6 %stack.40.scal = f32[8]{0:T(128)} concatenate(f32[1]{0:T(128)S(6)} %div.15, f32[1]{0:T(128)S(6)} %div.16, f32[1]{0:T(128)S(6)} %div.17, f32[1]{0:T(128)S(6)} %div.18, f32[1]{0:T(128)} %bitcast, f32[1]{0:T(128)} %bitcast.1, f32[1]{0:T(128)} %bitcast.2, f32[1]{0:T(128)} %bitcast.3), dimensions={0} | concatenate | bytes 64 | tf_op jit(solution)/shard_map/stack | solution.py:304
  1.5 3.2 %prep.1 = (bf16[16,64,256]{2,1,0:T(8,128)(2,1)}, bf16[16,64,256]{2,1,0:T(8,128)(2,1)}, bf16[16,8,256]{2,1,0:T(8,128)(2,1)}, bf16[16,8,256]{2,1,0:T(8,128)(2,1)},...) custom-call(f32[8]{0:T(128)} %stack.40.scal, bf16[1280,128]{1,0:T(8,128)(2,1)} %bitcast.15, f32[1280,128]{1,0:T(8,128)} %bitcast.13), custom_call_target="tpu_custom_call" | custom-call | tf_op jit(solution)/shard_map/prep/pallas_call | solution.py:94
  4.8 2.5 %collective-permute-start = (bf16[16,8,256]{2,1,0:T(8,128)(2,1)}, bf16[16,8,256]{2,1,0:T(8,128)(2,1)S(1)}, u32[]{:S(2)}, u32[]{:S(2)}) collective-permute-start(bf16[16,8,256]{2,1,0:T(8,128)(2,1)} %get-tuple-element.13), channel_id=1, source_target_pairs={{0,4},{1,5},{2,6},{3,7},{4,0},{5,1},{6,2},{7,3},{8,12},{9,13},{10,... | collective-permute-start | bytes 196616 | tf_op jit(solution)/shard_map/ppermute | solution.py:310
  7.2 7.9 %collective-permute-start.1 = (bf16[16,8,256]{2,1,0:T(8,128)(2,1)}, bf16[16,8,256]{2,1,0:T(8,128)(2,1)S(1)}, u32[]{:S(2)}, u32[]{:S(2)}) collective-permute-start(bf16[16,8,256]{2,1,0:T(8,128)(2,1)} %get-tuple-element.14), channel_id=1, source_target_pairs={{0,252},{1,253},{2,254},{3,255},{4,8},{5,9},{6,10},{7,11},{8,4},{9... | collective-permute-start | bytes 196616 | tf_op jit(solution)/shard_map/ppermute | solution.py:310
  15.1 1.2 %collective-permute-start.2 = (bf16[9,64,256]{2,1,0:T(8,128)(2,1)}, bf16[9,64,256]{2,1,0:T(8,128)(2,1)S(1)}, u32[]{:S(2)}, u32[]{:S(2)}) collective-permute-start(bf16[9,64,256]{2,1,0:T(8,128)(2,1)} %get-tuple-element.15), channel_id=1, source_target_pairs={{0,1},{1,0},{2,3},{3,2},{4,5},{5,4},{6,7},{7,6},{8,9},{9,8},{10,11... | collective-permute-start | bytes 884744 | tf_op jit(solution)/shard_map/ppermute | solution.py:310
  16.3 4.4 %collective-permute-start.3 = (bf16[9,64,256]{2,1,0:T(8,128)(2,1)}, bf16[9,64,256]{2,1,0:T(8,128)(2,1)S(1)}, u32[]{:S(2)}, u32[]{:S(2)}) collective-permute-start(bf16[9,64,256]{2,1,0:T(8,128)(2,1)} %get-tuple-element.16), channel_id=1, source_target_pairs={{1,2},{2,1},{5,6},{6,5},{9,10},{10,9},{13,14},{14,13},{17,18},{18,... | collective-permute-start | bytes 884744 | tf_op jit(solution)/shard_map/ppermute | solution.py:310
  20.8 0.0 collective-permute-done.edge_a
  20.8 0.0 copy-start.2
  20.8 0.0 collective-permute-done.1.edge_b
  20.8 0.0 copy-start.3
  20.8 2.6 %collective-permute-start.5 = (bf16[2,9,8,256]{3,2,1,0:T(8,128)(2,1)S(1)}, bf16[2,9,8,256]{3,2,1,0:T(8,128)(2,1)S(1)}, u32[]{:S(2)}, u32[]{:S(2)}) collective-permute-start(bf16[2,9,8,256]{3,2,1,0:T(8,128)(2,1)S(1)} %get-tuple-element.17), channel_id=1, source_target_pairs={{1,2},{2,1},{5,6},{6,5},{9,10},{10,9},{13,14},{14,13},{17,18},{18,... | collective-permute-start | bytes 221192 | tf_op jit(solution)/shard_map/ppermute | solution.py:310
  23.5 0.3 collective-permute-start.4
  23.8 0.0 copy-done.4
  23.8 0.9 %copy.14.k_in = bf16[9,128,80]{2,1,0:T(8,128)(2,1)} copy(bf16[9,128,80]{1,2,0:T(8,128)(2,1)S(1)} %copy-done.4) | data formatting | bytes 368640 | tf_op args[3]
  24.7 0.0 copy-done.5
  24.7 0.9 %copy.15.k_noisy = bf16[9,128,80]{2,1,0:T(8,128)(2,1)} copy(bf16[9,128,80]{1,2,0:T(8,128)(2,1)S(1)} %copy-done.5) | data formatting | bytes 368640 | tf_op args[9]
  25.6 2.4 %collective-permute-done.5.corner_b = bf16[2,9,8,256]{3,2,1,0:T(8,128)(2,1)S(1)} collective-permute-done((bf16[2,9,8,256]{3,2,1,0:T(8,128)(2,1)S(1)}, bf16[2,9,8,256]{3,2,1,0:T(8,128)(2,1)S(1)}, u32[]{:S(2)}, u32[]{:S(2)}) %collective-permute-start.5) | collective-permute-done | bytes 73760 | tf_op jit(solution)/shard_map/ppermute | solution.py:310
  28.0 0.0 copy-start.6
  28.0 0.0 collective-permute-done.4.corner_a
  28.0 0.0 collective-permute-done.2.lat_a
  28.0 0.0 copy-start
  28.0 0.0 collective-permute-done.3.lat_b
  28.1 0.0 copy-start.1
  28.1 0.0 copy-done.2
  28.1 0.0 copy-done.3
  28.1 0.6 %copy-done.6 = bf16[2,9,8,256]{3,2,1,0:T(8,128)(2,1)} copy-done((bf16[2,9,8,256]{3,2,1,0:T(8,128)(2,1)}, bf16[2,9,8,256]{3,2,1,0:T(8,128)(2,1)S(1)}, u32[]{:S(2)}) %copy-start.6) | copy-done | bytes 73752
  28.6 0.0 copy-done.7
  28.7 0.1 copy-done
  28.8 0.1 copy-done.1
  28.9 21.0 %net.1 = f32[1280,128]{1,0:T(8,128)} custom-call(f32[8]{0:T(128)} %stack.40.scal, bf16[16,64,256]{2,1,0:T(8,128)(2,1)} %get-tuple-element.11.own_c, bf16[16,64,256]{2,1,0:T(8,128)(2,1)} %get-tuple-element.12.own_s, bf16[16,8,256]{2,1,0:T(8,128)(2,1)} %copy-done.2, bf16[16,8,256]{2,1,0:T(8,128)(2,1)} %copy-done.3, bf16[9,64,256]{2,1,0:T(8,128)(2,1)} %copy-done, ...), custom_call_target="tpu_custom_call" | custom-call | tf_op jit(solution)/shard_map/net/pallas_call | solution.py:259
  (3 shorter events, 0.0 us)
Async XLA Ops:
  0.0 23.8 %copy-start.4 = (bf16[9,128,80]{1,2,0:T(8,128)(2,1)S(1)}, bf16[9,128,80]{1,2,0:T(8,128)(2,1)}, u32[]{:S(2)}) copy-start(bf16[9,128,80]{1,2,0:T(8,128)(2,1)} %param.16) | copy-start | bytes 552964
  0.0 24.7 %copy-start.5 = (bf16[9,128,80]{1,2,0:T(8,128)(2,1)S(1)}, bf16[9,128,80]{1,2,0:T(8,128)(2,1)}, u32[]{:S(2)}) copy-start(bf16[9,128,80]{1,2,0:T(8,128)(2,1)} %param.22) | copy-start | bytes 552964
  4.8 16.0 %collective-permute-start = (bf16[16,8,256]{2,1,0:T(8,128)(2,1)}, bf16[16,8,256]{2,1,0:T(8,128)(2,1)S(1)}, u32[]{:S(2)}, u32[]{:S(2)}) collective-permute-start(bf16[16,8,256]{2,1,0:T(8,128)(2,1)} %get-tuple-element.13), channel_id=1, source_target_pairs={{0,4},{1,5},{2,6},{3,7},{4,0},{5,1},{6,2},{7,3},{8,12},{9,13},{10,... | collective-permute-start | bytes 196616 | tf_op jit(solution)/shard_map/ppermute | solution.py:310
  7.2 13.6 %collective-permute-start.1 = (bf16[16,8,256]{2,1,0:T(8,128)(2,1)}, bf16[16,8,256]{2,1,0:T(8,128)(2,1)S(1)}, u32[]{:S(2)}, u32[]{:S(2)}) collective-permute-start(bf16[16,8,256]{2,1,0:T(8,128)(2,1)} %get-tuple-element.14), channel_id=1, source_target_pairs={{0,252},{1,253},{2,254},{3,255},{4,8},{5,9},{6,10},{7,11},{8,4},{9... | collective-permute-start | bytes 196616 | tf_op jit(solution)/shard_map/ppermute | solution.py:310
  15.1 12.9 %collective-permute-start.2 = (bf16[9,64,256]{2,1,0:T(8,128)(2,1)}, bf16[9,64,256]{2,1,0:T(8,128)(2,1)S(1)}, u32[]{:S(2)}, u32[]{:S(2)}) collective-permute-start(bf16[9,64,256]{2,1,0:T(8,128)(2,1)} %get-tuple-element.15), channel_id=1, source_target_pairs={{0,1},{1,0},{2,3},{3,2},{4,5},{5,4},{6,7},{7,6},{8,9},{9,8},{10,11... | collective-permute-start | bytes 884744 | tf_op jit(solution)/shard_map/ppermute | solution.py:310
  16.3 11.7 %collective-permute-start.3 = (bf16[9,64,256]{2,1,0:T(8,128)(2,1)}, bf16[9,64,256]{2,1,0:T(8,128)(2,1)S(1)}, u32[]{:S(2)}, u32[]{:S(2)}) collective-permute-start(bf16[9,64,256]{2,1,0:T(8,128)(2,1)} %get-tuple-element.16), channel_id=1, source_target_pairs={{1,2},{2,1},{5,6},{6,5},{9,10},{10,9},{13,14},{14,13},{17,18},{18,... | collective-permute-start | bytes 884744 | tf_op jit(solution)/shard_map/ppermute | solution.py:310
  20.8 7.3 %copy-start.2 = (bf16[16,8,256]{2,1,0:T(8,128)(2,1)}, bf16[16,8,256]{2,1,0:T(8,128)(2,1)S(1)}, u32[]{:S(2)}) copy-start(bf16[16,8,256]{2,1,0:T(8,128)(2,1)S(1)} %collective-permute-done.edge_a) | copy-start | bytes 196612
  20.8 7.3 %copy-start.3 = (bf16[16,8,256]{2,1,0:T(8,128)(2,1)}, bf16[16,8,256]{2,1,0:T(8,128)(2,1)S(1)}, u32[]{:S(2)}) copy-start(bf16[16,8,256]{2,1,0:T(8,128)(2,1)S(1)} %collective-permute-done.1.edge_b) | copy-start | bytes 196612
  20.8 7.2 %collective-permute-start.5 = (bf16[2,9,8,256]{3,2,1,0:T(8,128)(2,1)S(1)}, bf16[2,9,8,256]{3,2,1,0:T(8,128)(2,1)S(1)}, u32[]{:S(2)}, u32[]{:S(2)}) collective-permute-start(bf16[2,9,8,256]{3,2,1,0:T(8,128)(2,1)S(1)} %get-tuple-element.17), channel_id=1, source_target_pairs={{1,2},{2,1},{5,6},{6,5},{9,10},{10,9},{13,14},{14,13},{17,18},{18,... | collective-permute-start | bytes 221192 | tf_op jit(solution)/shard_map/ppermute | solution.py:310
  23.5 4.5 %collective-permute-start.4 = (bf16[2,9,8,256]{3,2,1,0:T(8,128)(2,1)S(1)}, bf16[2,9,8,256]{3,2,1,0:T(8,128)(2,1)S(1)}, u32[]{:S(2)}, u32[]{:S(2)}) collective-permute-start(bf16[2,9,8,256]{3,2,1,0:T(8,128)(2,1)S(1)} %get-tuple-element.18), channel_id=1, source_target_pairs={{0,1},{1,0},{2,3},{3,2},{4,5},{5,4},{6,7},{7,6},{8,9},{9,8},{10,11... | collective-permute-start | bytes 221192 | tf_op jit(solution)/shard_map/ppermute | solution.py:310
  28.0 0.6 %copy-start.6 = (bf16[2,9,8,256]{3,2,1,0:T(8,128)(2,1)}, bf16[2,9,8,256]{3,2,1,0:T(8,128)(2,1)S(1)}, u32[]{:S(2)}) copy-start(bf16[2,9,8,256]{3,2,1,0:T(8,128)(2,1)S(1)} %collective-permute-done.5.corner_b) | copy-start | bytes 221188
  28.0 0.7 %copy-start.7 = (bf16[2,9,8,256]{3,2,1,0:T(8,128)(2,1)}, bf16[2,9,8,256]{3,2,1,0:T(8,128)(2,1)S(1)}, u32[]{:S(2)}) copy-start(bf16[2,9,8,256]{3,2,1,0:T(8,128)(2,1)S(1)} %collective-permute-done.4.corner_a) | copy-start | bytes 221188
  28.0 0.8 %copy-start = (bf16[9,64,256]{2,1,0:T(8,128)(2,1)}, bf16[9,64,256]{2,1,0:T(8,128)(2,1)S(1)}, u32[]{:S(2)}) copy-start(bf16[9,64,256]{2,1,0:T(8,128)(2,1)S(1)} %collective-permute-done.2.lat_a) | copy-start | bytes 884740
  28.1 0.9 %copy-start.1 = (bf16[9,64,256]{2,1,0:T(8,128)(2,1)}, bf16[9,64,256]{2,1,0:T(8,128)(2,1)S(1)}, u32[]{:S(2)}) copy-start(bf16[9,64,256]{2,1,0:T(8,128)(2,1)S(1)} %collective-permute-done.3.lat_b) | copy-start | bytes 884740
where the time goes:
time: 50 us; the launch traced here: 49.9 us
  Pallas kernels  24.2 us (48%)
  starting transfers between devices  18.9 us (38%)
  local copies, waits for them, and re-layouts  3.26 us (7%)
  waiting for transfers between devices  2.44 us (5%)
  between operations  1.07 us (2%)
    pallas_call x1, Pallas kernels, net(): pl.pallas_call(net_body, out_shape=jax.ShapeDtypeStruct((CH * ROWS, 128),...  21 us
    ppermute x6, starting transfers between devices, on_device(): lax.ppermute(value, AXES, swap_pairs(mesh_shape, a, o))  18.9 us
    pallas_call x1, Pallas kernels, prep(): pl.pallas_call(prep_body, out_shape=(own, own, edge, edge, rows, rows), i...  3.21 us
    unnamed x18, local copies, waits for them, and re-layouts  2.65 us
    ppermute x6, waiting for transfers between devices, on_device(): lax.ppermute(value, AXES, swap_pairs(mesh_shape, a, o))  2.44 us
  transfers between devices with their start and end apart: 6, of which 1 were waited for; matrix products, arithmetic and copies ran while one was open for 4% of the time, Pallas kernels for 0%

commit v1 on v0

--- a/solution.py
+++ b/solution.py
@@ -44,9 +44,11 @@
     return lax.dot_general(x, w, (((1,), (1,)), ((), ())), preferred_element_type=F32)
 
 
-def prep_body(scal, cond, state, own_c, own_s, edge_a, edge_b, lat_a, lat_b, work):
-    lon_even = scal[6] > 0.5
-    lat_even = scal[7] > 0.5
+def prep_body(noise, cond, state, own_c, own_s, edge_a, edge_b, lat_a, lat_b, work):
+    lon_even = lax.axis_index("lon") % 2 == 0
+    lat_even = lax.axis_index("lat") % 2 == 0
+    sigma = jnp.full((1, 128), noise[0], F32)
+    scale_in = 1.0 / jnp.sqrt(sigma * sigma + 0.25)
     work[...] = cond[...].astype(F32)
     row = lax.broadcasted_iota(jnp.int32, (128, 128), 0)
     col = lax.broadcasted_iota(jnp.int32, (128, 128), 1)
@@ -55,7 +57,7 @@
     slot = lax.broadcasted_iota(jnp.int32, (8, 128), 0)
     for i in range(ROWS):
         c_row = work[pl.ds(i, CH, stride=ROWS), :].astype(BF16)
-        s_row = (scal[0] * state[pl.ds(i, CH, stride=ROWS), :]).astype(BF16)
+        s_row = (scale_in * state[pl.ds(i, CH, stride=ROWS), :]).astype(BF16)
         both = matmul_nt(pick, jnp.concatenate([c_row, blank, s_row, blank], 0))
         c_pair = jnp.concatenate([both[:PAIRS, :128], both[PAIRS:, :128]], 1)
         s_pair = jnp.concatenate([both[:PAIRS, 128:], both[PAIRS:, 128:]], 1)
@@ -86,7 +88,7 @@
             lat_b[k, :, lanes] = jnp.where(lat_even, rows[0], rows[1]).astype(BF16)
 
 
-def prep(scal, cond, state):
+def prep(noise, cond, state):
     vm = pl.BlockSpec(memory_space=VMEM)
     own = jax.ShapeDtypeStruct((ROWS, PAIRS, 256), BF16)
     edge = jax.ShapeDtypeStruct((ROWS, 8, 256), BF16)
@@ -97,8 +99,9 @@
         in_specs=[pl.BlockSpec(memory_space=pltpu.SMEM), vm, vm],
         out_specs=[vm] * 6,
         scratch_shapes=[VMEM((CH * ROWS, 128), F32)],
+        compiler_params=pltpu.CompilerParams(vmem_limit_bytes=12 << 20),
         name="prep",
-    )(scal, cond, state)
+    )(noise, cond, state)
 
 
 def pair_weights(w, di):
@@ -108,11 +111,22 @@
     return c([c([k1, k2], 1), c([k0, k1], 1), c([z, k0], 1), c([k2, z], 1)], 0)
 
 
-def pair_conv(x, w, centre, rows):
+def pair_weights_by_input(w, di):
+    k0, k1, k2 = w[3 * di], w[3 * di + 1], w[3 * di + 2]
+    z = jnp.zeros_like(k0)
+    c = jnp.concatenate
+    return c([c([k1, k0, z, k2], 1), c([k2, k1, k0, z], 1)], 0)
+
+
+def pair_conv(x, w, centre, rows, by_input=False):
     span = rows * PITCH
     taps = [x[(centre + d - 1) * PITCH : (centre + d - 1) * PITCH + span, :] for d in range(3)]
-    weights = jnp.concatenate([pair_weights(w, d) for d in range(3)], 1)
-    y = matmul_nt(jnp.concatenate(taps, 1), weights)
+    taps = jnp.concatenate(taps, 1)
+    if by_input:
+        weights = jnp.concatenate([pair_weights_by_input(w, d) for d in range(3)], 0)
+        y = jnp.dot(taps, weights, preferred_element_type=F32)
+    else:
+        y = matmul_nt(taps, jnp.concatenate([pair_weights(w, d) for d in range(3)], 1))
     even = y[:, 0:128] + pltpu.roll(y[:, 256:384], 1, 0)
     odd = y[:, 128:256] + pltpu.roll(y[:, 384:512], span - 1, 0)
     return even, odd
@@ -129,19 +143,26 @@
 
 
 def net_body(
-    scal, own_c, own_s, edge_a, edge_b, lat_a, lat_b, corner_a, corner_b, state,
+    n_lat,
+    noise, own_c, own_s, edge_a, edge_b, lat_a, lat_b, corner_a, corner_b, state,
     k_in, k_coarse, k_deeper, guide_w, scale, shift, k_noisy, k_block, k_branch, k_out,
     out, x_c, x_s, w_in, w_noisy, w_out, pooled, middle, guide, hidden, inner, mixed, turn,
 ):
-    top = scal[4]
-    bottom = scal[5]
-    lon_even = scal[6] > 0.5
-    lat_even = scal[7] > 0.5
+    lat = lax.axis_index("lat")
+    top = (lat > 0).astype(F32)
+    bottom = (lat < n_lat - 1).astype(F32)
+    lon_even = lax.axis_index("lon") % 2 == 0
+    lat_even = lat % 2 == 0
+    sigma = jnp.full((1, 128), noise[0], F32)
+    variance = sigma * sigma + 0.25
+    scale_skip = 0.25 / variance
+    scale_out = 0.5 * sigma / jnp.sqrt(variance)
+    noise_code = jnp.log(sigma) / 4.0
     free = 128 - CH
     for tap in range(9):
         for src, dst in ((k_in, w_in), (k_noisy, w_noisy)):
-            dst[tap, :, CH:] = jnp.zeros((128, free), BF16)
-            dst[tap, :, :CH] = src[tap]
+            dst[tap, CH:, :] = jnp.zeros((free, 128), BF16)
+            dst[tap, :CH, :] = src[tap]
         w_out[tap, CH:, :] = jnp.zeros((free, 128), BF16)
         w_out[tap, :CH, :] = k_out[tap]
 
@@ -197,7 +218,7 @@
             put(row, s_row, sides[0], sides[1], jnp.concatenate(picks, 1), mid_s)
 
     for ch in range(8):
-        even, odd = pair_conv(x_c, w_in, 1 + 4 * ch, 4)
+        even, odd = pair_conv(x_c, w_in, 1 + 4 * ch, 4, True)
         both = silu(even).astype(BF16).astype(F32) + silu(odd).astype(BF16).astype(F32)
         both = both.reshape(2, 2, PITCH, 128)
         mean = (both[:, 0] + both[:, 1]) * 0.25
@@ -212,12 +233,12 @@
             if row < 3 or row > 10:
                 v = v * (top if row < 3 else bottom)
             middle[row * PITCH : (row + 1) * PITCH, :] = v.astype(BF16)
-    embedded = scale[...] * scal[3] + shift[...]
+    embedded = scale[...] * noise_code + shift[...]
     for ch in range(6):
         d = silu(half_conv(middle, k_deeper, 1 + 2 * ch, 2)).astype(BF16)
         guide[2 * ch * PITCH : (2 * ch + 2) * PITCH, :] = matmul_nt(d, guide_w[...]) + embedded
     for ch in range(11):
-        even, odd = pair_conv(x_s, w_noisy, 1 + 2 * ch, 2)
+        even, odd = pair_conv(x_s, w_noisy, 1 + 2 * ch, 2, True)
         for q in range(2):
             row = 2 * ch + q
             g = guide[(row + 1) // 2 * PITCH : ((row + 1) // 2 + 1) * PITCH, :]
@@ -251,13 +272,13 @@
             turn[row, pl.ds(1, PAIRS, stride=2), :] = odd[at : at + PAIRS]
             head = turn[row].T[:CH]
             here = pl.ds(row, CH, stride=ROWS)
-            out[here, :] = scal[1] * state[here, :] + scal[2] * head
-
-
-def net(*args):
+            out[here, :] = scale_skip * state[here, :] + scale_out * head
+
+
+def net(n_lat, *args):
     vm = pl.BlockSpec(memory_space=VMEM)
     return pl.pallas_call(
-        net_body,
+        functools.partial(net_body, n_lat),
         out_shape=jax.ShapeDtypeStruct((CH * ROWS, 128), F32),
         in_specs=[pl.BlockSpec(memory_space=pltpu.SMEM)] + [vm] * (len(args) - 1),
         out_specs=vm,
@@ -275,7 +296,7 @@
             VMEM((18 * PITCH, 256), BF16),
             VMEM((ROWS, 128, 128), F32),
         ],
-        compiler_params=pltpu.CompilerParams(vmem_limit_bytes=56 << 20),
+        compiler_params=pltpu.CompilerParams(vmem_limit_bytes=24 << 20),
         name="net",
     )(*args)
 
@@ -296,31 +317,25 @@
     kernel_branch,
     kernel_output,
 ):
-    sigma = noise_level[0]
-    variance = sigma * sigma + 0.25
-    root = jnp.sqrt(variance)
-    lon, lat = lax.axis_index("lon"), lax.axis_index("lat")
-    flags = [lat > 0, lat < mesh_shape[1] - 1, lon % 2 == 0, lat % 2 == 0]
-    scal = jnp.stack(
-        [1.0 / root, 0.25 / variance, 0.5 * sigma / root, jnp.log(sigma) / 4.0] + [f.astype(F32) for f in flags]
-    )
+    lon_even, lat_even = lax.axis_index("lon") % 2 == 0, lax.axis_index("lat") % 2 == 0
     cond = conditions.reshape(CH * ROWS, 128)
     state = noisy_state.reshape(CH * ROWS, 128)
-    own_c, own_s, edge_a, edge_b, lat_a, lat_b = prep(scal, cond, state)
+    own_c, own_s, edge_a, edge_b, lat_a, lat_b = prep(noise_level, cond, state)
     permute = lambda value, a, o: lax.ppermute(value, AXES, swap_pairs(mesh_shape, a, o))
     edge_a = permute(edge_a, None, "A")
     edge_b = permute(edge_b, None, "B")
     lat_a = permute(lat_a, "A", None)
     lat_b = permute(lat_b, "B", None)
-    lon_even, lat_even = scal[6] > 0.5, scal[7] > 0.5
     sides = jnp.stack([jnp.where(lon_even, edge_b, edge_a), jnp.where(lon_even, edge_a, edge_b)])
     first, last = sides[:, :DEEP], sides[:, ROWS - DEEP :]
     corner_a = permute(jnp.where(lat_even, last, first), "A", None)
     corner_b = permute(jnp.where(lat_even, first, last), "B", None)
+    by_input = lambda kernel: kernel.transpose(0, 2, 1)
     out = net(
-        scal, own_c, own_s, edge_a, edge_b, lat_a, lat_b, corner_a, corner_b, state,
-        kernel_input, kernel_coarse, kernel_deeper, guide_weight, time_scale[None], time_shift[None],
-        kernel_noisy, kernel_block, kernel_branch, kernel_output,
+        mesh_shape[1],
+        noise_level, own_c, own_s, edge_a, edge_b, lat_a, lat_b, corner_a, corner_b, state,
+        by_input(kernel_input), kernel_coarse, kernel_deeper, guide_weight, time_scale[None], time_shift[None],
+        by_input(kernel_noisy), kernel_block, kernel_branch, kernel_output,
     )
     return out.reshape(noisy_state.shape)
 

time: 50 us -> 49.9 us (level)
  Pallas kernels: 24.2 us -> 18.5 us
  local copies, waits for them, and re-layouts: 3.26 us -> 7.07 us
  waiting for transfers between devices: 2.44 us -> 4.25 us
    unnamed x18 -> x26, local copies, waits for them, and re-layouts: 2.65 us -> 7.07 us
    pallas_call x1, Pallas kernels: 21 us -> 16.7 us  [net(): pl.pallas_call(functools.partial(net_body, n_lat), out_shape=jax.ShapeDty...]
    ppermute x6, waiting for transfers between devices: 2.44 us -> 4.25 us  [on_device(): lax.ppermute(value, AXES, swap_pairs(mesh_shape, a, o))]
    pallas_call x1, Pallas kernels: 3.21 us -> 1.76 us  [prep(): pl.pallas_call(prep_body, out_shape=(own, own, edge, edge, rows, rows), i...]
    another operation x1 -> x0, local copies, waits for them, and re-layouts: 0.61 us -> none  [on_device(): jnp.stack([1.0 / root, 0.25 / variance, 0.5 * sigma / root, jnp.log(sigma...]
  transfers between devices with their start and end apart: 6 -> 6, of which waited for: 1 -> 1; matrix products, arithmetic and copies ran while one was open for 4% -> 0% of each run, Pallas kernels for 0% -> 0%
where the time goes in v1:
time: 49.9 us; the launch traced here: 49.6 us
  starting transfers between devices  18.9 us (38%)
  Pallas kernels  18.5 us (37%)
  local copies, waits for them, and re-layouts  7.07 us (14%)
  waiting for transfers between devices  4.25 us (9%)
  between operations  0.84 us (2%)
    ppermute x6, starting transfers between devices, on_device(): lax.ppermute(value, AXES, swap_pairs(mesh_shape, a, o))  18.9 us
    pallas_call x1, Pallas kernels, net(): pl.pallas_call(functools.partial(net_body, n_lat), out_shape=jax.ShapeDty...  16.7 us
    unnamed x26, local copies, waits for them, and re-layouts  7.07 us
    ppermute x6, waiting for transfers between devices, on_device(): lax.ppermute(value, AXES, swap_pairs(mesh_shape, a, o))  4.25 us
    pallas_call x1, Pallas kernels, prep(): pl.pallas_call(prep_body, out_shape=(own, own, edge, edge, rows, rows), i...  1.76 us
  transfers between devices with their start and end apart: 6, of which 1 were waited for; matrix products, arithmetic and copies ran while one was open for 0% of the time, Pallas kernels for 0%

profile of v1, /device:TPU:1, one launch (start us, length us, event | category | flops | bytes accessed | tf_op | source)
XLA Modules:
  0.0 49.6 jit_solution(17305501011888050468)
XLA Ops:
  0.0 0.0 copy-start.12
  0.0 0.0 copy-start.11
  0.7 0.0 copy-start
  0.7 1.1 %copy-done = f32[1,80,16,128]{3,2,1,0:T(8,128)S(1)} copy-done((f32[1,80,16,128]{3,2,1,0:T(8,128)S(1)}, f32[1,80,16,128]{3,2,1,0:T(8,128)}, u32[]{:S(2)}) %copy-start) | copy-done | bytes 655384
  1.8 0.0 copy-start.4
  1.8 1.0 %copy-done.4 = bf16[80,16,128]{2,1,0:T(8,128)(2,1)S(1)} copy-done((bf16[80,16,128]{2,1,0:T(8,128)(2,1)S(1)}, bf16[80,16,128]{2,1,0:T(8,128)(2,1)}, u32[]{:S(2)}) %copy-start.4) | copy-done | bytes 327704
  2.8 1.8 %prep.1 = (bf16[16,64,256]{2,1,0:T(8,128)(2,1)S(1)}, bf16[16,64,256]{2,1,0:T(8,128)(2,1)S(1)}, bf16[16,8,256]{2,1,0:T(8,128)(2,1)S(1)}, bf16[16,8,256]{2,1,0:T(8...) custom-call(f32[1]{0:T(128)S(6)} %copy.14.noise, bf16[1280,128]{1,0:T(8,128)(2,1)S(1)} %bitcast.13, ...), custom_call_target="tpu_custom_call" | custom-call | tf_op jit(solution)/shard_map/prep/pallas_call | solution.py:96
  4.5 2.5 %collective-permute-start = (bf16[16,8,256]{2,1,0:T(8,128)(2,1)S(1)}, bf16[16,8,256]{2,1,0:T(8,128)(2,1)S(1)}, u32[]{:S(2)}, u32[]{:S(2)}) collective-permute-start(bf16[16,8,256]{2,1,0:T(8,128)(2,1)S(1)} %get-tuple-element.13), channel_id=1, source_target_pairs={{0,4},{1,5},{2,6},{3,7},{4,0},{5,1},{6,2},{7,3},{8,12},{9,13},{10,... | collective-permute-start | bytes 196616 | tf_op jit(solution)/shard_map/ppermute | solution.py:324
  7.0 7.9 %collective-permute-start.1 = (bf16[16,8,256]{2,1,0:T(8,128)(2,1)S(1)}, bf16[16,8,256]{2,1,0:T(8,128)(2,1)S(1)}, u32[]{:S(2)}, u32[]{:S(2)}) collective-permute-start(bf16[16,8,256]{2,1,0:T(8,128)(2,1)S(1)} %get-tuple-element.14), channel_id=1, source_target_pairs={{0,252},{1,253},{2,254},{3,255},{4,8},{5,9},{6,10},{7,11},{8,4},{9... | collective-permute-start | bytes 196616 | tf_op jit(solution)/shard_map/ppermute | solution.py:324
  14.9 1.2 %collective-permute-start.2 = (bf16[9,64,256]{2,1,0:T(8,128)(2,1)}, bf16[9,64,256]{2,1,0:T(8,128)(2,1)S(1)}, u32[]{:S(2)}, u32[]{:S(2)}) collective-permute-start(bf16[9,64,256]{2,1,0:T(8,128)(2,1)} %get-tuple-element.15), channel_id=1, source_target_pairs={{0,1},{1,0},{2,3},{3,2},{4,5},{5,4},{6,7},{7,6},{8,9},{9,8},{10,11... | collective-permute-start | bytes 884744 | tf_op jit(solution)/shard_map/ppermute | solution.py:324
  16.1 4.4 %collective-permute-start.3 = (bf16[9,64,256]{2,1,0:T(8,128)(2,1)}, bf16[9,64,256]{2,1,0:T(8,128)(2,1)S(1)}, u32[]{:S(2)}, u32[]{:S(2)}) collective-permute-start(bf16[9,64,256]{2,1,0:T(8,128)(2,1)} %get-tuple-element.16), channel_id=1, source_target_pairs={{1,2},{2,1},{5,6},{6,5},{9,10},{10,9},{13,14},{14,13},{17,18},{18,... | collective-permute-start | bytes 884744 | tf_op jit(solution)/shard_map/ppermute | solution.py:324
  20.5 0.0 collective-permute-done.edge_a
  20.5 0.0 collective-permute-done.1.edge_b
  20.6 2.6 %collective-permute-start.5 = (bf16[2,9,8,256]{3,2,1,0:T(8,128)(2,1)S(1)}, bf16[2,9,8,256]{3,2,1,0:T(8,128)(2,1)S(1)}, u32[]{:S(2)}, u32[]{:S(2)}) collective-permute-start(bf16[2,9,8,256]{3,2,1,0:T(8,128)(2,1)S(1)} %get-tuple-element.17), channel_id=1, source_target_pairs={{1,2},{2,1},{5,6},{6,5},{9,10},{10,9},{13,14},{14,13},{17,18},{18,... | collective-permute-start | bytes 221192 | tf_op jit(solution)/shard_map/ppermute | solution.py:324
  23.3 0.3 collective-permute-start.4
  23.5 4.2 %collective-permute-done.5.corner_b = bf16[2,9,8,256]{3,2,1,0:T(8,128)(2,1)S(1)} collective-permute-done((bf16[2,9,8,256]{3,2,1,0:T(8,128)(2,1)S(1)}, bf16[2,9,8,256]{3,2,1,0:T(8,128)(2,1)S(1)}, u32[]{:S(2)}, u32[]{:S(2)}) %collective-permute-start.5) | collective-permute-done | bytes 73760 | tf_op jit(solution)/shard_map/ppermute | solution.py:324
  27.8 0.0 collective-permute-done.4.corner_a
  27.8 0.0 collective-permute-done.2.lat_a
  27.8 0.0 collective-permute-done.3.lat_b
  27.8 0.0 copy-done.12
  27.8 0.0 copy-done.11
  27.8 0.0 copy-done.1
  27.8 0.0 copy-done.3
  27.8 0.0 copy-done.5
  27.8 0.0 copy-done.10
  27.8 0.0 copy-start.2
  27.9 1.3 %copy-done.2 = bf16[9,256,256]{2,1,0:T(8,128)(2,1)S(1)} copy-done((bf16[9,256,256]{2,1,0:T(8,128)(2,1)S(1)}, bf16[9,256,256]{2,1,0:T(8,128)(2,1)}, u32[]{:S(2)}) %copy-start.2) | copy-done | bytes 1179672
  29.1 1.0 %copy-done.6 = bf16[9,128,128]{2,1,0:T(8,128)(2,1)S(1)} copy-done((bf16[9,128,128]{2,1,0:T(8,128)(2,1)S(1)}, bf16[9,128,128]{2,1,0:T(8,128)(2,1)}, u32[]{:S(2)}) %copy-start.6) | copy-done | bytes 294936
  30.1 0.9 %copy-done.7 = bf16[9,128,80]{1,2,0:T(8,128)(2,1)S(1)} copy-done((bf16[9,128,80]{1,2,0:T(8,128)(2,1)S(1)}, bf16[9,128,80]{1,2,0:T(8,128)(2,1)}, u32[]{:S(2)}) %copy-start.7) | copy-done | bytes 184344
  31.0 0.9 %copy-done.8 = bf16[9,128,80]{1,2,0:T(8,128)(2,1)S(1)} copy-done((bf16[9,128,80]{1,2,0:T(8,128)(2,1)S(1)}, bf16[9,128,80]{1,2,0:T(8,128)(2,1)}, u32[]{:S(2)}) %copy-start.8) | copy-done | bytes 184344
  31.9 0.9 %copy-done.9 = bf16[9,80,128]{2,1,0:T(8,128)(2,1)S(1)} copy-done((bf16[9,80,128]{2,1,0:T(8,128)(2,1)S(1)}, bf16[9,80,128]{2,1,0:T(8,128)(2,1)}, u32[]{:S(2)}) %copy-start.9) | copy-done | bytes 184344
  32.8 16.7 %net.1 = f32[1280,128]{1,0:T(8,128)} custom-call(f32[1]{0:T(128)S(6)} %copy.14.noise, bf16[16,64,256]{2,1,0:T(8,128)(2,1)S(1)} %get-tuple-element.11.own_c, bf16[16,64,256]{2,1,0:T(8,128)(2,1)S(1)} %get-tuple-element.12.own_s, bf16[16,8,256]{2,1,0:T(8,128)(2,1)S(1)} %collective-permute-done.edge_a, bf16[16,8,256]{2,1,0:T(8,128)(2,1)S(1)} %collective-permute-done.1.edge_b, ...), custom_call_target="tpu_custom_call" | custom-call | tf_op jit(solution)/shard_map/net/pallas_call | solution.py:280
  (10 shorter events, 0.0 us)
Async XLA Ops:
  0.0 27.8 %copy-start.12 = (f32[128]{0:T(128)S(1)}, f32[128]{0:T(128)}, u32[]{:S(2)}) copy-start(f32[128]{0:T(128)} %param.21) | copy-start | bytes 1540
  0.0 27.8 %copy-start.11 = (f32[128]{0:T(128)S(1)}, f32[128]{0:T(128)}, u32[]{:S(2)}) copy-start(f32[128]{0:T(128)} %param.20) | copy-start | bytes 1540
  0.7 1.1 %copy-start = (f32[1,80,16,128]{3,2,1,0:T(8,128)S(1)}, f32[1,80,16,128]{3,2,1,0:T(8,128)}, u32[]{:S(2)}) copy-start(f32[1,80,16,128]{3,2,1,0:T(8,128)} %param.14) | copy-start | bytes 1966084
  1.8 1.0 %copy-start.4 = (bf16[80,16,128]{2,1,0:T(8,128)(2,1)S(1)}, bf16[80,16,128]{2,1,0:T(8,128)(2,1)}, u32[]{:S(2)}) copy-start(bf16[80,16,128]{2,1,0:T(8,128)(2,1)} %param.13) | copy-start | bytes 983044
  2.7 25.1 %copy-start.1 = (f32[1,80,16,128]{3,2,1,0:T(8,128)S(1)}, f32[1,80,16,128]{3,2,1,0:T(8,128)}, u32[]{:S(2)}) copy-start(f32[1,80,16,128]{3,2,1,0:T(8,128)} %param.14) | copy-start | bytes 1966084
  2.7 25.1 %copy-start.3 = (bf16[9,256,128]{2,1,0:T(8,128)(2,1)S(1)}, bf16[9,256,128]{2,1,0:T(8,128)(2,1)}, u32[]{:S(2)}) copy-start(bf16[9,256,128]{2,1,0:T(8,128)(2,1)} %k_coarse.1) | copy-start | bytes 1769476
  2.8 25.1 %copy-start.5 = (bf16[9,128,128]{2,1,0:T(8,128)(2,1)S(1)}, bf16[9,128,128]{2,1,0:T(8,128)(2,1)}, u32[]{:S(2)}) copy-start(bf16[9,128,128]{2,1,0:T(8,128)(2,1)} %k_block.1) | copy-start | bytes 884740
  2.8 25.1 %copy-start.10 = (bf16[128,256]{1,0:T(8,128)(2,1)S(1)}, bf16[128,256]{1,0:T(8,128)(2,1)}, u32[]{:S(2)}) copy-start(bf16[128,256]{1,0:T(8,128)(2,1)} %guide_w.1) | copy-start | bytes 196612
  4.5 16.0 %collective-permute-start = (bf16[16,8,256]{2,1,0:T(8,128)(2,1)S(1)}, bf16[16,8,256]{2,1,0:T(8,128)(2,1)S(1)}, u32[]{:S(2)}, u32[]{:S(2)}) collective-permute-start(bf16[16,8,256]{2,1,0:T(8,128)(2,1)S(1)} %get-tuple-element.13), channel_id=1, source_target_pairs={{0,4},{1,5},{2,6},{3,7},{4,0},{5,1},{6,2},{7,3},{8,12},{9,13},{10,... | collective-permute-start | bytes 196616 | tf_op jit(solution)/shard_map/ppermute | solution.py:324
  7.0 13.6 %collective-permute-start.1 = (bf16[16,8,256]{2,1,0:T(8,128)(2,1)S(1)}, bf16[16,8,256]{2,1,0:T(8,128)(2,1)S(1)}, u32[]{:S(2)}, u32[]{:S(2)}) collective-permute-start(bf16[16,8,256]{2,1,0:T(8,128)(2,1)S(1)} %get-tuple-element.14), channel_id=1, source_target_pairs={{0,252},{1,253},{2,254},{3,255},{4,8},{5,9},{6,10},{7,11},{8,4},{9... | collective-permute-start | bytes 196616 | tf_op jit(solution)/shard_map/ppermute | solution.py:324
  14.9 12.9 %collective-permute-start.2 = (bf16[9,64,256]{2,1,0:T(8,128)(2,1)}, bf16[9,64,256]{2,1,0:T(8,128)(2,1)S(1)}, u32[]{:S(2)}, u32[]{:S(2)}) collective-permute-start(bf16[9,64,256]{2,1,0:T(8,128)(2,1)} %get-tuple-element.15), channel_id=1, source_target_pairs={{0,1},{1,0},{2,3},{3,2},{4,5},{5,4},{6,7},{7,6},{8,9},{9,8},{10,11... | collective-permute-start | bytes 884744 | tf_op jit(solution)/shard_map/ppermute | solution.py:324
  16.1 11.7 %collective-permute-start.3 = (bf16[9,64,256]{2,1,0:T(8,128)(2,1)}, bf16[9,64,256]{2,1,0:T(8,128)(2,1)S(1)}, u32[]{:S(2)}, u32[]{:S(2)}) collective-permute-start(bf16[9,64,256]{2,1,0:T(8,128)(2,1)} %get-tuple-element.16), channel_id=1, source_target_pairs={{1,2},{2,1},{5,6},{6,5},{9,10},{10,9},{13,14},{14,13},{17,18},{18,... | collective-permute-start | bytes 884744 | tf_op jit(solution)/shard_map/ppermute | solution.py:324
  20.6 7.2 %collective-permute-start.5 = (bf16[2,9,8,256]{3,2,1,0:T(8,128)(2,1)S(1)}, bf16[2,9,8,256]{3,2,1,0:T(8,128)(2,1)S(1)}, u32[]{:S(2)}, u32[]{:S(2)}) collective-permute-start(bf16[2,9,8,256]{3,2,1,0:T(8,128)(2,1)S(1)} %get-tuple-element.17), channel_id=1, source_target_pairs={{1,2},{2,1},{5,6},{6,5},{9,10},{10,9},{13,14},{14,13},{17,18},{18,... | collective-permute-start | bytes 221192 | tf_op jit(solution)/shard_map/ppermute | solution.py:324
  23.3 4.5 %collective-permute-start.4 = (bf16[2,9,8,256]{3,2,1,0:T(8,128)(2,1)S(1)}, bf16[2,9,8,256]{3,2,1,0:T(8,128)(2,1)S(1)}, u32[]{:S(2)}, u32[]{:S(2)}) collective-permute-start(bf16[2,9,8,256]{3,2,1,0:T(8,128)(2,1)S(1)} %get-tuple-element.18), channel_id=1, source_target_pairs={{0,1},{1,0},{2,3},{3,2},{4,5},{5,4},{6,7},{7,6},{8,9},{9,8},{10,11... | collective-permute-start | bytes 221192 | tf_op jit(solution)/shard_map/ppermute | solution.py:324
  27.8 1.3 %copy-start.2 = (bf16[9,256,256]{2,1,0:T(8,128)(2,1)S(1)}, bf16[9,256,256]{2,1,0:T(8,128)(2,1)}, u32[]{:S(2)}) copy-start(bf16[9,256,256]{2,1,0:T(8,128)(2,1)} %k_deeper.1) | copy-start | bytes 3538948
  29.1 1.0 %copy-start.6 = (bf16[9,128,128]{2,1,0:T(8,128)(2,1)S(1)}, bf16[9,128,128]{2,1,0:T(8,128)(2,1)}, u32[]{:S(2)}) copy-start(bf16[9,128,128]{2,1,0:T(8,128)(2,1)} %k_branch.1) | copy-start | bytes 884740
  30.1 0.9 %copy-start.7 = (bf16[9,128,80]{1,2,0:T(8,128)(2,1)S(1)}, bf16[9,128,80]{1,2,0:T(8,128)(2,1)}, u32[]{:S(2)}) copy-start(bf16[9,128,80]{1,2,0:T(8,128)(2,1)} %param.16) | copy-start | bytes 552964
  31.0 0.9 %copy-start.8 = (bf16[9,128,80]{1,2,0:T(8,128)(2,1)S(1)}, bf16[9,128,80]{1,2,0:T(8,128)(2,1)}, u32[]{:S(2)}) copy-start(bf16[9,128,80]{1,2,0:T(8,128)(2,1)} %param.22) | copy-start | bytes 552964
  31.9 0.9 %copy-start.9 = (bf16[9,80,128]{2,1,0:T(8,128)(2,1)S(1)}, bf16[9,80,128]{2,1,0:T(8,128)(2,1)}, u32[]{:S(2)}) copy-start(bf16[9,80,128]{2,1,0:T(8,128)(2,1)} %k_out.1) | copy-start | bytes 552964

commit v2 on v1

--- a/solution.py
+++ b/solution.py
@@ -44,17 +44,25 @@
     return lax.dot_general(x, w, (((1,), (1,)), ((), ())), preferred_element_type=F32)
 
 
-def prep_body(noise, cond, state, own_c, own_s, edge_a, edge_b, lat_a, lat_b, work):
+def prep_body(noise, cond_hbm, state_hbm, own_c, own_s, edge_a, edge_b, lat_a, lat_b, cond, state, work, arrived):
+    copies = [
+        pltpu.make_async_copy(cond_hbm, cond, arrived.at[0]),
+        pltpu.make_async_copy(state_hbm, state, arrived.at[1]),
+    ]
+    for copy in copies:
+        copy.start()
     lon_even = lax.axis_index("lon") % 2 == 0
     lat_even = lax.axis_index("lat") % 2 == 0
     sigma = jnp.full((1, 128), noise[0], F32)
     scale_in = 1.0 / jnp.sqrt(sigma * sigma + 0.25)
-    work[...] = cond[...].astype(F32)
     row = lax.broadcasted_iota(jnp.int32, (128, 128), 0)
     col = lax.broadcasted_iota(jnp.int32, (128, 128), 1)
     pick = (col == jnp.where(row < PAIRS, 2 * row, 2 * (row - PAIRS) + 1)).astype(BF16)
     blank = jnp.zeros((128 - CH, 128), BF16)
     slot = lax.broadcasted_iota(jnp.int32, (8, 128), 0)
+    for copy in copies:
+        copy.wait()
+    work[...] = cond[...].astype(F32)
     for i in range(ROWS):
         c_row = work[pl.ds(i, CH, stride=ROWS), :].astype(BF16)
         s_row = (scale_in * state[pl.ds(i, CH, stride=ROWS), :]).astype(BF16)
@@ -96,9 +104,14 @@
     return pl.pallas_call(
         prep_body,
         out_shape=(own, own, edge, edge, rows, rows),
-        in_specs=[pl.BlockSpec(memory_space=pltpu.SMEM), vm, vm],
+        in_specs=[pl.BlockSpec(memory_space=pltpu.SMEM)] + [pl.BlockSpec(memory_space=pltpu.HBM)] * 2,
         out_specs=[vm] * 6,
-        scratch_shapes=[VMEM((CH * ROWS, 128), F32)],
+        scratch_shapes=[
+            VMEM((CH * ROWS, 128), BF16),
+            VMEM((CH * ROWS, 128), F32),
+            VMEM((CH * ROWS, 128), F32),
+            pltpu.SemaphoreType.DMA((2,)),
+        ],
         compiler_params=pltpu.CompilerParams(vmem_limit_bytes=12 << 20),
         name="prep",
     )(noise, cond, state)
@@ -142,11 +155,93 @@
     return y[:, n : 2 * n] + pltpu.roll(y[:, :n], 1, 0) + pltpu.roll(y[:, 2 * n :], span - 1, 0)
 
 
+def pool(x, w, centre, rows):
+    even, odd = pair_conv(x, w, centre, rows, True)
+    both = silu(even).astype(BF16).astype(F32) + silu(odd).astype(BF16).astype(F32)
+    both = both.reshape(rows // 2, 2, PITCH, 128)
+    return ((both[:, 0] + both[:, 1]) * 0.25).reshape(rows // 2 * PITCH, 128)
+
+
+def put_row(x_c, c_row, x_s, s_row, left, right, middle_c, middle_s):
+    slot = lax.broadcasted_iota(jnp.int32, (8, 256), 0)
+    if c_row is not None:
+        at = c_row * PITCH
+        x_c[at : at + 8, :] = jnp.where(slot > 2, left, 0.0).astype(BF16)
+        x_c[at + 8 : at + 72, :] = middle_c
+        x_c[at + 72 : at + 80, :] = jnp.where(slot < 5, right, 0.0).astype(BF16)
+    if s_row is not None:
+        at = s_row * PITCH
+        x_s[at : at + 8, :] = jnp.where(slot > 5, pltpu.roll(left, 5, 0), 0.0).astype(BF16)
+        x_s[at + 8 : at + 72, :] = middle_s
+        x_s[at + 72 : at + 80, :] = jnp.where(slot < 2, pltpu.roll(right, 3, 0), 0.0).astype(BF16)
+
+
+def inner_body(
+    own_c, own_s, edge_a, edge_b, k_in, k_noisy, k_coarse, k_deeper, k_guide, k_block, k_branch, k_out,
+    w_in, w_noisy, w_coarse, w_deeper, w_guide, w_block, w_branch, w_out, pooled, opening, middle, guide,
+    x_c, x_s, arrived,
+):
+    free = 128 - CH
+    narrow = lambda w: w.at[:, :CH, :]
+    moves = [
+        (k_in, narrow(w_in)), (k_noisy, narrow(w_noisy)), (k_coarse, w_coarse), (k_deeper, w_deeper),
+        (k_guide, w_guide), (k_block, w_block), (k_branch, w_branch), (k_out, narrow(w_out)),
+    ]
+    copies = [pltpu.make_async_copy(src, dst, arrived.at[n]) for n, (src, dst) in enumerate(moves)]
+    for copy in copies:
+        copy.start()
+    for w in (w_in, w_noisy, w_out):
+        w[:, CH:, :] = jnp.zeros((9, free, 128), BF16)
+    lon_even = lax.axis_index("lon") % 2 == 0
+    for i in range(ROWS):
+        a, b = edge_a[i].astype(F32), edge_b[i].astype(F32)
+        put_row(x_c, i, x_s, i, jnp.where(lon_even, b, a), jnp.where(lon_even, a, b), own_c[i], own_s[i])
+    copies[0].wait()
+    for ch in range(2):
+        pooled[3 * ch * PITCH : (3 * ch + 3) * PITCH, :] = pool(x_c, w_in, 2 + 6 * ch, 6).astype(BF16)
+    copies[1].wait()
+    for ch in range(2):
+        for half, v in enumerate(pair_conv(x_s, w_noisy, 1 + 7 * ch, 7, True)):
+            opening[7 * ch * PITCH : (7 * ch + 7) * PITCH, 128 * half : 128 * half + 128] = v
+    copies[2].wait()
+    middle[...] = silu(half_conv(pooled, w_coarse, 1, 4)).astype(BF16)
+    copies[3].wait()
+    copies[4].wait()
+    guide[...] = matmul_nt(silu(half_conv(middle, w_deeper, 1, 2)).astype(BF16), w_guide[...])
+    for copy in copies[5:]:
+        copy.wait()
+
+
+def inner(*args):
+    vm = pl.BlockSpec(memory_space=VMEM)
+    wide = lambda n, k: jax.ShapeDtypeStruct((9, n, k), BF16)
+    rows = lambda n, lanes, dtype: jax.ShapeDtypeStruct((n * PITCH, lanes), dtype)
+    out_shape = (
+        wide(128, 128), wide(128, 128), wide(256, 128), wide(256, 256), jax.ShapeDtypeStruct((128, 256), BF16),
+        wide(128, 128), wide(128, 128), wide(128, 128),
+        rows(6, 128, BF16), rows(14, 256, F32), rows(4, 256, BF16), rows(2, 128, F32),
+    )
+    return pl.pallas_call(
+        inner_body,
+        out_shape=out_shape,
+        in_specs=[vm] * 4 + [pl.BlockSpec(memory_space=pltpu.HBM)] * 8,
+        out_specs=[vm] * len(out_shape),
+        scratch_shapes=[
+            VMEM((ROWS * PITCH, 256), BF16),
+            VMEM((ROWS * PITCH, 256), BF16),
+            pltpu.SemaphoreType.DMA((8,)),
+        ],
+        compiler_params=pltpu.CompilerParams(vmem_limit_bytes=16 << 20),
+        cost_estimate=pl.CostEstimate(flops=3 * 10**9, bytes_accessed=6 * 10**6, transcendentals=10**6),
+        name="inner",
+    )(*args)
+
+
 def net_body(
     n_lat,
-    noise, own_c, own_s, edge_a, edge_b, lat_a, lat_b, corner_a, corner_b, state,
-    k_in, k_coarse, k_deeper, guide_w, scale, shift, k_noisy, k_block, k_branch, k_out,
-    out, x_c, x_s, w_in, w_noisy, w_out, pooled, middle, guide, hidden, inner, mixed, turn,
+    noise, own_c, own_s, edge_a, edge_b, lat_a, lat_b, corner_a, corner_b, state, scale, shift,
+    w_in, w_noisy, w_coarse, w_deeper, w_guide, w_block, w_branch, w_out, pooled_in, opening, middle_in, guide_in,
+    out, x_c, x_s, pooled, middle, guide, hidden, inner, mixed, turn,
 ):
     lat = lax.axis_index("lat")
     top = (lat > 0).astype(F32)
@@ -159,36 +254,19 @@
     scale_out = 0.5 * sigma / jnp.sqrt(variance)
     noise_code = jnp.log(sigma) / 4.0
     free = 128 - CH
-    for tap in range(9):
-        for src, dst in ((k_in, w_in), (k_noisy, w_noisy)):
-            dst[tap, CH:, :] = jnp.zeros((free, 128), BF16)
-            dst[tap, :CH, :] = src[tap]
-        w_out[tap, CH:, :] = jnp.zeros((free, 128), BF16)
-        w_out[tap, :CH, :] = k_out[tap]
-
-    slot = lax.broadcasted_iota(jnp.int32, (8, 256), 0)
     lane = lax.broadcasted_iota(jnp.int32, (1, 128), 1)
 
-    def put(c_row, s_row, left, right, middle_c, middle_s):
-        x_c[c_row * PITCH : c_row * PITCH + 8, :] = jnp.where(slot > 2, left, 0.0).astype(BF16)
-        x_c[c_row * PITCH + 8 : c_row * PITCH + 72, :] = middle_c
-        x_c[c_row * PITCH + 72 : c_row * PITCH + 80, :] = jnp.where(slot < 5, right, 0.0).astype(BF16)
-        if s_row is not None:
-            s_left = jnp.where(slot > 5, pltpu.roll(left, 5, 0), 0.0)
-            s_right = jnp.where(slot < 2, pltpu.roll(right, 3, 0), 0.0)
-            x_s[s_row * PITCH : s_row * PITCH + 8, :] = s_left.astype(BF16)
-            x_s[s_row * PITCH + 8 : s_row * PITCH + 72, :] = middle_s
-            x_s[s_row * PITCH + 72 : s_row * PITCH + 80, :] = s_right.astype(BF16)
-
-    for i in range(ROWS):
+    for i in (0, 1, 2, 13, 14, 15):
         a, b = edge_a[i].astype(F32), edge_b[i].astype(F32)
-        put(DEEP + i, THIN + i, jnp.where(lon_even, b, a), jnp.where(lon_even, a, b), own_c[i], own_s[i])
+        s_row = THIN + i if i < 2 else i - 8 if i > 13 else None
+        put_row(
+            x_c, DEEP + i if i < 3 else i - 1, x_s, s_row,
+            jnp.where(lon_even, b, a), jnp.where(lon_even, a, b), own_c[i], own_s[i],
+        )
     for below in range(2):
         for k in range(DEEP):
-            r = k - (DEEP - THIN) if not below else k
-            s_row = r if not below else THIN + ROWS + k
-            if not 0 <= r < THIN:
-                s_row = None
+            r = k if below else k - (DEEP - THIN)
+            s_row = (8 + r if below else r) if 0 <= r < THIN else None
             picks = []
             for half in range(2):
                 lanes = slice(128 * half, 128 * half + 128)
@@ -210,63 +288,51 @@
                 mid_s = jnp.concatenate(mids, 1)
             sides = []
             for side in range(2):
-                pair = []
-                for corner in (corner_a, corner_b):
-                    pair.append(corner[side, k].astype(F32))
-                sides.append(jnp.where(lat_even, pair[0], pair[1]) if below else jnp.where(lat_even, pair[1], pair[0]))
-            row = DEEP + ROWS + k if below else k
-            put(row, s_row, sides[0], sides[1], jnp.concatenate(picks, 1), mid_s)
-
-    for ch in range(8):
-        even, odd = pair_conv(x_c, w_in, 1 + 4 * ch, 4, True)
-        both = silu(even).astype(BF16).astype(F32) + silu(odd).astype(BF16).astype(F32)
-        both = both.reshape(2, 2, PITCH, 128)
-        mean = (both[:, 0] + both[:, 1]) * 0.25
-        if ch < 2 or ch > 5:
-            mean = mean * (top if ch < 2 else bottom)
-        pooled[2 * ch * PITCH : (2 * ch + 2) * PITCH, :] = mean.reshape(2 * PITCH, 128).astype(BF16)
-    for ch in range(7):
-        m = silu(half_conv(pooled, k_coarse, 1 + 2 * ch, 2))
-        for q in range(2):
-            row = 2 * ch + q
-            v = m[q * PITCH : (q + 1) * PITCH]
-            if row < 3 or row > 10:
-                v = v * (top if row < 3 else bottom)
-            middle[row * PITCH : (row + 1) * PITCH, :] = v.astype(BF16)
+                a, b = corner_a[side, k].astype(F32), corner_b[side, k].astype(F32)
+                sides.append(jnp.where(lat_even, a, b) if below else jnp.where(lat_even, b, a))
+            put_row(x_c, 15 + k if below else k, x_s, s_row, sides[0], sides[1], jnp.concatenate(picks, 1), mid_s)
+
+    def put(ref, row, rows, value, above, below, lanes=slice(None)):
+        for q in range(rows):
+            v = value[q * PITCH : (q + 1) * PITCH]
+            if row + q < above:
+                v = v * top
+            if row + q >= below:
+                v = v * bottom
+            ref[(row + q) * PITCH : (row + q + 1) * PITCH, lanes] = v.astype(ref.dtype)
+
+    pooled[5 * PITCH : 11 * PITCH, :] = pooled_in[...]
+    for centre, rows, row in ((1, 10, 0), (13, 10, 11)):
+        put(pooled, row, rows // 2, pool(x_c, w_in, centre, rows), 4, 12)
+    middle[5 * PITCH : 9 * PITCH, :] = middle_in[...]
+    for row, rows in ((0, 5), (9, 5)):
+        put(middle, row, rows, silu(half_conv(pooled, w_coarse, row + 1, rows)), 3, 11)
     embedded = scale[...] * noise_code + shift[...]
-    for ch in range(6):
-        d = silu(half_conv(middle, k_deeper, 1 + 2 * ch, 2)).astype(BF16)
-        guide[2 * ch * PITCH : (2 * ch + 2) * PITCH, :] = matmul_nt(d, guide_w[...]) + embedded
-    for ch in range(11):
-        even, odd = pair_conv(x_s, w_noisy, 1 + 2 * ch, 2, True)
-        for q in range(2):
-            row = 2 * ch + q
-            g = guide[(row + 1) // 2 * PITCH : ((row + 1) // 2 + 1) * PITCH, :]
-            for half, v in enumerate((even, odd)):
-                v = silu(v[q * PITCH : (q + 1) * PITCH] + g)
-                if row < 3 or row > 18:
-                    v = v * (top if row < 3 else bottom)
-                hidden[row * PITCH : (row + 1) * PITCH, 128 * half : 128 * half + 128] = v.astype(BF16)
-    for ch in range(10):
-        for half, v in enumerate(pair_conv(hidden, k_block, 1 + 2 * ch, 2)):
-            v = silu(v)
-            if ch in (0, 9):
-                v = v * (top if ch == 0 else bottom)
-            inner[2 * ch * PITCH : (2 * ch + 2) * PITCH, 128 * half : 128 * half + 128] = v.astype(BF16)
-    for ch in range(9):
-        h = hidden[(2 + 2 * ch) * PITCH : (4 + 2 * ch) * PITCH, :].astype(F32)
-        for half, v in enumerate(pair_conv(inner, k_branch, 1 + 2 * ch, 2)):
-            v = silu(v + h[:, 128 * half : 128 * half + 128])
-            for q in range(2):
-                row = 2 * ch + q
-                u = v[q * PITCH : (q + 1) * PITCH]
-                if row in (0, 17):
-                    u = u * (top if row == 0 else bottom)
-                mixed[row * PITCH : (row + 1) * PITCH, 128 * half : 128 * half + 128] = u.astype(BF16)
-    for ch in range(8):
-        even, odd = pair_conv(mixed, w_out, 1 + 2 * ch, 2)
-        for q in range(2):
-            row = 2 * ch + q
+    guide[5 * PITCH : 7 * PITCH, :] = guide_in[...] + embedded
+    for row, rows in ((0, 5), (7, 5)):
+        d = silu(half_conv(middle, w_deeper, row + 1, rows)).astype(BF16)
+        guide[row * PITCH : (row + rows) * PITCH, :] = matmul_nt(d, w_guide[...]) + embedded
+    for row, rows in ((0, 4), (4, 14), (18, 4)):
+        if rows == 14:
+            sums = opening[:, 0:128], opening[:, 128:256]
+        else:
+            sums = pair_conv(x_s, w_noisy, 1 if row == 0 else 7, rows, True)
+        for half, v in enumerate(sums):
+            g = [guide[(row + q + 1) // 2 * PITCH : ((row + q + 1) // 2 + 1) * PITCH, :] for q in range(rows)]
+            v = silu(v + jnp.concatenate(g, 0))
+            put(hidden, row, rows, v, 3, 19, slice(128 * half, 128 * half + 128))
+    for row in (0, 10):
+        for half, v in enumerate(pair_conv(hidden, w_block, 1 + row, 10)):
+            put(inner, row, 10, silu(v), 2, 18, slice(128 * half, 128 * half + 128))
+    for row in (0, 9):
+        h = hidden[(2 + row) * PITCH : (11 + row) * PITCH, :].astype(F32)
+        for half, v in enumerate(pair_conv(inner, w_branch, 1 + row, 9)):
+            lanes = slice(128 * half, 128 * half + 128)
+            put(mixed, row, 9, silu(v + h[:, lanes]), 1, 17, lanes)
+    for first in (0, 8):
+        even, odd = pair_conv(mixed, w_out, 1 + first, 8)
+        for q in range(8):
+            row = first + q
             at = q * PITCH + EDGE
             turn[row, pl.ds(0, PAIRS, stride=2), :] = even[at : at + PAIRS]
             turn[row, pl.ds(1, PAIRS, stride=2), :] = odd[at : at + PAIRS]
@@ -283,11 +349,8 @@
         in_specs=[pl.BlockSpec(memory_space=pltpu.SMEM)] + [vm] * (len(args) - 1),
         out_specs=vm,
         scratch_shapes=[
-            VMEM((34 * PITCH, 256), BF16),
             VMEM((24 * PITCH, 256), BF16),
-            VMEM((9, 128, 128), BF16),
-            VMEM((9, 128, 128), BF16),
-            VMEM((9, 128, 128), BF16),
+            VMEM((12 * PITCH, 256), BF16),
             VMEM((16 * PITCH, 128), BF16),
             VMEM((14 * PITCH, 256), BF16),
             VMEM((12 * PITCH, 128), F32),
@@ -320,7 +383,7 @@
     lon_even, lat_even = lax.axis_index("lon") % 2 == 0, lax.axis_index("lat") % 2 == 0
     cond = conditions.reshape(CH * ROWS, 128)
     state = noisy_state.reshape(CH * ROWS, 128)
-    own_c, own_s, edge_a, edge_b, lat_a, lat_b = prep(noise_level, cond, state)
+    own_c, own_s, edge_a, edge_b, lat_a, lat_b = prep(noise_level, *(pltpu.with_memory_space_constraint(value, pltpu.HBM) for value in (cond, state)))
     permute = lambda value, a, o: lax.ppermute(value, AXES, swap_pairs(mesh_shape, a, o))
     edge_a = permute(edge_a, None, "A")
     edge_b = permute(edge_b, None, "B")
@@ -331,11 +394,15 @@
     corner_a = permute(jnp.where(lat_even, last, first), "A", None)
     corner_b = permute(jnp.where(lat_even, first, last), "B", None)
     by_input = lambda kernel: kernel.transpose(0, 2, 1)
+    weights = (
+        by_input(kernel_input), by_input(kernel_noisy), kernel_coarse, kernel_deeper,
+        guide_weight, kernel_block, kernel_branch, kernel_output,
+    )
+    in_hbm = lambda value: pltpu.with_memory_space_constraint(value, pltpu.HBM)
+    rest = inner(own_c, own_s, edge_a, edge_b, *map(in_hbm, weights))
     out = net(
-        mesh_shape[1],
-        noise_level, own_c, own_s, edge_a, edge_b, lat_a, lat_b, corner_a, corner_b, state,
-        by_input(kernel_input), kernel_coarse, kernel_deeper, guide_weight, time_scale[None], time_shift[None],
-        by_input(kernel_noisy), kernel_block, kernel_branch, kernel_output,
+        mesh_shape[1], noise_level, own_c, own_s, edge_a, edge_b, lat_a, lat_b, corner_a, corner_b, state,
+        time_scale[None], time_shift[None], *rest,
     )
     return out.reshape(noisy_state.shape)
 

time: 49.9 us -> 36.1 us (0.72)
  local copies, waits for them, and re-layouts: 7.07 us -> 0.02 us
  waiting for transfers between devices: 4.25 us -> 0.02 us
  Pallas kernels: 18.5 us -> 16 us
    pallas_call x1, Pallas kernels: 16.7 us -> 9.39 us  [net(): pl.pallas_call(functools.partial(net_body, n_lat), out_shape=jax.ShapeDty...]
    unnamed x26 -> x6, local copies, waits for them, and re-layouts: 7.07 us -> 0.02 us
    pallas_call x0 -> x1, Pallas kernels: none -> 4.5 us  [inner(): pl.pallas_call(inner_body, out_shape=out_shape, in_specs=[vm] * 4 + [pl.B...]
    ppermute x6, waiting for transfers between devices: 4.25 us -> 0.02 us  [on_device(): lax.ppermute(value, AXES, swap_pairs(mesh_shape, a, o))]
  transfers between devices with their start and end apart: 6 -> 6, of which waited for: 1 -> 0; matrix products, arithmetic and copies ran while one was open for 0% -> 0% of each run, Pallas kernels for 0% -> 13%
where the time goes in v2:
time: 36.1 us; the launch traced here: 35.9 us
  starting transfers between devices  19 us (53%)
  Pallas kernels  16 us (44%)
  between operations  0.83 us (2%)
    ppermute x6, starting transfers between devices, on_device(): lax.ppermute(value, AXES, swap_pairs(mesh_shape, a, o))  19 us
    pallas_call x1, Pallas kernels, net(): pl.pallas_call(functools.partial(net_body, n_lat), out_shape=jax.ShapeDty...  9.39 us
    pallas_call x1, Pallas kernels, inner(): pl.pallas_call(inner_body, out_shape=out_shape, in_specs=[vm] * 4 + [pl.B...  4.5 us
    pallas_call x1, Pallas kernels, prep(): pl.pallas_call(prep_body, out_shape=(own, own, edge, edge, rows, rows), i...  2.15 us
  transfers between devices with their start and end apart: 6, of which 0 were waited for; matrix products, arithmetic and copies ran while one was open for 0% of the time, Pallas kernels for 13%

profile of v2, /device:TPU:1, one launch (start us, length us, event | category | flops | bytes accessed | tf_op | source)
XLA Modules:
  0.0 35.9 jit_solution(15409655301739981025)
XLA Ops:
  0.7 2.1 %prep.1 = (bf16[16,64,256]{2,1,0:T(8,128)(2,1)S(1)}, bf16[16,64,256]{2,1,0:T(8,128)(2,1)S(1)}, bf16[16,8,256]{2,1,0:T(8,128)(2,1)S(1)}, bf16[16,8,256]{2,1,0:T(8...) custom-call(f32[1]{0:T(128)S(6)} %copy.14.noise, bf16[1280,128]{1,0:T(8,128)(2,1)} %bitcast.15, ...), custom_call_target="tpu_custom_call" | custom-call | tf_op jit(solution)/shard_map/prep/pallas_call | solution.py:104
  2.8 2.6 %collective-permute-start = (bf16[16,8,256]{2,1,0:T(8,128)(2,1)S(1)}, bf16[16,8,256]{2,1,0:T(8,128)(2,1)S(1)}, u32[]{:S(2)}, u32[]{:S(2)}) collective-permute-start(bf16[16,8,256]{2,1,0:T(8,128)(2,1)S(1)} %get-tuple-element.25), channel_id=1, source_target_pairs={{0,4},{1,5},{2,6},{3,7},{4,0},{5,1},{6,2},{7,3},{8,12},{9,13},{10,... | collective-permute-start | bytes 196616 | tf_op jit(solution)/shard_map/ppermute | solution.py:387
  5.4 7.9 %collective-permute-start.1 = (bf16[16,8,256]{2,1,0:T(8,128)(2,1)S(1)}, bf16[16,8,256]{2,1,0:T(8,128)(2,1)S(1)}, u32[]{:S(2)}, u32[]{:S(2)}) collective-permute-start(bf16[16,8,256]{2,1,0:T(8,128)(2,1)S(1)} %get-tuple-element.26), channel_id=1, source_target_pairs={{0,252},{1,253},{2,254},{3,255},{4,8},{5,9},{6,10},{7,11},{8,4},{9... | collective-permute-start | bytes 196616 | tf_op jit(solution)/shard_map/ppermute | solution.py:387
  13.2 1.2 %collective-permute-start.2 = (bf16[9,64,256]{2,1,0:T(8,128)(2,1)S(1)}, bf16[9,64,256]{2,1,0:T(8,128)(2,1)S(1)}, u32[]{:S(2)}, u32[]{:S(2)}) collective-permute-start(bf16[9,64,256]{2,1,0:T(8,128)(2,1)S(1)} %get-tuple-element.27), channel_id=1, source_target_pairs={{0,1},{1,0},{2,3},{3,2},{4,5},{5,4},{6,7},{7,6},{8,9},{9,8},{10,11... | collective-permute-start | bytes 884744 | tf_op jit(solution)/shard_map/ppermute | solution.py:387
  14.5 4.4 %collective-permute-start.3 = (bf16[9,64,256]{2,1,0:T(8,128)(2,1)S(1)}, bf16[9,64,256]{2,1,0:T(8,128)(2,1)S(1)}, u32[]{:S(2)}, u32[]{:S(2)}) collective-permute-start(bf16[9,64,256]{2,1,0:T(8,128)(2,1)S(1)} %get-tuple-element.28), channel_id=1, source_target_pairs={{1,2},{2,1},{5,6},{6,5},{9,10},{10,9},{13,14},{14,13},{17,18},{18,... | collective-permute-start | bytes 884744 | tf_op jit(solution)/shard_map/ppermute | solution.py:387
  18.9 0.0 collective-permute-done.edge_a
  18.9 0.0 collective-permute-done.1.edge_b
  19.0 2.6 %collective-permute-start.5 = (bf16[2,9,8,256]{3,2,1,0:T(8,128)(2,1)S(1)}, bf16[2,9,8,256]{3,2,1,0:T(8,128)(2,1)S(1)}, u32[]{:S(2)}, u32[]{:S(2)}) collective-permute-start(bf16[2,9,8,256]{3,2,1,0:T(8,128)(2,1)S(1)} %get-tuple-element.41), channel_id=1, source_target_pairs={{1,2},{2,1},{5,6},{6,5},{9,10},{10,9},{13,14},{14,13},{17,18},{18,... | collective-permute-start | bytes 221192 | tf_op jit(solution)/shard_map/ppermute | solution.py:387
  21.6 0.3 collective-permute-start.4
  21.9 0.0 copy-start
  21.9 0.0 copy-start.1
  21.9 0.0 copy-start.2
  22.0 4.5 %inner.1 = (bf16[9,128,128]{2,1,0:T(8,128)(2,1)S(1)}, bf16[9,128,128]{2,1,0:T(8,128)(2,1)S(1)}, bf16[9,256,128]{2,1,0:T(8,128)(2,1)S(1)}, bf16[9,256,256]{2,1,0:...) custom-call(bf16[16,64,256]{2,1,0:T(8,128)(2,1)S(1)} %get-tuple-elem, ...), custom_call_target="tpu_custom_call" | custom-call | flops 3000000000 | bytes 6000000 | tf_op jit(solution)/shard_map/inner/pallas_call | solution.py:224
  26.5 0.0 collective-permute-done.5.corner_b
  26.5 0.0 collective-permute-done.4.corner_a
  26.5 0.0 collective-permute-done.2.lat_a
  26.5 0.0 collective-permute-done.3.lat_b
  26.5 0.0 copy-done
  26.5 0.0 copy-done.1
  26.5 0.0 copy-done.2
  26.5 9.4 %net.1 = f32[1280,128]{1,0:T(8,128)} custom-call(f32[1]{0:T(128)S(6)} %copy.14.noise, bf16[16,64,256]{2,1,0:T(8,128)(2,1)S(1)} %get-tuple-element.23.own_c, bf16[16,64,256]{2,1,0:T(8,128)(2,1)S(1)} %get-tuple-element.24.own_s, bf16[16,8,256]{2,1,0:T(8,128)(2,1)S(1)} %collective-permute-done.edge_a, bf16[16,8,256]{2,1,0:T(8,128)(2,1)S(1)} %collective-permute-done.1.edge_b, ...), custom_call_target="tpu_custom_call" | custom-call | tf_op jit(solution)/shard_map/net/pallas_call | solution.py:346
  (2 shorter events, 0.0 us)
Async XLA Ops:
  2.8 16.1 %collective-permute-start = (bf16[16,8,256]{2,1,0:T(8,128)(2,1)S(1)}, bf16[16,8,256]{2,1,0:T(8,128)(2,1)S(1)}, u32[]{:S(2)}, u32[]{:S(2)}) collective-permute-start(bf16[16,8,256]{2,1,0:T(8,128)(2,1)S(1)} %get-tuple-element.25), channel_id=1, source_target_pairs={{0,4},{1,5},{2,6},{3,7},{4,0},{5,1},{6,2},{7,3},{8,12},{9,13},{10,... | collective-permute-start | bytes 196616 | tf_op jit(solution)/shard_map/ppermute | solution.py:387
  5.4 13.6 %collective-permute-start.1 = (bf16[16,8,256]{2,1,0:T(8,128)(2,1)S(1)}, bf16[16,8,256]{2,1,0:T(8,128)(2,1)S(1)}, u32[]{:S(2)}, u32[]{:S(2)}) collective-permute-start(bf16[16,8,256]{2,1,0:T(8,128)(2,1)S(1)} %get-tuple-element.26), channel_id=1, source_target_pairs={{0,252},{1,253},{2,254},{3,255},{4,8},{5,9},{6,10},{7,11},{8,4},{9... | collective-permute-start | bytes 196616 | tf_op jit(solution)/shard_map/ppermute | solution.py:387
  13.2 13.2 %collective-permute-start.2 = (bf16[9,64,256]{2,1,0:T(8,128)(2,1)S(1)}, bf16[9,64,256]{2,1,0:T(8,128)(2,1)S(1)}, u32[]{:S(2)}, u32[]{:S(2)}) collective-permute-start(bf16[9,64,256]{2,1,0:T(8,128)(2,1)S(1)} %get-tuple-element.27), channel_id=1, source_target_pairs={{0,1},{1,0},{2,3},{3,2},{4,5},{5,4},{6,7},{7,6},{8,9},{9,8},{10,11... | collective-permute-start | bytes 884744 | tf_op jit(solution)/shard_map/ppermute | solution.py:387
  14.5 12.0 %collective-permute-start.3 = (bf16[9,64,256]{2,1,0:T(8,128)(2,1)S(1)}, bf16[9,64,256]{2,1,0:T(8,128)(2,1)S(1)}, u32[]{:S(2)}, u32[]{:S(2)}) collective-permute-start(bf16[9,64,256]{2,1,0:T(8,128)(2,1)S(1)} %get-tuple-element.28), channel_id=1, source_target_pairs={{1,2},{2,1},{5,6},{6,5},{9,10},{10,9},{13,14},{14,13},{17,18},{18,... | collective-permute-start | bytes 884744 | tf_op jit(solution)/shard_map/ppermute | solution.py:387
  19.0 7.5 %collective-permute-start.5 = (bf16[2,9,8,256]{3,2,1,0:T(8,128)(2,1)S(1)}, bf16[2,9,8,256]{3,2,1,0:T(8,128)(2,1)S(1)}, u32[]{:S(2)}, u32[]{:S(2)}) collective-permute-start(bf16[2,9,8,256]{3,2,1,0:T(8,128)(2,1)S(1)} %get-tuple-element.41), channel_id=1, source_target_pairs={{1,2},{2,1},{5,6},{6,5},{9,10},{10,9},{13,14},{14,13},{17,18},{18,... | collective-permute-start | bytes 221192 | tf_op jit(solution)/shard_map/ppermute | solution.py:387
  21.6 4.8 %collective-permute-start.4 = (bf16[2,9,8,256]{3,2,1,0:T(8,128)(2,1)S(1)}, bf16[2,9,8,256]{3,2,1,0:T(8,128)(2,1)S(1)}, u32[]{:S(2)}, u32[]{:S(2)}) collective-permute-start(bf16[2,9,8,256]{3,2,1,0:T(8,128)(2,1)S(1)} %get-tuple-element.42), channel_id=1, source_target_pairs={{0,1},{1,0},{2,3},{3,2},{4,5},{5,4},{6,7},{7,6},{8,9},{9,8},{10,11... | collective-permute-start | bytes 221192 | tf_op jit(solution)/shard_map/ppermute | solution.py:387
  21.9 4.6 %copy-start = (f32[1,80,16,128]{3,2,1,0:T(8,128)S(1)}, f32[1,80,16,128]{3,2,1,0:T(8,128)}, u32[]{:S(2)}) copy-start(f32[1,80,16,128]{3,2,1,0:T(8,128)} %param.14) | copy-start | bytes 1966084
  21.9 4.6 %copy-start.1 = (f32[128]{0:T(128)S(1)}, f32[128]{0:T(128)}, u32[]{:S(2)}) copy-start(f32[128]{0:T(128)} %param.20) | copy-start | bytes 1540
  21.9 4.6 %copy-start.2 = (f32[128]{0:T(128)S(1)}, f32[128]{0:T(128)}, u32[]{:S(2)}) copy-start(f32[128]{0:T(128)} %param.21) | copy-start | bytes 1540

commit v3 on v2

--- a/solution.py
+++ b/solution.py
@@ -9,8 +9,9 @@
 
 F32 = jnp.float32
 BF16 = jnp.bfloat16
-PITCH = 80
-EDGE = 8
+PITCH = 72
+EDGE = 4
+WIDE = 80
 ROWS = 16
 PAIRS = 64
 CH = 80
@@ -44,10 +45,15 @@
     return lax.dot_general(x, w, (((1,), (1,)), ((), ())), preferred_element_type=F32)
 
 
-def prep_body(noise, cond_hbm, state_hbm, own_c, own_s, edge_a, edge_b, lat_a, lat_b, cond, state, work, arrived):
+def prep_body(
+    noise, cond_hbm, state_hbm, k_in, k_noisy, own_c, own_s, edge_a, edge_b, lat_a, lat_b, w_in, w_noisy,
+    cond, state, work, arrived,
+):
     copies = [
         pltpu.make_async_copy(cond_hbm, cond, arrived.at[0]),
         pltpu.make_async_copy(state_hbm, state, arrived.at[1]),
+        pltpu.make_async_copy(k_in, w_in.at[:, :CH, :], arrived.at[2]),
+        pltpu.make_async_copy(k_noisy, w_noisy.at[:, :CH, :], arrived.at[3]),
     ]
     for copy in copies:
         copy.start()
@@ -60,7 +66,9 @@
     pick = (col == jnp.where(row < PAIRS, 2 * row, 2 * (row - PAIRS) + 1)).astype(BF16)
     blank = jnp.zeros((128 - CH, 128), BF16)
     slot = lax.broadcasted_iota(jnp.int32, (8, 128), 0)
-    for copy in copies:
+    for w in (w_in, w_noisy):
+        w[:, CH:, :] = jnp.zeros((9, 128 - CH, 128), BF16)
+    for copy in copies[:2]:
         copy.wait()
     work[...] = cond[...].astype(F32)
     for i in range(ROWS):
@@ -94,27 +102,30 @@
                 rows.append(value)
             lat_a[k, :, lanes] = jnp.where(lat_even, rows[1], rows[0]).astype(BF16)
             lat_b[k, :, lanes] = jnp.where(lat_even, rows[0], rows[1]).astype(BF16)
-
-
-def prep(noise, cond, state):
+    for copy in copies[2:]:
+        copy.wait()
+
+
+def prep(noise, *args):
     vm = pl.BlockSpec(memory_space=VMEM)
     own = jax.ShapeDtypeStruct((ROWS, PAIRS, 256), BF16)
     edge = jax.ShapeDtypeStruct((ROWS, 8, 256), BF16)
     rows = jax.ShapeDtypeStruct((DEEP, PAIRS, 256), BF16)
+    weights = jax.ShapeDtypeStruct((9, 128, 128), BF16)
     return pl.pallas_call(
         prep_body,
-        out_shape=(own, own, edge, edge, rows, rows),
-        in_specs=[pl.BlockSpec(memory_space=pltpu.SMEM)] + [pl.BlockSpec(memory_space=pltpu.HBM)] * 2,
-        out_specs=[vm] * 6,
+        out_shape=(own, own, edge, edge, rows, rows, weights, weights),
+        in_specs=[pl.BlockSpec(memory_space=pltpu.SMEM)] + [pl.BlockSpec(memory_space=pltpu.HBM)] * 4,
+        out_specs=[vm] * 8,
         scratch_shapes=[
             VMEM((CH * ROWS, 128), BF16),
             VMEM((CH * ROWS, 128), F32),
             VMEM((CH * ROWS, 128), F32),
-            pltpu.SemaphoreType.DMA((2,)),
+            pltpu.SemaphoreType.DMA((4,)),
         ],
         compiler_params=pltpu.CompilerParams(vmem_limit_bytes=12 << 20),
         name="prep",
-    )(noise, cond, state)
+    )(noise, *args)
 
 
 def pair_weights(w, di):
@@ -131,9 +142,9 @@
     return c([c([k1, k0, z, k2], 1), c([k2, k1, k0, z], 1)], 0)
 
 
-def pair_conv(x, w, centre, rows, by_input=False):
-    span = rows * PITCH
-    taps = [x[(centre + d - 1) * PITCH : (centre + d - 1) * PITCH + span, :] for d in range(3)]
+def pair_conv(x, w, centre, rows, by_input=False, pitch=PITCH):
+    span = rows * pitch
+    taps = [x[(centre + d - 1) * pitch : (centre + d - 1) * pitch + span, :] for d in range(3)]
     taps = jnp.concatenate(taps, 1)
     if by_input:
         weights = jnp.concatenate([pair_weights_by_input(w, d) for d in range(3)], 0)
@@ -156,59 +167,56 @@
 
 
 def pool(x, w, centre, rows):
-    even, odd = pair_conv(x, w, centre, rows, True)
+    even, odd = pair_conv(x, w, centre, rows, True, WIDE)
     both = silu(even).astype(BF16).astype(F32) + silu(odd).astype(BF16).astype(F32)
-    both = both.reshape(rows // 2, 2, PITCH, 128)
-    return ((both[:, 0] + both[:, 1]) * 0.25).reshape(rows // 2 * PITCH, 128)
+    both = both.reshape(rows // 2, 2, WIDE, 128)
+    mean = (both[:, 0] + both[:, 1]) * 0.25
+    shift = 8 - EDGE
+    return mean[:, shift : shift + PITCH].reshape(rows // 2 * PITCH, 128)
 
 
 def put_row(x_c, c_row, x_s, s_row, left, right, middle_c, middle_s):
     slot = lax.broadcasted_iota(jnp.int32, (8, 256), 0)
     if c_row is not None:
-        at = c_row * PITCH
+        at = c_row * WIDE
         x_c[at : at + 8, :] = jnp.where(slot > 2, left, 0.0).astype(BF16)
         x_c[at + 8 : at + 72, :] = middle_c
         x_c[at + 72 : at + 80, :] = jnp.where(slot < 5, right, 0.0).astype(BF16)
     if s_row is not None:
         at = s_row * PITCH
-        x_s[at : at + 8, :] = jnp.where(slot > 5, pltpu.roll(left, 5, 0), 0.0).astype(BF16)
-        x_s[at + 8 : at + 72, :] = middle_s
-        x_s[at + 72 : at + 80, :] = jnp.where(slot < 2, pltpu.roll(right, 3, 0), 0.0).astype(BF16)
+        x_s[at : at + 4, :] = jnp.where(slot > 1, pltpu.roll(left, 1, 0), 0.0)[:4].astype(BF16)
+        x_s[at + 4 : at + 68, :] = middle_s
+        x_s[at + 68 : at + 72, :] = jnp.where(slot < 2, pltpu.roll(right, 3, 0), 0.0)[:4].astype(BF16)
 
 
 def inner_body(
-    own_c, own_s, edge_a, edge_b, k_in, k_noisy, k_coarse, k_deeper, k_guide, k_block, k_branch, k_out,
-    w_in, w_noisy, w_coarse, w_deeper, w_guide, w_block, w_branch, w_out, pooled, opening, middle, guide,
+    own_c, own_s, edge_a, edge_b, w_in, w_noisy, k_coarse, k_deeper, k_guide, k_block, k_branch, k_out,
+    w_coarse, w_deeper, w_guide, w_block, w_branch, w_out, pooled, opening, middle, guide,
     x_c, x_s, arrived,
 ):
-    free = 128 - CH
-    narrow = lambda w: w.at[:, :CH, :]
     moves = [
-        (k_in, narrow(w_in)), (k_noisy, narrow(w_noisy)), (k_coarse, w_coarse), (k_deeper, w_deeper),
-        (k_guide, w_guide), (k_block, w_block), (k_branch, w_branch), (k_out, narrow(w_out)),
+        (k_coarse, w_coarse), (k_deeper, w_deeper), (k_guide, w_guide),
+        (k_block, w_block), (k_branch, w_branch), (k_out, w_out.at[:, :CH, :]),
     ]
     copies = [pltpu.make_async_copy(src, dst, arrived.at[n]) for n, (src, dst) in enumerate(moves)]
     for copy in copies:
         copy.start()
-    for w in (w_in, w_noisy, w_out):
-        w[:, CH:, :] = jnp.zeros((9, free, 128), BF16)
+    w_out[:, CH:, :] = jnp.zeros((9, 128 - CH, 128), BF16)
     lon_even = lax.axis_index("lon") % 2 == 0
     for i in range(ROWS):
         a, b = edge_a[i].astype(F32), edge_b[i].astype(F32)
         put_row(x_c, i, x_s, i, jnp.where(lon_even, b, a), jnp.where(lon_even, a, b), own_c[i], own_s[i])
-    copies[0].wait()
     for ch in range(2):
         pooled[3 * ch * PITCH : (3 * ch + 3) * PITCH, :] = pool(x_c, w_in, 2 + 6 * ch, 6).astype(BF16)
+    for row, rows in ((0, 6), (6, 8)):
+        for half, v in enumerate(pair_conv(x_s, w_noisy, 1 + row, rows, True)):
+            opening[row * PITCH : (row + rows) * PITCH, 128 * half : 128 * half + 128] = v
+    copies[0].wait()
+    middle[...] = silu(half_conv(pooled, w_coarse, 1, 4)).astype(BF16)
     copies[1].wait()
-    for ch in range(2):
-        for half, v in enumerate(pair_conv(x_s, w_noisy, 1 + 7 * ch, 7, True)):
-            opening[7 * ch * PITCH : (7 * ch + 7) * PITCH, 128 * half : 128 * half + 128] = v
     copies[2].wait()
-    middle[...] = silu(half_conv(pooled, w_coarse, 1, 4)).astype(BF16)
-    copies[3].wait()
-    copies[4].wait()
     guide[...] = matmul_nt(silu(half_conv(middle, w_deeper, 1, 2)).astype(BF16), w_guide[...])
-    for copy in copies[5:]:
+    for copy in copies[3:]:
         copy.wait()
 
 
@@ -217,19 +225,19 @@
     wide = lambda n, k: jax.ShapeDtypeStruct((9, n, k), BF16)
     rows = lambda n, lanes, dtype: jax.ShapeDtypeStruct((n * PITCH, lanes), dtype)
     out_shape = (
-        wide(128, 128), wide(128, 128), wide(256, 128), wide(256, 256), jax.ShapeDtypeStruct((128, 256), BF16),
+        wide(256, 128), wide(256, 256), jax.ShapeDtypeStruct((128, 256), BF16),
         wide(128, 128), wide(128, 128), wide(128, 128),
         rows(6, 128, BF16), rows(14, 256, F32), rows(4, 256, BF16), rows(2, 128, F32),
     )
     return pl.pallas_call(
         inner_body,
         out_shape=out_shape,
-        in_specs=[vm] * 4 + [pl.BlockSpec(memory_space=pltpu.HBM)] * 8,
+        in_specs=[vm] * 6 + [pl.BlockSpec(memory_space=pltpu.HBM)] * 6,
         out_specs=[vm] * len(out_shape),
         scratch_shapes=[
+            VMEM((ROWS * WIDE, 256), BF16),
             VMEM((ROWS * PITCH, 256), BF16),
-            VMEM((ROWS * PITCH, 256), BF16),
-            pltpu.SemaphoreType.DMA((8,)),
+            pltpu.SemaphoreType.DMA((6,)),
         ],
         compiler_params=pltpu.CompilerParams(vmem_limit_bytes=16 << 20),
         cost_estimate=pl.CostEstimate(flops=3 * 10**9, bytes_accessed=6 * 10**6, transcendentals=10**6),
@@ -293,13 +301,14 @@
             put_row(x_c, 15 + k if below else k, x_s, s_row, sides[0], sides[1], jnp.concatenate(picks, 1), mid_s)
 
     def put(ref, row, rows, value, above, below, lanes=slice(None)):
-        for q in range(rows):
-            v = value[q * PITCH : (q + 1) * PITCH]
-            if row + q < above:
-                v = v * top
-            if row + q >= below:
-                v = v * bottom
-            ref[(row + q) * PITCH : (row + q + 1) * PITCH, lanes] = v.astype(ref.dtype)
+        over = min(max(above - row, 0), rows)
+        under = min(max(row + rows - below, 0), rows)
+        parts = [value[over * PITCH : (rows - under) * PITCH]]
+        if over:
+            parts.insert(0, value[: over * PITCH] * top)
+        if under:
+            parts.append(value[(rows - under) * PITCH :] * bottom)
+        ref[row * PITCH : (row + rows) * PITCH, lanes] = jnp.concatenate(parts, 0).astype(ref.dtype)
 
     pooled[5 * PITCH : 11 * PITCH, :] = pooled_in[...]
     for centre, rows, row in ((1, 10, 0), (13, 10, 11)):
@@ -324,19 +333,19 @@
     for row in (0, 10):
         for half, v in enumerate(pair_conv(hidden, w_block, 1 + row, 10)):
             put(inner, row, 10, silu(v), 2, 18, slice(128 * half, 128 * half + 128))
-    for row in (0, 9):
-        h = hidden[(2 + row) * PITCH : (11 + row) * PITCH, :].astype(F32)
-        for half, v in enumerate(pair_conv(inner, w_branch, 1 + row, 9)):
+    for row, rows in ((0, 10), (10, 8)):
+        h = hidden[(2 + row) * PITCH : (2 + row + rows) * PITCH, :].astype(F32)
+        for half, v in enumerate(pair_conv(inner, w_branch, 1 + row, rows)):
             lanes = slice(128 * half, 128 * half + 128)
-            put(mixed, row, 9, silu(v + h[:, lanes]), 1, 17, lanes)
-    for first in (0, 8):
-        even, odd = pair_conv(mixed, w_out, 1 + first, 8)
-        for q in range(8):
+            put(mixed, row, rows, silu(v + h[:, lanes]), 1, 17, lanes)
+    for first, rows in ((0, 6), (6, 6), (12, 4)):
+        even, odd = pair_conv(mixed, w_out, 1 + first, rows)
+        for q in range(rows):
             row = first + q
-            at = q * PITCH + EDGE
-            turn[row, pl.ds(0, PAIRS, stride=2), :] = even[at : at + PAIRS]
-            turn[row, pl.ds(1, PAIRS, stride=2), :] = odd[at : at + PAIRS]
-            head = turn[row].T[:CH]
+            at = slice(q * PITCH, (q + 1) * PITCH)
+            turn[row, pl.ds(0, PITCH, stride=2), :] = even[at]
+            turn[row, pl.ds(1, PITCH, stride=2), :] = odd[at]
+            head = turn[row, 2 * EDGE : 2 * (EDGE + PAIRS), :].T[:CH]
             here = pl.ds(row, CH, stride=ROWS)
             out[here, :] = scale_skip * state[here, :] + scale_out * head
 
@@ -349,7 +358,7 @@
         in_specs=[pl.BlockSpec(memory_space=pltpu.SMEM)] + [vm] * (len(args) - 1),
         out_specs=vm,
         scratch_shapes=[
-            VMEM((24 * PITCH, 256), BF16),
+            VMEM((24 * WIDE, 256), BF16),
             VMEM((12 * PITCH, 256), BF16),
             VMEM((16 * PITCH, 128), BF16),
             VMEM((14 * PITCH, 256), BF16),
@@ -357,7 +366,7 @@
             VMEM((22 * PITCH, 256), BF16),
             VMEM((20 * PITCH, 256), BF16),
             VMEM((18 * PITCH, 256), BF16),
-            VMEM((ROWS, 128, 128), F32),
+            VMEM((ROWS, 2 * PITCH, 128), F32),
         ],
         compiler_params=pltpu.CompilerParams(vmem_limit_bytes=24 << 20),
         name="net",
@@ -383,26 +392,25 @@
     lon_even, lat_even = lax.axis_index("lon") % 2 == 0, lax.axis_index("lat") % 2 == 0
     cond = conditions.reshape(CH * ROWS, 128)
     state = noisy_state.reshape(CH * ROWS, 128)
-    own_c, own_s, edge_a, edge_b, lat_a, lat_b = prep(noise_level, *(pltpu.with_memory_space_constraint(value, pltpu.HBM) for value in (cond, state)))
+    by_input = lambda kernel: kernel.transpose(0, 2, 1)
+    in_hbm = lambda *values: [pltpu.with_memory_space_constraint(value, pltpu.HBM) for value in values]
+    own_c, own_s, edge_a, edge_b, lat_a, lat_b, w_in, w_noisy = prep(
+        noise_level, *in_hbm(cond, state, by_input(kernel_input), by_input(kernel_noisy))
+    )
     permute = lambda value, a, o: lax.ppermute(value, AXES, swap_pairs(mesh_shape, a, o))
+    edge_b = permute(edge_b, None, "B")
     edge_a = permute(edge_a, None, "A")
-    edge_b = permute(edge_b, None, "B")
     lat_a = permute(lat_a, "A", None)
     lat_b = permute(lat_b, "B", None)
     sides = jnp.stack([jnp.where(lon_even, edge_b, edge_a), jnp.where(lon_even, edge_a, edge_b)])
     first, last = sides[:, :DEEP], sides[:, ROWS - DEEP :]
     corner_a = permute(jnp.where(lat_even, last, first), "A", None)
     corner_b = permute(jnp.where(lat_even, first, last), "B", None)
-    by_input = lambda kernel: kernel.transpose(0, 2, 1)
-    weights = (
-        by_input(kernel_input), by_input(kernel_noisy), kernel_coarse, kernel_deeper,
-        guide_weight, kernel_block, kernel_branch, kernel_output,
-    )
-    in_hbm = lambda value: pltpu.with_memory_space_constraint(value, pltpu.HBM)
-    rest = inner(own_c, own_s, edge_a, edge_b, *map(in_hbm, weights))
+    weights = in_hbm(kernel_coarse, kernel_deeper, guide_weight, kernel_block, kernel_branch, kernel_output)
+    rest = inner(own_c, own_s, edge_a, edge_b, w_in, w_noisy, *weights)
     out = net(
         mesh_shape[1], noise_level, own_c, own_s, edge_a, edge_b, lat_a, lat_b, corner_a, corner_b, state,
-        time_scale[None], time_shift[None], *rest,
+        time_scale[None], time_shift[None], w_in, w_noisy, *rest,
     )
     return out.reshape(noisy_state.shape)
 

time: 36.1 us -> 35.3 us (0.978)
  Pallas kernels: 16 us -> 14.4 us
  waiting for transfers between devices: 0.02 us -> 0.91 us
    pallas_call x2, Pallas kernels: 6.65 us -> 5.46 us  [the longest x1 3.29 us: inner(): pl.pallas_call(inner_body, out_shape=out_shape, in_specs=[vm] * 6 + [pl.B...]
    ppermute x6, waiting for transfers between devices: 0.02 us -> 0.91 us  [on_device(): lax.ppermute(value, AXES, swap_pairs(mesh_shape, a, o))]
    pallas_call x1, Pallas kernels: 9.39 us -> 8.96 us  [net(): pl.pallas_call(functools.partial(net_body, n_lat), out_shape=jax.ShapeDty...]
  transfers between devices with their start and end apart: 6 -> 6, of which waited for: 0 -> 1; matrix products, arithmetic and copies ran while one was open for 0% -> 0% of each run, Pallas kernels for 13% -> 9%
where the time goes in v3:
time: 35.3 us; the launch traced here: 35.2 us
  starting transfers between devices  19 us (54%)
  Pallas kernels  14.4 us (41%)
  waiting for transfers between devices  0.91 us (3%)
  between operations  0.8 us (2%)
    ppermute x6, starting transfers between devices, on_device(): lax.ppermute(value, AXES, swap_pairs(mesh_shape, a, o))  19 us
    pallas_call x1, Pallas kernels, net(): pl.pallas_call(functools.partial(net_body, n_lat), out_shape=jax.ShapeDty...  8.96 us
    pallas_call x1, Pallas kernels, inner(): pl.pallas_call(inner_body, out_shape=out_shape, in_specs=[vm] * 6 + [pl.B...  3.29 us
    pallas_call x1, Pallas kernels, prep(): pl.pallas_call(prep_body, out_shape=(own, own, edge, edge, rows, rows, we...  2.17 us
    ppermute x6, waiting for transfers between devices, on_device(): lax.ppermute(value, AXES, swap_pairs(mesh_shape, a, o))  0.91 us
  transfers between devices with their start and end apart: 6, of which 1 were waited for; matrix products, arithmetic and copies ran while one was open for 0% of the time, Pallas kernels for 9%

profile of v3, /device:TPU:1, one launch (start us, length us, event | category | flops | bytes accessed | tf_op | source)
XLA Modules:
  0.0 35.2 jit_solution(8580973958491633598)
XLA Ops:
  0.7 2.2 %prep.1 = (bf16[16,64,256]{2,1,0:T(8,128)(2,1)S(1)}, bf16[16,64,256]{2,1,0:T(8,128)(2,1)S(1)}, bf16[16,8,256]{2,1,0:T(8,128)(2,1)S(1)}, bf16[16,8,256]{2,1,0:T(8...) custom-call(f32[1]{0:T(128)S(6)} %copy.14.noise, ...), custom_call_target="tpu_custom_call" | custom-call | tf_op jit(solution)/shard_map/prep/pallas_call | solution.py:115
  2.8 2.6 %collective-permute-start = (bf16[16,8,256]{2,1,0:T(8,128)(2,1)S(1)}, bf16[16,8,256]{2,1,0:T(8,128)(2,1)S(1)}, u32[]{:S(2)}, u32[]{:S(2)}) collective-permute-start(bf16[16,8,256]{2,1,0:T(8,128)(2,1)S(1)} %get-tuple-element.25), channel_id=1, source_target_pairs={{0,4},{1,5},{2,6},{3,7},{4,0},{5,1},{6,2},{7,3},{8,12},{9,13},{10,... | collective-permute-start | bytes 196616 | tf_op jit(solution)/shard_map/ppermute | solution.py:400
  5.4 7.9 %collective-permute-start.1 = (bf16[16,8,256]{2,1,0:T(8,128)(2,1)S(1)}, bf16[16,8,256]{2,1,0:T(8,128)(2,1)S(1)}, u32[]{:S(2)}, u32[]{:S(2)}) collective-permute-start(bf16[16,8,256]{2,1,0:T(8,128)(2,1)S(1)} %get-tuple-element.26), channel_id=1, source_target_pairs={{0,252},{1,253},{2,254},{3,255},{4,8},{5,9},{6,10},{7,11},{8,4},{9... | collective-permute-start | bytes 196616 | tf_op jit(solution)/shard_map/ppermute | solution.py:400
  13.3 1.2 %collective-permute-start.2 = (bf16[9,64,256]{2,1,0:T(8,128)(2,1)S(1)}, bf16[9,64,256]{2,1,0:T(8,128)(2,1)S(1)}, u32[]{:S(2)}, u32[]{:S(2)}) collective-permute-start(bf16[9,64,256]{2,1,0:T(8,128)(2,1)S(1)} %get-tuple-element.27), channel_id=1, source_target_pairs={{0,1},{1,0},{2,3},{3,2},{4,5},{5,4},{6,7},{7,6},{8,9},{9,8},{10,11... | collective-permute-start | bytes 884744 | tf_op jit(solution)/shard_map/ppermute | solution.py:400
  14.5 4.4 %collective-permute-start.3 = (bf16[9,64,256]{2,1,0:T(8,128)(2,1)S(1)}, bf16[9,64,256]{2,1,0:T(8,128)(2,1)S(1)}, u32[]{:S(2)}, u32[]{:S(2)}) collective-permute-start(bf16[9,64,256]{2,1,0:T(8,128)(2,1)S(1)} %get-tuple-element.28), channel_id=1, source_target_pairs={{1,2},{2,1},{5,6},{6,5},{9,10},{10,9},{13,14},{14,13},{17,18},{18,... | collective-permute-start | bytes 884744 | tf_op jit(solution)/shard_map/ppermute | solution.py:400
  18.9 0.0 collective-permute-done.edge_a
  18.9 0.0 collective-permute-done.1.edge_b
  19.0 2.6 %collective-permute-start.5 = (bf16[2,9,8,256]{3,2,1,0:T(8,128)(2,1)S(1)}, bf16[2,9,8,256]{3,2,1,0:T(8,128)(2,1)S(1)}, u32[]{:S(2)}, u32[]{:S(2)}) collective-permute-start(bf16[2,9,8,256]{3,2,1,0:T(8,128)(2,1)S(1)} %get-tuple-element.41), channel_id=1, source_target_pairs={{1,2},{2,1},{5,6},{6,5},{9,10},{10,9},{13,14},{14,13},{17,18},{18,... | collective-permute-start | bytes 221192 | tf_op jit(solution)/shard_map/ppermute | solution.py:400
  21.7 0.3 collective-permute-start.4
  21.9 0.0 copy-start
  21.9 0.0 copy-start.1
  22.0 0.0 copy-start.2
  22.0 3.3 %inner.1 = (bf16[9,256,128]{2,1,0:T(8,128)(2,1)S(1)}, bf16[9,256,256]{2,1,0:T(8,128)(2,1)S(1)}, bf16[128,256]{1,0:T(8,128)(2,1)S(1)}, bf16[9,128,128]{2,1,0:T(8,...) custom-call(bf16[16,64,256]{2,1,0:T(8,128)(2,1)S(1)} %get-tuple-elem, ...), custom_call_target="tpu_custom_call" | custom-call | flops 3000000000 | bytes 6000000 | tf_op jit(solution)/shard_map/inner/pallas_call | solution.py:232
  25.3 0.9 %collective-permute-done.5.corner_b = bf16[2,9,8,256]{3,2,1,0:T(8,128)(2,1)S(1)} collective-permute-done((bf16[2,9,8,256]{3,2,1,0:T(8,128)(2,1)S(1)}, bf16[2,9,8,256]{3,2,1,0:T(8,128)(2,1)S(1)}, u32[]{:S(2)}, u32[]{:S(2)}) %collective-permute-start.5) | collective-permute-done | bytes 73760 | tf_op jit(solution)/shard_map/ppermute | solution.py:400
  26.2 0.0 collective-permute-done.4.corner_a
  26.2 0.0 collective-permute-done.2.lat_a
  26.2 0.0 collective-permute-done.3.lat_b
  26.2 0.0 copy-done
  26.2 0.0 copy-done.1
  26.2 0.0 copy-done.2
  26.2 9.0 %net.1 = f32[1280,128]{1,0:T(8,128)} custom-call(f32[1]{0:T(128)S(6)} %copy.14.noise, bf16[16,64,256]{2,1,0:T(8,128)(2,1)S(1)} %get-tuple-element.23.own_c, bf16[16,64,256]{2,1,0:T(8,128)(2,1)S(1)} %get-tuple-element.24.own_s, bf16[16,8,256]{2,1,0:T(8,128)(2,1)S(1)} %collective-permute-done.edge_a, bf16[16,8,256]{2,1,0:T(8,128)(2,1)S(1)} %collective-permute-done.1.edge_b, ...), custom_call_target="tpu_custom_call" | custom-call | tf_op jit(solution)/shard_map/net/pallas_call | solution.py:355
  (2 shorter events, 0.0 us)
Async XLA Ops:
  2.8 16.1 %collective-permute-start = (bf16[16,8,256]{2,1,0:T(8,128)(2,1)S(1)}, bf16[16,8,256]{2,1,0:T(8,128)(2,1)S(1)}, u32[]{:S(2)}, u32[]{:S(2)}) collective-permute-start(bf16[16,8,256]{2,1,0:T(8,128)(2,1)S(1)} %get-tuple-element.25), channel_id=1, source_target_pairs={{0,4},{1,5},{2,6},{3,7},{4,0},{5,1},{6,2},{7,3},{8,12},{9,13},{10,... | collective-permute-start | bytes 196616 | tf_op jit(solution)/shard_map/ppermute | solution.py:400
  5.4 13.6 %collective-permute-start.1 = (bf16[16,8,256]{2,1,0:T(8,128)(2,1)S(1)}, bf16[16,8,256]{2,1,0:T(8,128)(2,1)S(1)}, u32[]{:S(2)}, u32[]{:S(2)}) collective-permute-start(bf16[16,8,256]{2,1,0:T(8,128)(2,1)S(1)} %get-tuple-element.26), channel_id=1, source_target_pairs={{0,252},{1,253},{2,254},{3,255},{4,8},{5,9},{6,10},{7,11},{8,4},{9... | collective-permute-start | bytes 196616 | tf_op jit(solution)/shard_map/ppermute | solution.py:400
  13.3 12.9 %collective-permute-start.2 = (bf16[9,64,256]{2,1,0:T(8,128)(2,1)S(1)}, bf16[9,64,256]{2,1,0:T(8,128)(2,1)S(1)}, u32[]{:S(2)}, u32[]{:S(2)}) collective-permute-start(bf16[9,64,256]{2,1,0:T(8,128)(2,1)S(1)} %get-tuple-element.27), channel_id=1, source_target_pairs={{0,1},{1,0},{2,3},{3,2},{4,5},{5,4},{6,7},{7,6},{8,9},{9,8},{10,11... | collective-permute-start | bytes 884744 | tf_op jit(solution)/shard_map/ppermute | solution.py:400
  14.5 11.7 %collective-permute-start.3 = (bf16[9,64,256]{2,1,0:T(8,128)(2,1)S(1)}, bf16[9,64,256]{2,1,0:T(8,128)(2,1)S(1)}, u32[]{:S(2)}, u32[]{:S(2)}) collective-permute-start(bf16[9,64,256]{2,1,0:T(8,128)(2,1)S(1)} %get-tuple-element.28), channel_id=1, source_target_pairs={{1,2},{2,1},{5,6},{6,5},{9,10},{10,9},{13,14},{14,13},{17,18},{18,... | collective-permute-start | bytes 884744 | tf_op jit(solution)/shard_map/ppermute | solution.py:400
  19.0 7.2 %collective-permute-start.5 = (bf16[2,9,8,256]{3,2,1,0:T(8,128)(2,1)S(1)}, bf16[2,9,8,256]{3,2,1,0:T(8,128)(2,1)S(1)}, u32[]{:S(2)}, u32[]{:S(2)}) collective-permute-start(bf16[2,9,8,256]{3,2,1,0:T(8,128)(2,1)S(1)} %get-tuple-element.41), channel_id=1, source_target_pairs={{1,2},{2,1},{5,6},{6,5},{9,10},{10,9},{13,14},{14,13},{17,18},{18,... | collective-permute-start | bytes 221192 | tf_op jit(solution)/shard_map/ppermute | solution.py:400
  21.7 4.5 %collective-permute-start.4 = (bf16[2,9,8,256]{3,2,1,0:T(8,128)(2,1)S(1)}, bf16[2,9,8,256]{3,2,1,0:T(8,128)(2,1)S(1)}, u32[]{:S(2)}, u32[]{:S(2)}) collective-permute-start(bf16[2,9,8,256]{3,2,1,0:T(8,128)(2,1)S(1)} %get-tuple-element.42), channel_id=1, source_target_pairs={{0,1},{1,0},{2,3},{3,2},{4,5},{5,4},{6,7},{7,6},{8,9},{9,8},{10,11... | collective-permute-start | bytes 221192 | tf_op jit(solution)/shard_map/ppermute | solution.py:400
  21.9 4.3 %copy-start = (f32[1,80,16,128]{3,2,1,0:T(8,128)S(1)}, f32[1,80,16,128]{3,2,1,0:T(8,128)}, u32[]{:S(2)}) copy-start(f32[1,80,16,128]{3,2,1,0:T(8,128)} %param.14) | copy-start | bytes 1966084
  21.9 4.3 %copy-start.1 = (f32[128]{0:T(128)S(1)}, f32[128]{0:T(128)}, u32[]{:S(2)}) copy-start(f32[128]{0:T(128)} %param.20) | copy-start | bytes 1540
  22.0 4.2 %copy-start.2 = (f32[128]{0:T(128)S(1)}, f32[128]{0:T(128)}, u32[]{:S(2)}) copy-start(f32[128]{0:T(128)} %param.21) | copy-start | bytes 1540

commit v4 on v3

v4 whole, which is shorter than its diff:
```python
import functools

import jax
import jax.numpy as jnp
from jax import lax
from jax.experimental import pallas as pl
from jax.experimental.pallas import tpu as pltpu
from jax.sharding import PartitionSpec as P

F32 = jnp.float32
BF16 = jnp.bfloat16
PITCH = 72
EDGE = 4
STRIP = 16
ROWS = 16
PAIRS = 64
CH = 80
DEEP = 9
THIN = 4
VMEM = pltpu.VMEM
AXES = ("lon", "lat")


def swap_pairs(mesh_shape, lat, lon):
    n_lon, n_lat = mesh_shape
    pairs = []
    for o in range(n_lon):
        for a in range(n_lat):
            b, p = a, o
            if lat:
                b = a ^ 1 if lat == "A" else a - 1 + 2 * (a % 2)
            if lon:
                p = (o ^ 1 if lon == "A" else o - 1 + 2 * (o % 2)) % n_lon
            if 0 <= b < n_lat:
                pairs.append((o * n_lat + a, p * n_lat + b))
    return pairs


def silu(v):
    h = v * 0.5
    return h + h * jnp.tanh(h)


def matmul_nt(x, w):
    return lax.dot_general(x, w, (((1,), (1,)), ((), ())), preferred_element_type=F32)


def prep_body(
    noise, cond_hbm, state_hbm, k_in, k_noisy, own_c, own_s, left, right, small_a, small_b, lat_a, lat_b, w_in, w_noisy,
    cond, state, work, arrived,
):
    copies = [
        pltpu.make_async_copy(cond_hbm, cond, arrived.at[0]),
        pltpu.make_async_copy(state_hbm, state, arrived.at[1]),
        pltpu.make_async_copy(k_in, w_in.at[:, :CH, :], arrived.at[2]),
        pltpu.make_async_copy(k_noisy, w_noisy.at[:, :CH, :], arrived.at[3]),
    ]
    for copy in copies:
        copy.start()
    lat_even = lax.axis_index("lat") % 2 == 0
    sigma = jnp.full((1, 128), noise[0], F32)
    scale_in = 1.0 / jnp.sqrt(sigma * sigma + 0.25)
    row = lax.broadcasted_iota(jnp.int32, (128, 128), 0)
    col = lax.broadcasted_iota(jnp.int32, (128, 128), 1)
    pick = (col == jnp.where(row < PAIRS, 2 * row, 2 * (row - PAIRS) + 1)).astype(BF16)
    blank = jnp.zeros((128 - CH, 128), BF16)
    slot = lax.broadcasted_iota(jnp.int32, (8, 128), 0)
    for w in (w_in, w_noisy):
        w[:, CH:, :] = jnp.zeros((9, 128 - CH, 128), BF16)
    for copy in copies[:2]:
        copy.wait()
    work[...] = cond[...].astype(F32)
    for i in range(ROWS):
        c_row = work[pl.ds(i, CH, stride=ROWS), :].astype(BF16)
        s_row = (scale_in * state[pl.ds(i, CH, stride=ROWS), :]).astype(BF16)
        both = matmul_nt(pick, jnp.concatenate([c_row, blank, s_row, blank], 0))
        c_pair = jnp.concatenate([both[:PAIRS, :128], both[PAIRS:, :128]], 1)
        s_pair = jnp.concatenate([both[:PAIRS, 128:], both[PAIRS:, 128:]], 1)
        own_c[i] = c_pair.astype(BF16)
        own_s[i] = s_pair.astype(BF16)
        for half in range(2):
            lanes = slice(128 * half, 128 * half + 128)
            left[i, :, lanes] = jnp.where(slot < 5, c_pair[:8, lanes], pltpu.roll(s_pair[:8, lanes], 5, 0)).astype(BF16)
            right[i, :, lanes] = jnp.where(slot > 2, c_pair[-8:, lanes], pltpu.roll(s_pair[-8:, lanes], 3, 0)).astype(BF16)
    for side, edge in enumerate((left, right)):
        first, last = edge[:DEEP].astype(F32), edge[ROWS - DEEP :].astype(F32)
        small_a[side] = jnp.where(lat_even, last, first).astype(BF16)
        small_b[side] = jnp.where(lat_even, first, last).astype(BF16)
    lane = lax.broadcasted_iota(jnp.int32, (PAIRS, 128), 1)
    free = 128 - CH
    for k in range(DEEP):
        for half in range(2):
            lanes = slice(128 * half, 128 * half + 128)
            rows = []
            for first, s_first in ((0, 0), (ROWS - DEEP, ROWS - THIN)):
                value = own_c[first + k, :, lanes].astype(F32)
                n = 2 * k + half
                if n < 4 * THIN:
                    r, h = divmod(n // 2, 2)
                    part = own_s[s_first + r, :, 128 * h : 128 * h + 128].astype(F32)
                    part = pltpu.roll(part, (CH - free * (n % 2)) % 128, 1)
                    value = jnp.where(lane < CH, value, part)
                rows.append(value)
            lat_a[k, :, lanes] = jnp.where(lat_even, rows[1], rows[0]).astype(BF16)
            lat_b[k, :, lanes] = jnp.where(lat_even, rows[0], rows[1]).astype(BF16)
    for copy in copies[2:]:
        copy.wait()


def prep(noise, *args):
    vm = pl.BlockSpec(memory_space=VMEM)
    own = jax.ShapeDtypeStruct((ROWS, PAIRS, 256), BF16)
    edge = jax.ShapeDtypeStruct((ROWS, 8, 256), BF16)
    small = jax.ShapeDtypeStruct((2, DEEP, 8, 256), BF16)
    rows = jax.ShapeDtypeStruct((DEEP, PAIRS, 256), BF16)
    weights = jax.ShapeDtypeStruct((9, 128, 128), BF16)
    return pl.pallas_call(
        prep_body,
        out_shape=(own, own, edge, edge, small, small, rows, rows, weights, weights),
        in_specs=[pl.BlockSpec(memory_space=pltpu.SMEM)] + [pl.BlockSpec(memory_space=pltpu.HBM)] * 4,
        out_specs=[vm] * 10,
        scratch_shapes=[
            VMEM((CH * ROWS, 128), BF16),
            VMEM((CH * ROWS, 128), F32),
            VMEM((CH * ROWS, 128), F32),
            pltpu.SemaphoreType.DMA((4,)),
        ],
        compiler_params=pltpu.CompilerParams(vmem_limit_bytes=12 << 20),
        name="prep",
    )(noise, *args)


def pair_weights(w, di):
    k0, k1, k2 = w[3 * di], w[3 * di + 1], w[3 * di + 2]
    z = jnp.zeros_like(k0)
    c = jnp.concatenate
    return c([c([k1, k2], 1), c([k0, k1], 1), c([z, k0], 1), c([k2, z], 1)], 0)


def pair_weights_by_input(w, di):
    k0, k1, k2 = w[3 * di], w[3 * di + 1], w[3 * di + 2]
    z = jnp.zeros_like(k0)
    c = jnp.concatenate
    return c([c([k1, k0, z, k2], 1), c([k2, k1, k0, z], 1)], 0)


def pair_conv(x, w, centre, rows, by_input=False, pitch=PITCH):
    span = rows * pitch
    taps = [x[(centre + d - 1) * pitch : (centre + d - 1) * pitch + span, :] for d in range(3)]
    taps = jnp.concatenate(taps, 1)
    if by_input:
        weights = jnp.concatenate([pair_weights_by_input(w, d) for d in range(3)], 0)
        y = jnp.dot(taps, weights, preferred_element_type=F32)
    else:
        y = matmul_nt(taps, jnp.concatenate([pair_weights(w, d) for d in range(3)], 1))
    even = y[:, 0:128] + pltpu.roll(y[:, 256:384], 1, 0)
    odd = y[:, 128:256] + pltpu.roll(y[:, 384:512], span - 1, 0)
    return even, odd


def half_conv(x, w, centre, rows):
    span = rows * PITCH
    c = jnp.concatenate
    taps = c([x[(centre + d - 1) * PITCH : (centre + d - 1) * PITCH + span, :] for d in range(3)], 1)
    weights = c([c([w[3 * d + b] for d in range(3)], 1) for b in range(3)], 0)
    y = matmul_nt(taps, weights)
    n = y.shape[1] // 3
    return y[:, n : 2 * n] + pltpu.roll(y[:, :n], 1, 0) + pltpu.roll(y[:, 2 * n :], span - 1, 0)


def pool(x, w, centre, rows, pitch):
    even, odd = pair_conv(x, w, centre, rows, True, pitch)
    both = silu(even).astype(BF16).astype(F32) + silu(odd).astype(BF16).astype(F32)
    both = both.reshape(rows // 2, 2, pitch, 128)
    return (both[:, 0] + both[:, 1]) * 0.25


def band(n_lat):
    lat = lax.axis_index("lat")
    return (lat > 0).astype(F32), (lat < n_lat - 1).astype(F32)


def inner_body(
    n_lat,
    own_c, own_s, lat_a, lat_b, w_in, w_noisy, k_coarse, k_deeper, k_guide, k_block, k_branch, k_out,
    w_coarse, w_deeper, w_guide, w_block, w_branch, w_out, pooled, opening,
    x_c, x_s, arrived,
):
    moves = [
        (k_coarse, w_coarse), (k_deeper, w_deeper), (k_guide, w_guide),
        (k_block, w_block), (k_branch, w_branch), (k_out, w_out.at[:, :CH, :]),
    ]
    copies = [pltpu.make_async_copy(src, dst, arrived.at[n]) for n, (src, dst) in enumerate(moves)]
    for copy in copies:
        copy.start()
    w_out[:, CH:, :] = jnp.zeros((9, 128 - CH, 128), BF16)
    top, bottom = band(n_lat)
    lat_even = lax.axis_index("lat") % 2 == 0
    free = 128 - CH
    lane = lax.broadcasted_iota(jnp.int32, (1, 128), 1)
    x_c[DEEP * PAIRS : (DEEP + ROWS) * PAIRS, :] = own_c[...].reshape(ROWS * PAIRS, 256)
    x_s[THIN * PAIRS : (THIN + ROWS) * PAIRS, :] = own_s[...].reshape(ROWS * PAIRS, 256)
    for below in range(2):

        def received(k, lanes):
            a, b = lat_a[k, :, lanes].astype(F32), lat_b[k, :, lanes].astype(F32)
            return jnp.where(lat_even, a, b) if below else jnp.where(lat_even, b, a)

        for k in range(DEEP):
            at = (DEEP + ROWS + k if below else k) * PAIRS
            x_c[at : at + PAIRS, :] = received(k, slice(None)).astype(BF16)
        for r in range(THIN):
            at = (THIN + ROWS + r if below else r) * PAIRS
            for h in range(2):
                n = 2 * (2 * r + h)
                parts = [
                    pltpu.roll(received(m // 2, slice(128 * (m % 2), 128 * (m % 2) + 128)), (128 - CH + free * (m % 2)) % 128, 1)
                    for m in (n, n + 1)
                ]
                x_s[at : at + PAIRS, 128 * h : 128 * h + 128] = jnp.where(lane < free, *parts).astype(BF16)
    for row, rows in ((0, 5), (5, 5), (10, 6)):
        mean = pool(x_c, w_in, 1 + 2 * row, 2 * rows, PAIRS)
        for q in range(rows):
            v = mean[q]
            if row + q < 4:
                v = v * top
            if row + q >= 12:
                v = v * bottom
            at = (row + q) * PITCH + EDGE
            pooled[at : at + PAIRS, :] = v.astype(BF16)
    for row, rows in ((0, 10), (10, 12)):
        for half, v in enumerate(pair_conv(x_s, w_noisy, 1 + row, rows, True, PAIRS)):
            for q in range(rows):
                at = (row + q) * PITCH + EDGE
                opening[at : at + PAIRS, 128 * half : 128 * half + 128] = v[q * PAIRS : (q + 1) * PAIRS]
    for copy in copies:
        copy.wait()


def inner(n_lat, *args):
    vm = pl.BlockSpec(memory_space=VMEM)
    wide = lambda n, k: jax.ShapeDtypeStruct((9, n, k), BF16)
    out_shape = (
        wide(256, 128), wide(256, 256), jax.ShapeDtypeStruct((128, 256), BF16),
        wide(128, 128), wide(128, 128), wide(128, 128),
        jax.ShapeDtypeStruct((16 * PITCH, 128), BF16), jax.ShapeDtypeStruct((22 * PITCH, 256), F32),
    )
    return pl.pallas_call(
        functools.partial(inner_body, n_lat),
        out_shape=out_shape,
        in_specs=[vm] * 6 + [pl.BlockSpec(memory_space=pltpu.HBM)] * 6,
        out_specs=[vm] * len(out_shape),
        scratch_shapes=[
            VMEM((34 * PAIRS, 256), BF16),
            VMEM((24 * PAIRS, 256), BF16),
            pltpu.SemaphoreType.DMA((6,)),
        ],
        compiler_params=pltpu.CompilerParams(vmem_limit_bytes=20 << 20),
        cost_estimate=pl.CostEstimate(flops=3 * 10**9, bytes_accessed=6 * 10**6, transcendentals=10**6),
        name="inner",
    )(*args)


def net_body(
    n_lat,
    noise, sent_a, sent_b, edge_a, edge_b, state, scale, shift,
    w_in, w_noisy, w_coarse, w_deeper, w_guide, w_block, w_branch, w_out, pooled_in, opening,
    out, x_c, x_s, pooled, middle, guide, hidden, inner, mixed, turn,
):
    top, bottom = band(n_lat)
    lon_even = lax.axis_index("lon") % 2 == 0
    sigma = jnp.full((1, 128), noise[0], F32)
    variance = sigma * sigma + 0.25
    scale_skip = 0.25 / variance
    scale_out = 0.5 * sigma / jnp.sqrt(variance)
    noise_code = jnp.log(sigma) / 4.0

    slot = lax.broadcasted_iota(jnp.int32, (8, 256), 0)
    for k in range(DEEP + ROWS + DEEP):
        sa, sb = sent_a[k].astype(F32), sent_b[k].astype(F32)
        ea, eb = edge_a[k].astype(F32), edge_b[k].astype(F32)
        own_left, own_right = jnp.where(lon_even, sb, sa), jnp.where(lon_even, sa, sb)
        left, right = jnp.where(lon_even, eb, ea), jnp.where(lon_even, ea, eb)
        strip = [
            pltpu.roll(jnp.where(slot > 2, left, own_left), 5, 0),
            pltpu.roll(jnp.where(slot < 5, right, own_right), 3, 0),
        ]
        x_c[k * STRIP : (k + 1) * STRIP, :] = jnp.concatenate(strip, 0).astype(BF16)
        r = k - (DEEP - THIN)
        if 0 <= r < THIN + ROWS + THIN:
            strip = [
                jnp.where(slot < 2, pltpu.roll(left, 7, 0), jnp.where(slot < 5, pltpu.roll(own_left, 5, 0), 0.0)),
                jnp.where(slot > 4, right, jnp.where(slot > 1, pltpu.roll(own_right, 2, 0), 0.0)),
            ]
            x_s[r * STRIP : (r + 1) * STRIP, :] = jnp.concatenate(strip, 0).astype(BF16)

    def put(ref, row, rows, value, above, below, lanes=slice(None)):
        over = min(max(above - row, 0), rows)
        under = min(max(row + rows - below, 0), rows)
        parts = [value[over * PITCH : (rows - under) * PITCH]]
        if over:
            parts.insert(0, value[: over * PITCH] * top)
        if under:
            parts.append(value[(rows - under) * PITCH :] * bottom)
        ref[row * PITCH : (row + rows) * PITCH, lanes] = jnp.concatenate(parts, 0).astype(ref.dtype)

    place = lax.broadcasted_iota(jnp.int32, (8, 128), 0)
    pooled[...] = pooled_in[...]
    mean = pool(x_c, w_in, 1, 32, STRIP)
    for row in range(16):
        v = mean[row] * top if row < 4 else mean[row] * bottom if row > 11 else mean[row]
        at = row * PITCH
        first = pooled_in[at : at + 8, :].astype(F32)
        pooled[at : at + 8, :] = jnp.where(place < 5, pltpu.roll(v[:8], 7, 0), first).astype(BF16)
        last = pooled_in[at + 64 : at + 72, :].astype(F32)
        pooled[at + 64 : at + 72, :] = jnp.where(place > 2, pltpu.roll(v[8:], 1, 0), last).astype(BF16)
    for row, rows in ((0, 8), (8, 6)):
        put(middle, row, rows, silu(half_conv(pooled, w_coarse, row + 1, rows)), 3, 11)
    embedded = scale[...] * noise_code + shift[...]
    for row, rows in ((0, 6), (6, 6)):
        d = silu(half_conv(middle, w_deeper, row + 1, rows)).astype(BF16)
        guide[row * PITCH : (row + rows) * PITCH, :] = matmul_nt(d, w_guide[...]) + embedded
    strips = pair_conv(x_s, w_noisy, 1, 22, True, STRIP)
    for row, rows in ((0, 12), (12, 10)):
        for half, strip in enumerate(strips):
            lanes = slice(128 * half, 128 * half + 128)
            parts = []
            for q in range(row, row + rows):
                at = q * PITCH
                left = pltpu.roll(strip[q * STRIP : q * STRIP + 8], 2, 0)
                first = jnp.where(place < 2, 0.0, jnp.where(place < 5, left, opening[at : at + 8, lanes]))
                right = pltpu.roll(strip[q * STRIP + 8 : q * STRIP + 16], 7, 0)
                last = jnp.where(place > 5, 0.0, jnp.where(place > 2, right, opening[at + 64 : at + 72, lanes]))
                g = (q + 1) // 2 * PITCH
                parts.append(jnp.concatenate([first, opening[at + 8 : at + 64, lanes], last], 0) + guide[g : g + PITCH, :])
            put(hidden, row, rows, silu(jnp.concatenate(parts, 0)), 3, 19, lanes)
    for row in (0, 10):
        for half, v in enumerate(pair_conv(hidden, w_block, 1 + row, 10)):
            put(inner, row, 10, silu(v), 2, 18, slice(128 * half, 128 * half + 128))
    for row, rows in ((0, 10), (10, 8)):
        h = hidden[(2 + row) * PITCH : (2 + row + rows) * PITCH, :].astype(F32)
        for half, v in enumerate(pair_conv(inner, w_branch, 1 + row, rows)):
            lanes = slice(128 * half, 128 * half + 128)
            put(mixed, row, rows, silu(v + h[:, lanes]), 1, 17, lanes)
    for first, rows in ((0, 6), (6, 6), (12, 4)):
        even, odd = pair_conv(mixed, w_out, 1 + first, rows)
        for q in range(rows):
            row = first + q
            at = slice(q * PITCH, (q + 1) * PITCH)
            turn[row, pl.ds(0, PITCH, stride=2), :] = even[at]
            turn[row, pl.ds(1, PITCH, stride=2), :] = odd[at]
            head = turn[row, 2 * EDGE : 2 * (EDGE + PAIRS), :].T[:CH]
            here = pl.ds(row, CH, stride=ROWS)
            out[here, :] = scale_skip * state[here, :] + scale_out * head


def net(n_lat, *args):
    vm = pl.BlockSpec(memory_space=VMEM)
    return pl.pallas_call(
        functools.partial(net_body, n_lat),
        out_shape=jax.ShapeDtypeStruct((CH * ROWS, 128), F32),
        in_specs=[pl.BlockSpec(memory_space=pltpu.SMEM)] + [vm] * (len(args) - 1),
        out_specs=vm,
        scratch_shapes=[
            VMEM((34 * STRIP, 256), BF16),
            VMEM((24 * STRIP, 256), BF16),
            VMEM((16 * PITCH, 128), BF16),
            VMEM((14 * PITCH, 256), BF16),
            VMEM((12 * PITCH, 128), F32),
            VMEM((22 * PITCH, 256), BF16),
            VMEM((20 * PITCH, 256), BF16),
            VMEM((18 * PITCH, 256), BF16),
            VMEM((ROWS, 2 * PITCH, 128), F32),
        ],
        compiler_params=pltpu.CompilerParams(vmem_limit_bytes=24 << 20),
        name="net",
    )(*args)


def on_device(
    mesh_shape,
    conditions,
    noisy_state,
    noise_level,
    kernel_input,
    kernel_coarse,
    kernel_deeper,
    guide_weight,
    time_scale,
    time_shift,
    kernel_noisy,
    kernel_block,
    kernel_branch,
    kernel_output,
):
    lon_even, lat_even = lax.axis_index("lon") % 2 == 0, lax.axis_index("lat") % 2 == 0
    cond = conditions.reshape(CH * ROWS, 128)
    state = noisy_state.reshape(CH * ROWS, 128)
    by_input = lambda kernel: kernel.transpose(0, 2, 1)
    in_hbm = lambda *values: [pltpu.with_memory_space_constraint(value, pltpu.HBM) for value in values]
    own_c, own_s, left, right, small_a, small_b, lat_a, lat_b, w_in, w_noisy = prep(
        noise_level, *in_hbm(cond, state, by_input(kernel_input), by_input(kernel_noisy))
    )
    permute = lambda value, a, o: lax.ppermute(value, AXES, swap_pairs(mesh_shape, a, o))
    small_b = permute(small_b, "B", None)
    small_a = permute(small_a, "A", None)
    lat_b = permute(lat_b, "B", None)
    lat_a = permute(lat_a, "A", None)
    above, below = jnp.where(lat_even, small_b, small_a), jnp.where(lat_even, small_a, small_b)
    left, right = (jnp.concatenate([above[n], edge, below[n]]) for n, edge in enumerate((left, right)))
    sent_a, sent_b = jnp.where(lon_even, right, left), jnp.where(lon_even, left, right)
    edge_b = permute(sent_b, None, "B")
    edge_a = permute(sent_a, None, "A")
    weights = in_hbm(kernel_coarse, kernel_deeper, guide_weight, kernel_block, kernel_branch, kernel_output)
    rest = inner(mesh_shape[1], own_c, own_s, lat_a, lat_b, w_in, w_noisy, *weights)
    out = net(
        mesh_shape[1], noise_level, sent_a, sent_b, edge_a, edge_b, state,
        time_scale[None], time_shift[None], w_in, w_noisy, *rest,
    )
    return out.reshape(noisy_state.shape)


def solution(mesh):
    tile = P(None, "lat", "lon")
    member = P(None, None, "lat", "lon")
    return jax.shard_map(
        functools.partial(on_device, (mesh.shape["lon"], mesh.shape["lat"])),
        mesh=mesh,
        in_specs=(tile, member) + (P(),) * 11,
        out_specs=member,
        check_vma=False,
    )
```

time: 35.3 us -> 33.7 us (0.955)
  starting transfers between devices: 19 us -> 17.3 us
    ppermute x6, starting transfers between devices: 19 us -> 17.3 us  [on_device(): lax.ppermute(value, AXES, swap_pairs(mesh_shape, a, o))]
    pallas_call x2, Pallas kernels: 5.46 us -> 6.4 us  [the longest x1 4.21 us: inner(): pl.pallas_call(functools.partial(inner_body, n_lat), out_shape=out_shape,...]
    pallas_call x1, Pallas kernels: 8.96 us -> 8.29 us  [net(): pl.pallas_call(functools.partial(net_body, n_lat), out_shape=jax.ShapeDty...]
  transfers between devices with their start and end apart: 6 -> 6, of which waited for: 1 -> 1; matrix products, arithmetic and copies ran while one was open for 0% -> 0% of each run, Pallas kernels for 9% -> 13%
where the time goes in v4:
time: 33.7 us; the launch traced here: 33.6 us
  starting transfers between devices  17.3 us (51%)
  Pallas kernels  14.7 us (44%)
  between operations  0.79 us (2%)
  waiting for transfers between devices  0.65 us (2%)
    ppermute x6, starting transfers between devices, on_device(): lax.ppermute(value, AXES, swap_pairs(mesh_shape, a, o))  17.3 us
    pallas_call x1, Pallas kernels, net(): pl.pallas_call(functools.partial(net_body, n_lat), out_shape=jax.ShapeDty...  8.29 us
    pallas_call x1, Pallas kernels, inner(): pl.pallas_call(functools.partial(inner_body, n_lat), out_shape=out_shape,...  4.21 us
    pallas_call x1, Pallas kernels, prep(): pl.pallas_call(prep_body, out_shape=(own, own, edge, edge, small, small,...  2.19 us
  transfers between devices with their start and end apart: 6, of which 1 were waited for; matrix products, arithmetic and copies ran while one was open for 0% of the time, Pallas kernels for 13%

profile of v4, /device:TPU:1, one launch (start us, length us, event | category | flops | bytes accessed | tf_op | source)
XLA Modules:
  0.0 33.6 jit_solution(17746541973871419673)
XLA Ops:
  0.7 2.2 %prep.1 = (bf16[16,64,256]{2,1,0:T(8,128)(2,1)S(1)}, bf16[16,64,256]{2,1,0:T(8,128)(2,1)S(1)}, bf16[16,8,256]{2,1,0:T(8,128)(2,1)S(1)}, bf16[16,8,256]{2,1,0:T(8...) custom-call(f32[1]{0:T(128)S(6)} %copy.14.noise, ...), custom_call_target="tpu_custom_call" | custom-call | tf_op jit(solution)/shard_map/prep/pallas_call | solution.py:117
  2.8 6.2 %collective-permute-start = (bf16[2,9,8,256]{3,2,1,0:T(8,128)(2,1)S(1)}, bf16[2,9,8,256]{3,2,1,0:T(8,128)(2,1)S(1)}, u32[]{:S(2)}, u32[]{:S(2)}) collective-permute-start(bf16[2,9,8,256]{3,2,1,0:T(8,128)(2,1)S(1)} %get-tuple-element.23), channel_id=1, source_target_pairs={{1,2},{2,1},{5,6},{6,5},{9,10},{10,9},{13,14},{14,13},{17,18},{18,... | collective-permute-start | bytes 221192 | tf_op jit(solution)/shard_map/ppermute | solution.py:404
  9.1 0.1 collective-permute-start.1
  9.2 0.5 %collective-permute-start.4 = (bf16[9,64,256]{2,1,0:T(8,128)(2,1)S(1)}, bf16[9,64,256]{2,1,0:T(8,128)(2,1)S(1)}, u32[]{:S(2)}, u32[]{:S(2)}) collective-permute-start(bf16[9,64,256]{2,1,0:T(8,128)(2,1)S(1)} %get-tuple-element.31), channel_id=1, source_target_pairs={{0,1},{1,0},{2,3},{3,2},{4,5},{5,4},{6,7},{7,6},{8,9},{9,8},{10,11... | collective-permute-start | bytes 884744 | tf_op jit(solution)/shard_map/ppermute | solution.py:404
  9.7 1.9 %collective-permute-start.5 = (bf16[9,64,256]{2,1,0:T(8,128)(2,1)S(1)}, bf16[9,64,256]{2,1,0:T(8,128)(2,1)S(1)}, u32[]{:S(2)}, u32[]{:S(2)}) collective-permute-start(bf16[9,64,256]{2,1,0:T(8,128)(2,1)S(1)} %get-tuple-element.32), channel_id=1, source_target_pairs={{1,2},{2,1},{5,6},{6,5},{9,10},{10,9},{13,14},{14,13},{17,18},{18,... | collective-permute-start | bytes 884744 | tf_op jit(solution)/shard_map/ppermute | solution.py:404
  11.6 0.0 collective-permute-done
  11.6 0.0 collective-permute-done.1
  11.7 8.6 %collective-permute-start.3 = (bf16[34,8,256]{2,1,0:T(8,128)(2,1)S(1)}, bf16[34,8,256]{2,1,0:T(8,128)(2,1)S(1)}, u32[]{:S(2)}, u32[]{:S(2)}) collective-permute-start(bf16[34,8,256]{2,1,0:T(8,128)(2,1)S(1)} %get-tuple-element.41.sent_b), channel_id=1, source_target_pairs={{0,252},{1,253},{2,254},{3,255},{4,8},{5,9},{6,10},{7,11},{8,4},{9... | collective-permute-start | bytes 417800 | tf_op jit(solution)/shard_map/ppermute | solution.py:404
  20.4 0.0 collective-permute-start.2
  20.4 0.0 collective-permute-done.4.lat_a
  20.4 0.6 %collective-permute-done.5.lat_b = bf16[9,64,256]{2,1,0:T(8,128)(2,1)S(1)} collective-permute-done((bf16[9,64,256]{2,1,0:T(8,128)(2,1)S(1)}, bf16[9,64,256]{2,1,0:T(8,128)(2,1)S(1)}, u32[]{:S(2)}, u32[]{:S(2)}) %collective-permute-start.5) | collective-permute-done | bytes 294944 | tf_op jit(solution)/shard_map/ppermute | solution.py:404
  21.0 0.0 copy-start
  21.0 0.0 copy-start.1
  21.0 0.0 copy-start.2
  21.0 4.2 %inner.1 = (bf16[9,256,128]{2,1,0:T(8,128)(2,1)S(1)}, bf16[9,256,256]{2,1,0:T(8,128)(2,1)S(1)}, bf16[128,256]{1,0:T(8,128)(2,1)S(1)}, bf16[9,128,128]{2,1,0:T(8,...) custom-call(bf16[16,64,256]{2,1,0:T(8,128)(2,1)S(1)} %get-tuple-elem, ...), custom_call_target="tpu_custom_call" | custom-call | flops 3000000000 | bytes 6000000 | tf_op jit(solution)/shard_map/inner/pallas_call | solution.py:248
  25.2 0.0 collective-permute-done.3.edge_b
  25.2 0.0 collective-permute-done.2.edge_a
  25.2 0.0 copy-done
  25.2 0.0 copy-done.1
  25.3 0.0 copy-done.2
  25.3 8.3 %net.1 = f32[1280,128]{1,0:T(8,128)} custom-call(f32[1]{0:T(128)S(6)} %copy.14.noise, bf16[34,8,256]{2,1,0:T(8,128)(2,1)S(1)} %get-tuple-element.42.sent_a, bf16[34,8,256]{2,1,0:T(8,128)(2,1)S(1)} %get-tuple-element.41.sent_b, bf16[34,8,256]{2,1,0:T(8,128)(2,1)S(1)} %collective-permute-done.2.edge_a, bf16[34,8,256]{2,1,0:T(8,128)(2,1)S(1)} %collective-permute-done.3.edge_b, ...), custom_call_target="tpu_custom_call" | custom-call | tf_op jit(solution)/shard_map/net/pallas_call | solution.py:359
  (3 shorter events, 0.1 us)
Async XLA Ops:
  2.8 8.8 %collective-permute-start = (bf16[2,9,8,256]{3,2,1,0:T(8,128)(2,1)S(1)}, bf16[2,9,8,256]{3,2,1,0:T(8,128)(2,1)S(1)}, u32[]{:S(2)}, u32[]{:S(2)}) collective-permute-start(bf16[2,9,8,256]{3,2,1,0:T(8,128)(2,1)S(1)} %get-tuple-element.23), channel_id=1, source_target_pairs={{1,2},{2,1},{5,6},{6,5},{9,10},{10,9},{13,14},{14,13},{17,18},{18,... | collective-permute-start | bytes 221192 | tf_op jit(solution)/shard_map/ppermute | solution.py:404
  9.1 2.5 %collective-permute-start.1 = (bf16[2,9,8,256]{3,2,1,0:T(8,128)(2,1)S(1)}, bf16[2,9,8,256]{3,2,1,0:T(8,128)(2,1)S(1)}, u32[]{:S(2)}, u32[]{:S(2)}) collective-permute-start(bf16[2,9,8,256]{3,2,1,0:T(8,128)(2,1)S(1)} %get-tuple-element.24), channel_id=1, source_target_pairs={{0,1},{1,0},{2,3},{3,2},{4,5},{5,4},{6,7},{7,6},{8,9},{9,8},{10,11... | collective-permute-start | bytes 221192 | tf_op jit(solution)/shard_map/ppermute | solution.py:404
  9.2 11.2 %collective-permute-start.4 = (bf16[9,64,256]{2,1,0:T(8,128)(2,1)S(1)}, bf16[9,64,256]{2,1,0:T(8,128)(2,1)S(1)}, u32[]{:S(2)}, u32[]{:S(2)}) collective-permute-start(bf16[9,64,256]{2,1,0:T(8,128)(2,1)S(1)} %get-tuple-element.31), channel_id=1, source_target_pairs={{0,1},{1,0},{2,3},{3,2},{4,5},{5,4},{6,7},{7,6},{8,9},{9,8},{10,11... | collective-permute-start | bytes 884744 | tf_op jit(solution)/shard_map/ppermute | solution.py:404
  9.7 11.3 %collective-permute-start.5 = (bf16[9,64,256]{2,1,0:T(8,128)(2,1)S(1)}, bf16[9,64,256]{2,1,0:T(8,128)(2,1)S(1)}, u32[]{:S(2)}, u32[]{:S(2)}) collective-permute-start(bf16[9,64,256]{2,1,0:T(8,128)(2,1)S(1)} %get-tuple-element.32), channel_id=1, source_target_pairs={{1,2},{2,1},{5,6},{6,5},{9,10},{10,9},{13,14},{14,13},{17,18},{18,... | collective-permute-start | bytes 884744 | tf_op jit(solution)/shard_map/ppermute | solution.py:404
  11.7 13.5 %collective-permute-start.3 = (bf16[34,8,256]{2,1,0:T(8,128)(2,1)S(1)}, bf16[34,8,256]{2,1,0:T(8,128)(2,1)S(1)}, u32[]{:S(2)}, u32[]{:S(2)}) collective-permute-start(bf16[34,8,256]{2,1,0:T(8,128)(2,1)S(1)} %get-tuple-element.41.sent_b), channel_id=1, source_target_pairs={{0,252},{1,253},{2,254},{3,255},{4,8},{5,9},{6,10},{7,11},{8,4},{9... | collective-permute-start | bytes 417800 | tf_op jit(solution)/shard_map/ppermute | solution.py:404
  20.4 4.9 %collective-permute-start.2 = (bf16[34,8,256]{2,1,0:T(8,128)(2,1)S(1)}, bf16[34,8,256]{2,1,0:T(8,128)(2,1)S(1)}, u32[]{:S(2)}, u32[]{:S(2)}) collective-permute-start(bf16[34,8,256]{2,1,0:T(8,128)(2,1)S(1)} %get-tuple-element.42.sent_a), channel_id=1, source_target_pairs={{0,4},{1,5},{2,6},{3,7},{4,0},{5,1},{6,2},{7,3},{8,12},{9,13},{10,... | collective-permute-start | bytes 417800 | tf_op jit(solution)/shard_map/ppermute | solution.py:404
  21.0 4.2 %copy-start = (f32[1,80,16,128]{3,2,1,0:T(8,128)S(1)}, f32[1,80,16,128]{3,2,1,0:T(8,128)}, u32[]{:S(2)}) copy-start(f32[1,80,16,128]{3,2,1,0:T(8,128)} %param.14) | copy-start | bytes 1966084
  21.0 4.3 %copy-start.1 = (f32[128]{0:T(128)S(1)}, f32[128]{0:T(128)}, u32[]{:S(2)}) copy-start(f32[128]{0:T(128)} %param.20) | copy-start | bytes 1540
  21.0 4.3 %copy-start.2 = (f32[128]{0:T(128)S(1)}, f32[128]{0:T(128)}, u32[]{:S(2)}) copy-start(f32[128]{0:T(128)} %param.21) | copy-start | bytes 1540

commit v5 on v4

--- a/solution.py
+++ b/solution.py
@@ -76,8 +76,8 @@
         both = matmul_nt(pick, jnp.concatenate([c_row, blank, s_row, blank], 0))
         c_pair = jnp.concatenate([both[:PAIRS, :128], both[PAIRS:, :128]], 1)
         s_pair = jnp.concatenate([both[:PAIRS, 128:], both[PAIRS:, 128:]], 1)
-        own_c[i] = c_pair.astype(BF16)
-        own_s[i] = s_pair.astype(BF16)
+        own_c[i * PAIRS : (i + 1) * PAIRS, :] = c_pair.astype(BF16)
+        own_s[i * PAIRS : (i + 1) * PAIRS, :] = s_pair.astype(BF16)
         for half in range(2):
             lanes = slice(128 * half, 128 * half + 128)
             left[i, :, lanes] = jnp.where(slot < 5, c_pair[:8, lanes], pltpu.roll(s_pair[:8, lanes], 5, 0)).astype(BF16)
@@ -93,11 +93,13 @@
             lanes = slice(128 * half, 128 * half + 128)
             rows = []
             for first, s_first in ((0, 0), (ROWS - DEEP, ROWS - THIN)):
-                value = own_c[first + k, :, lanes].astype(F32)
+                at = (first + k) * PAIRS
+                value = own_c[at : at + PAIRS, lanes].astype(F32)
                 n = 2 * k + half
                 if n < 4 * THIN:
                     r, h = divmod(n // 2, 2)
-                    part = own_s[s_first + r, :, 128 * h : 128 * h + 128].astype(F32)
+                    at = (s_first + r) * PAIRS
+                    part = own_s[at : at + PAIRS, 128 * h : 128 * h + 128].astype(F32)
                     part = pltpu.roll(part, (CH - free * (n % 2)) % 128, 1)
                     value = jnp.where(lane < CH, value, part)
                 rows.append(value)
@@ -109,7 +111,7 @@
 
 def prep(noise, *args):
     vm = pl.BlockSpec(memory_space=VMEM)
-    own = jax.ShapeDtypeStruct((ROWS, PAIRS, 256), BF16)
+    own = jax.ShapeDtypeStruct((ROWS * PAIRS, 256), BF16)
     edge = jax.ShapeDtypeStruct((ROWS, 8, 256), BF16)
     small = jax.ShapeDtypeStruct((2, DEEP, 8, 256), BF16)
     rows = jax.ShapeDtypeStruct((DEEP, PAIRS, 256), BF16)
@@ -180,9 +182,40 @@
     return (lat > 0).astype(F32), (lat < n_lat - 1).astype(F32)
 
 
+def early():
+    return lax.axis_index("lon") % 8 < 2
+
+
+def own_body(ahead, own_c, own_s, w_in, w_noisy, pooled, opening):
+    @pl.when(early() if ahead else jnp.logical_not(early()))
+    def _():
+        mean = pool(own_c, w_in, 2, 12, PAIRS)
+        for q in range(6):
+            pooled[q * PITCH + EDGE : q * PITCH + EDGE + PAIRS, :] = mean[q].astype(BF16)
+        for row, rows in ((0, 6), (6, 8)):
+            for half, v in enumerate(pair_conv(own_s, w_noisy, 1 + row, rows, True, PAIRS)):
+                for q in range(rows):
+                    at = (row + q) * PITCH + EDGE
+                    opening[at : at + PAIRS, 128 * half : 128 * half + 128] = v[q * PAIRS : (q + 1) * PAIRS]
+
+
+def own_rows(ahead, *args):
+    vm = pl.BlockSpec(memory_space=VMEM)
+    return pl.pallas_call(
+        functools.partial(own_body, ahead),
+        out_shape=(jax.ShapeDtypeStruct((6 * PITCH, 128), BF16), jax.ShapeDtypeStruct((14 * PITCH, 256), F32)),
+        in_specs=[vm] * len(args),
+        out_specs=[vm] * 2,
+        compiler_params=pltpu.CompilerParams(vmem_limit_bytes=6 << 20),
+        cost_estimate=pl.CostEstimate(flops=2 * 10**9, bytes_accessed=3 * 10**6, transcendentals=5 * 10**5),
+        name="own_rows",
+    )(*args)
+
+
 def inner_body(
     n_lat,
-    own_c, own_s, lat_a, lat_b, w_in, w_noisy, k_coarse, k_deeper, k_guide, k_block, k_branch, k_out,
+    own_c, own_s, lat_a, lat_b, w_in, w_noisy, pool_1, open_1, pool_2, open_2,
+    k_coarse, k_deeper, k_guide, k_block, k_branch, k_out,
     w_coarse, w_deeper, w_guide, w_block, w_branch, w_out, pooled, opening,
     x_c, x_s, arrived,
 ):
@@ -198,8 +231,9 @@
     lat_even = lax.axis_index("lat") % 2 == 0
     free = 128 - CH
     lane = lax.broadcasted_iota(jnp.int32, (1, 128), 1)
-    x_c[DEEP * PAIRS : (DEEP + ROWS) * PAIRS, :] = own_c[...].reshape(ROWS * PAIRS, 256)
-    x_s[THIN * PAIRS : (THIN + ROWS) * PAIRS, :] = own_s[...].reshape(ROWS * PAIRS, 256)
+    for x, own, n, deep in ((x_c, own_c, 3, DEEP), (x_s, own_s, 2, THIN)):
+        x[deep * PAIRS : (deep + n) * PAIRS, :] = own[: n * PAIRS, :]
+        x[(deep + n) * PAIRS : (deep + 2 * n) * PAIRS, :] = own[(ROWS - n) * PAIRS :, :]
     for below in range(2):
 
         def received(k, lanes):
@@ -207,10 +241,10 @@
             return jnp.where(lat_even, a, b) if below else jnp.where(lat_even, b, a)
 
         for k in range(DEEP):
-            at = (DEEP + ROWS + k if below else k) * PAIRS
+            at = (DEEP + 6 + k if below else k) * PAIRS
             x_c[at : at + PAIRS, :] = received(k, slice(None)).astype(BF16)
         for r in range(THIN):
-            at = (THIN + ROWS + r if below else r) * PAIRS
+            at = (THIN + 4 + r if below else r) * PAIRS
             for h in range(2):
                 n = 2 * (2 * r + h)
                 parts = [
@@ -218,9 +252,9 @@
                     for m in (n, n + 1)
                 ]
                 x_s[at : at + PAIRS, 128 * h : 128 * h + 128] = jnp.where(lane < free, *parts).astype(BF16)
-    for row, rows in ((0, 5), (5, 5), (10, 6)):
-        mean = pool(x_c, w_in, 1 + 2 * row, 2 * rows, PAIRS)
-        for q in range(rows):
+    for row, centre in ((0, 1), (11, 13)):
+        mean = pool(x_c, w_in, centre, 10, PAIRS)
+        for q in range(5):
             v = mean[q]
             if row + q < 4:
                 v = v * top
@@ -228,11 +262,14 @@
                 v = v * bottom
             at = (row + q) * PITCH + EDGE
             pooled[at : at + PAIRS, :] = v.astype(BF16)
-    for row, rows in ((0, 10), (10, 12)):
-        for half, v in enumerate(pair_conv(x_s, w_noisy, 1 + row, rows, True, PAIRS)):
-            for q in range(rows):
+    for row, centre in ((0, 1), (18, 7)):
+        for half, v in enumerate(pair_conv(x_s, w_noisy, centre, 4, True, PAIRS)):
+            for q in range(4):
                 at = (row + q) * PITCH + EDGE
                 opening[at : at + PAIRS, 128 * half : 128 * half + 128] = v[q * PAIRS : (q + 1) * PAIRS]
+    first = early()
+    pooled[5 * PITCH : 11 * PITCH, :] = jnp.where(first, pool_1[...].astype(F32), pool_2[...].astype(F32)).astype(BF16)
+    opening[4 * PITCH : 18 * PITCH, :] = jnp.where(first, open_1[...], open_2[...])
     for copy in copies:
         copy.wait()
 
@@ -248,14 +285,14 @@
     return pl.pallas_call(
         functools.partial(inner_body, n_lat),
         out_shape=out_shape,
-        in_specs=[vm] * 6 + [pl.BlockSpec(memory_space=pltpu.HBM)] * 6,
+        in_specs=[vm] * 10 + [pl.BlockSpec(memory_space=pltpu.HBM)] * 6,
         out_specs=[vm] * len(out_shape),
         scratch_shapes=[
-            VMEM((34 * PAIRS, 256), BF16),
             VMEM((24 * PAIRS, 256), BF16),
+            VMEM((12 * PAIRS, 256), BF16),
             pltpu.SemaphoreType.DMA((6,)),
         ],
-        compiler_params=pltpu.CompilerParams(vmem_limit_bytes=20 << 20),
+        compiler_params=pltpu.CompilerParams(vmem_limit_bytes=10 << 20),
         cost_estimate=pl.CostEstimate(flops=3 * 10**9, bytes_accessed=6 * 10**6, transcendentals=10**6),
         name="inner",
     )(*args)
@@ -314,7 +351,7 @@
         pooled[at : at + 8, :] = jnp.where(place < 5, pltpu.roll(v[:8], 7, 0), first).astype(BF16)
         last = pooled_in[at + 64 : at + 72, :].astype(F32)
         pooled[at + 64 : at + 72, :] = jnp.where(place > 2, pltpu.roll(v[8:], 1, 0), last).astype(BF16)
-    for row, rows in ((0, 8), (8, 6)):
+    for row, rows in ((0, 14),):
         put(middle, row, rows, silu(half_conv(pooled, w_coarse, row + 1, rows)), 3, 11)
     embedded = scale[...] * noise_code + shift[...]
     for row, rows in ((0, 6), (6, 6)):
@@ -372,7 +409,7 @@
             VMEM((18 * PITCH, 256), BF16),
             VMEM((ROWS, 2 * PITCH, 128), F32),
         ],
-        compiler_params=pltpu.CompilerParams(vmem_limit_bytes=24 << 20),
+        compiler_params=pltpu.CompilerParams(vmem_limit_bytes=14 << 20),
         name="net",
     )(*args)
 
@@ -409,10 +446,18 @@
     above, below = jnp.where(lat_even, small_b, small_a), jnp.where(lat_even, small_a, small_b)
     left, right = (jnp.concatenate([above[n], edge, below[n]]) for n, edge in enumerate((left, right)))
     sent_a, sent_b = jnp.where(lon_even, right, left), jnp.where(lon_even, left, right)
+    ahead = own_rows(True, own_c, own_s, w_in, w_noisy)
+    sent_a, sent_b, ahead, now_c, now_s = lax.optimization_barrier((sent_a, sent_b, ahead, own_c, own_s))
+    near = swap_pairs(mesh_shape, None, "A")
+    seam = lambda index: index // mesh_shape[1] % 8 < 2
+    edge_s = lax.ppermute(sent_a, AXES, [(i, j if seam(i) else i) for i, j in near])
     edge_b = permute(sent_b, None, "B")
-    edge_a = permute(sent_a, None, "A")
+    sent_late, edge_s = lax.optimization_barrier((sent_a, edge_s))
+    edge_a = lax.ppermute(sent_late, AXES, [(i, i if seam(i) else j) for i, j in near])
+    during = own_rows(False, now_c, now_s, w_in, w_noisy)
     weights = in_hbm(kernel_coarse, kernel_deeper, guide_weight, kernel_block, kernel_branch, kernel_output)
-    rest = inner(mesh_shape[1], own_c, own_s, lat_a, lat_b, w_in, w_noisy, *weights)
+    rest = inner(mesh_shape[1], own_c, own_s, lat_a, lat_b, w_in, w_noisy, *ahead, *during, *weights)
+    edge_a = jnp.where(lax.axis_index("lon") % 8 < 2, edge_s, edge_a)
     out = net(
         mesh_shape[1], noise_level, sent_a, sent_b, edge_a, edge_b, state,
         time_scale[None], time_shift[None], w_in, w_noisy, *rest,

time: 33.7 us -> 35.9 us (1.065)
  local copies, waits for them, and re-layouts: 0.03 us -> 1.01 us
  waiting for transfers between devices: 0.65 us -> 1.29 us
    ppermute x0 -> x2, starting transfers between devices: none -> 4.51 us  [the longest x1 3.68 us: on_device(): lax.ppermute(sent_a, AXES, [(i, j if seam(i) else i) for i, j in near])]
    ppermute x6 -> x5, starting transfers between devices: 17.3 us -> 12.9 us  [on_device(): lax.ppermute(value, AXES, swap_pairs(mesh_shape, a, o))]
    pallas_call x0 -> x2, Pallas kernels: none -> 1.55 us  [own_rows(): pl.pallas_call(functools.partial(own_body, ahead), out_shape=(jax.ShapeDt...]
    pallas_call x1, Pallas kernels: 4.21 us -> 2.83 us  [inner(): pl.pallas_call(functools.partial(inner_body, n_lat), out_shape=out_shape,...]
    unnamed x6 -> x10, local copies, waits for them, and re-layouts: 0.01 us -> 1 us
    ppermute x6 -> x5, waiting for transfers between devices: 0.65 us -> 1.29 us  [on_device(): lax.ppermute(value, AXES, swap_pairs(mesh_shape, a, o))]
  transfers between devices with their start and end apart: 6 -> 7, of which waited for: 1 -> 1; matrix products, arithmetic and copies ran while one was open for 0% -> 0% of each run, Pallas kernels for 13% -> 12%
where the time goes in v5:
time: 35.9 us; the launch traced here: 35.7 us
  starting transfers between devices  17.5 us (49%)
  Pallas kernels  15 us (42%)
  waiting for transfers between devices  1.29 us (4%)
  local copies, waits for them, and re-layouts  1.01 us (3%)
  between operations  0.82 us (2%)
    ppermute x5, starting transfers between devices, on_device(): lax.ppermute(value, AXES, swap_pairs(mesh_shape, a, o))  12.9 us
    pallas_call x1, Pallas kernels, net(): pl.pallas_call(functools.partial(net_body, n_lat), out_shape=jax.ShapeDty...  8.48 us
    ppermute x1, starting transfers between devices, on_device(): lax.ppermute(sent_a, AXES, [(i, j if seam(i) else i) for i, j in near])  3.68 us
    pallas_call x1, Pallas kernels, inner(): pl.pallas_call(functools.partial(inner_body, n_lat), out_shape=out_shape,...  2.83 us
    pallas_call x1, Pallas kernels, prep(): pl.pallas_call(prep_body, out_shape=(own, own, edge, edge, small, small,...  2.19 us
    pallas_call x2, Pallas kernels, own_rows(): pl.pallas_call(functools.partial(own_body, ahead), out_shape=(jax.ShapeDt...  1.55 us
    ppermute x5, waiting for transfers between devices, on_device(): lax.ppermute(value, AXES, swap_pairs(mesh_shape, a, o))  1.29 us
    unnamed x10, local copies, waits for them, and re-layouts  1 us
  transfers between devices with their start and end apart: 7, of which 1 were waited for; matrix products, arithmetic and copies ran while one was open for 0% of the time, Pallas kernels for 12%

profile of v5, /device:TPU:1, one launch (start us, length us, event | category | flops | bytes accessed | tf_op | source)
XLA Modules:
  0.0 35.7 jit_solution(3672861593239197150)
XLA Ops:
  0.7 2.2 %prep.1 = (bf16[1024,256]{1,0:T(8,128)(2,1)S(1)}, bf16[1024,256]{1,0:T(8,128)(2,1)S(1)}, bf16[16,8,256]{2,1,0:T(8,128)(2,1)S(1)}, bf16[16,8,256]{2,1,0:T(8,128)(...) custom-call(f32[1]{0:T(128)S(6)} %copy.14.noise, ...), custom_call_target="tpu_custom_call" | custom-call | tf_op jit(solution)/shard_map/prep/pallas_call | solution.py:119
  2.8 6.2 %collective-permute-start = (bf16[2,9,8,256]{3,2,1,0:T(8,128)(2,1)S(1)}, bf16[2,9,8,256]{3,2,1,0:T(8,128)(2,1)S(1)}, u32[]{:S(2)}, u32[]{:S(2)}) collective-permute-start(bf16[2,9,8,256]{3,2,1,0:T(8,128)(2,1)S(1)} %get-tuple-element.35), channel_id=1, source_target_pairs={{1,2},{2,1},{5,6},{6,5},{9,10},{10,9},{13,14},{14,13},{17,18},{18,... | collective-permute-start | bytes 221192 | tf_op jit(solution)/shard_map/ppermute | solution.py:441
  9.1 0.1 collective-permute-start.1
  9.2 0.5 %collective-permute-start.5 = (bf16[9,64,256]{2,1,0:T(8,128)(2,1)S(1)}, bf16[9,64,256]{2,1,0:T(8,128)(2,1)S(1)}, u32[]{:S(2)}, u32[]{:S(2)}) collective-permute-start(bf16[9,64,256]{2,1,0:T(8,128)(2,1)S(1)} %get-tuple-element.49), channel_id=1, source_target_pairs={{0,1},{1,0},{2,3},{3,2},{4,5},{5,4},{6,7},{7,6},{8,9},{9,8},{10,11... | collective-permute-start | bytes 884744 | tf_op jit(solution)/shard_map/ppermute | solution.py:441
  9.7 1.9 %collective-permute-start.6 = (bf16[9,64,256]{2,1,0:T(8,128)(2,1)S(1)}, bf16[9,64,256]{2,1,0:T(8,128)(2,1)S(1)}, u32[]{:S(2)}, u32[]{:S(2)}) collective-permute-start(bf16[9,64,256]{2,1,0:T(8,128)(2,1)S(1)} %get-tuple-element.50), channel_id=1, source_target_pairs={{1,2},{2,1},{5,6},{6,5},{9,10},{10,9},{13,14},{14,13},{17,18},{18,... | collective-permute-start | bytes 884744 | tf_op jit(solution)/shard_map/ppermute | solution.py:441
  11.6 1.5 %own_rows.2 = (bf16[432,128]{1,0:T(8,128)(2,1)S(1)}, f32[1008,256]{1,0:T(8,128)S(1)}) custom-call(bf16[1024,256]{1,0:T(8,128)(2,1)S(1)} %get-tuple-element.53.own_c, bf16[1024,256]{1,0:T(8,128)(2,1)S(1)} %get-tuple-element.54.own_s, bf16[9,128,128]{2,1,0:T(8,128)(2,1)S(1)} %get-tuple-element.41.w_in, bf16[9,128,128]{2,1,0:T(8,128)(2,1)S(1)} %get-tuple-element.42.w_noisy), custom_call_target="tpu_custom_call" | custom-call | flops 2000000000 | bytes 3000000 | tf_op jit(solution)/shard_map/own_rows/pallas_call | solution.py:204
  13.1 0.0 copy-start.3
  13.1 1.0 %copy-done.3 = f32[1008,256]{1,0:T(8,128)} copy-done((f32[1008,256]{1,0:T(8,128)}, f32[1008,256]{1,0:T(8,128)S(1)}, u32[]{:S(2)}) %copy-start.3) | copy-done | bytes 1032216
  14.1 0.0 collective-permute-done
  14.1 0.0 collective-permute-done.1
  14.2 0.0 copy-start.4
  14.2 3.7 %collective-permute-start.2 = (bf16[34,8,256]{2,1,0:T(8,128)(2,1)S(1)}, bf16[34,8,256]{2,1,0:T(8,128)(2,1)S(1)}, u32[]{:S(2)}, u32[]{:S(2)}) collective-permute-start(bf16[34,8,256]{2,1,0:T(8,128)(2,1)S(1)} %get-tuple-element.48.sent_a), channel_id=1, source_target_pairs={{0,4},{1,5},{2,6},{3,7},{4,0},{5,1},{6,2},{7,3},{8,8},{9,9},{10,10... | collective-permute-start | bytes 417800 | tf_op jit(solution)/shard_map/ppermute | solution.py:453
  17.9 4.2 %collective-permute-start.4 = (bf16[34,8,256]{2,1,0:T(8,128)(2,1)S(1)}, bf16[34,8,256]{2,1,0:T(8,128)(2,1)S(1)}, u32[]{:S(2)}, u32[]{:S(2)}) collective-permute-start(bf16[34,8,256]{2,1,0:T(8,128)(2,1)S(1)} %get-tuple-element.46.sent_b), channel_id=1, source_target_pairs={{0,252},{1,253},{2,254},{3,255},{4,8},{5,9},{6,10},{7,11},{8,4},{9... | collective-permute-start | bytes 417800 | tf_op jit(solution)/shard_map/ppermute | solution.py:441
  22.1 0.0 collective-permute-done.2
  22.1 0.8 %collective-permute-start.3 = (bf16[34,8,256]{2,1,0:T(8,128)(2,1)S(1)}, bf16[34,8,256]{2,1,0:T(8,128)(2,1)S(1)}, u32[]{:S(2)}, u32[]{:S(2)}) collective-permute-start(bf16[34,8,256]{2,1,0:T(8,128)(2,1)S(1)} %get-tuple-element.48.sent_a), channel_id=1, source_target_pairs={{0,0},{1,1},{2,2},{3,3},{4,4},{5,5},{6,6},{7,7},{8,12},{9,13},{10,... | collective-permute-start | bytes 417800 | tf_op jit(solution)/shard_map/ppermute | solution.py:456
  23.0 0.0 collective-permute-done.5.lat_a
  23.0 0.0 collective-permute-done.6.lat_b
  23.0 0.0 copy-done.4
  23.0 0.0 copy-start
  23.0 0.0 copy-start.1
  23.0 0.0 copy-start.2
  23.1 2.8 %inner.1 = (bf16[9,256,128]{2,1,0:T(8,128)(2,1)S(1)}, bf16[9,256,256]{2,1,0:T(8,128)(2,1)S(1)}, bf16[128,256]{1,0:T(8,128)(2,1)S(1)}, bf16[9,128,128]{2,1,0:T(8,...) custom-call(bf16[1024,256]{1,0:T(8,128)(2,1)S(1)} %get-tuple-element, ...), custom_call_target="tpu_custom_call" | custom-call | flops 3000000000 | bytes 6000000 | tf_op jit(solution)/shard_map/inner/pallas_call | solution.py:285
  25.9 0.0 collective-permute-done.3
  25.9 1.3 %collective-permute-done.4.edge_b = bf16[34,8,256]{2,1,0:T(8,128)(2,1)S(1)} collective-permute-done((bf16[34,8,256]{2,1,0:T(8,128)(2,1)S(1)}, bf16[34,8,256]{2,1,0:T(8,128)(2,1)S(1)}, u32[]{:S(2)}, u32[]{:S(2)}) %collective-permute-start.4) | collective-permute-done | bytes 139296 | tf_op jit(solution)/shard_map/ppermute | solution.py:441
  27.2 0.0 copy-done
  27.2 0.0 copy-done.1
  27.2 0.0 copy-done.2
  27.2 8.5 %net.1 = f32[1280,128]{1,0:T(8,128)} custom-call(f32[1]{0:T(128)S(6)} %copy.14.noise, bf16[34,8,256]{2,1,0:T(8,128)(2,1)S(1)} %get-tuple-element.48.sent_a, bf16[34,8,256]{2,1,0:T(8,128)(2,1)S(1)} %get-tuple-element.46.sent_b, bf16[34,8,256]{2,1,0:T(8,128)(2,1)S(1)} %broadcast_select_fusion.edge_a, bf16[34,8,256]{2,1,0:T(8,128)(2,1)S(1)} %collective-permute-done.4.edge_b, ...), custom_call_target="tpu_custom_call" | custom-call | tf_op jit(solution)/shard_map/net/pallas_call | solution.py:396
  (5 shorter events, 0.1 us)
Async XLA Ops:
  2.8 11.3 %collective-permute-start = (bf16[2,9,8,256]{3,2,1,0:T(8,128)(2,1)S(1)}, bf16[2,9,8,256]{3,2,1,0:T(8,128)(2,1)S(1)}, u32[]{:S(2)}, u32[]{:S(2)}) collective-permute-start(bf16[2,9,8,256]{3,2,1,0:T(8,128)(2,1)S(1)} %get-tuple-element.35), channel_id=1, source_target_pairs={{1,2},{2,1},{5,6},{6,5},{9,10},{10,9},{13,14},{14,13},{17,18},{18,... | collective-permute-start | bytes 221192 | tf_op jit(solution)/shard_map/ppermute | solution.py:441
  9.1 5.1 %collective-permute-start.1 = (bf16[2,9,8,256]{3,2,1,0:T(8,128)(2,1)S(1)}, bf16[2,9,8,256]{3,2,1,0:T(8,128)(2,1)S(1)}, u32[]{:S(2)}, u32[]{:S(2)}) collective-permute-start(bf16[2,9,8,256]{3,2,1,0:T(8,128)(2,1)S(1)} %get-tuple-element.36), channel_id=1, source_target_pairs={{0,1},{1,0},{2,3},{3,2},{4,5},{5,4},{6,7},{7,6},{8,9},{9,8},{10,11... | collective-permute-start | bytes 221192 | tf_op jit(solution)/shard_map/ppermute | solution.py:441
  9.2 13.8 %collective-permute-start.5 = (bf16[9,64,256]{2,1,0:T(8,128)(2,1)S(1)}, bf16[9,64,256]{2,1,0:T(8,128)(2,1)S(1)}, u32[]{:S(2)}, u32[]{:S(2)}) collective-permute-start(bf16[9,64,256]{2,1,0:T(8,128)(2,1)S(1)} %get-tuple-element.49), channel_id=1, source_target_pairs={{0,1},{1,0},{2,3},{3,2},{4,5},{5,4},{6,7},{7,6},{8,9},{9,8},{10,11... | collective-permute-start | bytes 884744 | tf_op jit(solution)/shard_map/ppermute | solution.py:441
  9.7 13.3 %collective-permute-start.6 = (bf16[9,64,256]{2,1,0:T(8,128)(2,1)S(1)}, bf16[9,64,256]{2,1,0:T(8,128)(2,1)S(1)}, u32[]{:S(2)}, u32[]{:S(2)}) collective-permute-start(bf16[9,64,256]{2,1,0:T(8,128)(2,1)S(1)} %get-tuple-element.50), channel_id=1, source_target_pairs={{1,2},{2,1},{5,6},{6,5},{9,10},{10,9},{13,14},{14,13},{17,18},{18,... | collective-permute-start | bytes 884744 | tf_op jit(solution)/shard_map/ppermute | solution.py:441
  13.1 1.0 %copy-start.3 = (f32[1008,256]{1,0:T(8,128)}, f32[1008,256]{1,0:T(8,128)S(1)}, u32[]{:S(2)}) copy-start(f32[1008,256]{1,0:T(8,128)S(1)} %get-tuple-element.52.open_1) | copy-start | bytes 3096580
  14.2 8.8 %copy-start.4 = (f32[1008,256]{1,0:T(8,128)S(1)}, f32[1008,256]{1,0:T(8,128)}, u32[]{:S(2)}) copy-start(f32[1008,256]{1,0:T(8,128)} %copy-done.3) | copy-start | bytes 3096580
  14.2 7.9 %collective-permute-start.2 = (bf16[34,8,256]{2,1,0:T(8,128)(2,1)S(1)}, bf16[34,8,256]{2,1,0:T(8,128)(2,1)S(1)}, u32[]{:S(2)}, u32[]{:S(2)}) collective-permute-start(bf16[34,8,256]{2,1,0:T(8,128)(2,1)S(1)} %get-tuple-element.48.sent_a), channel_id=1, source_target_pairs={{0,4},{1,5},{2,6},{3,7},{4,0},{5,1},{6,2},{7,3},{8,8},{9,9},{10,10... | collective-permute-start | bytes 417800 | tf_op jit(solution)/shard_map/ppermute | solution.py:453
  17.9 9.3 %collective-permute-start.4 = (bf16[34,8,256]{2,1,0:T(8,128)(2,1)S(1)}, bf16[34,8,256]{2,1,0:T(8,128)(2,1)S(1)}, u32[]{:S(2)}, u32[]{:S(2)}) collective-permute-start(bf16[34,8,256]{2,1,0:T(8,128)(2,1)S(1)} %get-tuple-element.46.sent_b), channel_id=1, source_target_pairs={{0,252},{1,253},{2,254},{3,255},{4,8},{5,9},{6,10},{7,11},{8,4},{9... | collective-permute-start | bytes 417800 | tf_op jit(solution)/shard_map/ppermute | solution.py:441
  22.1 3.8 %collective-permute-start.3 = (bf16[34,8,256]{2,1,0:T(8,128)(2,1)S(1)}, bf16[34,8,256]{2,1,0:T(8,128)(2,1)S(1)}, u32[]{:S(2)}, u32[]{:S(2)}) collective-permute-start(bf16[34,8,256]{2,1,0:T(8,128)(2,1)S(1)} %get-tuple-element.48.sent_a), channel_id=1, source_target_pairs={{0,0},{1,1},{2,2},{3,3},{4,4},{5,5},{6,6},{7,7},{8,12},{9,13},{10,... | collective-permute-start | bytes 417800 | tf_op jit(solution)/shard_map/ppermute | solution.py:456
  23.0 4.2 %copy-start = (f32[1,80,16,128]{3,2,1,0:T(8,128)S(1)}, f32[1,80,16,128]{3,2,1,0:T(8,128)}, u32[]{:S(2)}) copy-start(f32[1,80,16,128]{3,2,1,0:T(8,128)} %param.14) | copy-start | bytes 1966084
  23.0 4.2 %copy-start.1 = (f32[128]{0:T(128)S(1)}, f32[128]{0:T(128)}, u32[]{:S(2)}) copy-start(f32[128]{0:T(128)} %param.20) | copy-start | bytes 1540
  23.0 4.2 %copy-start.2 = (f32[128]{0:T(128)S(1)}, f32[128]{0:T(128)}, u32[]{:S(2)}) copy-start(f32[128]{0:T(128)} %param.21) | copy-start | bytes 1540

commit v6 on v5

--- a/solution.py
+++ b/solution.py
@@ -182,31 +182,25 @@
     return (lat > 0).astype(F32), (lat < n_lat - 1).astype(F32)
 
 
-def early():
-    return lax.axis_index("lon") % 8 < 2
-
-
-def own_body(ahead, own_c, own_s, w_in, w_noisy, pooled, opening):
-    @pl.when(early() if ahead else jnp.logical_not(early()))
-    def _():
-        mean = pool(own_c, w_in, 2, 12, PAIRS)
-        for q in range(6):
-            pooled[q * PITCH + EDGE : q * PITCH + EDGE + PAIRS, :] = mean[q].astype(BF16)
-        for row, rows in ((0, 6), (6, 8)):
-            for half, v in enumerate(pair_conv(own_s, w_noisy, 1 + row, rows, True, PAIRS)):
-                for q in range(rows):
-                    at = (row + q) * PITCH + EDGE
-                    opening[at : at + PAIRS, 128 * half : 128 * half + 128] = v[q * PAIRS : (q + 1) * PAIRS]
-
-
-def own_rows(ahead, *args):
+def own_body(own_c, own_s, w_in, w_noisy, pooled, opening):
+    mean = pool(own_c, w_in, 2, 12, PAIRS)
+    for q in range(6):
+        pooled[q * PITCH + EDGE : q * PITCH + EDGE + PAIRS, :] = mean[q].astype(BF16)
+    for row, rows in ((0, 6), (6, 8)):
+        for half, v in enumerate(pair_conv(own_s, w_noisy, 1 + row, rows, True, PAIRS)):
+            for q in range(rows):
+                at = (row + q) * PITCH + EDGE
+                opening[at : at + PAIRS, 128 * half : 128 * half + 128] = v[q * PAIRS : (q + 1) * PAIRS]
+
+
+def own_rows(*args):
     vm = pl.BlockSpec(memory_space=VMEM)
     return pl.pallas_call(
-        functools.partial(own_body, ahead),
+        own_body,
         out_shape=(jax.ShapeDtypeStruct((6 * PITCH, 128), BF16), jax.ShapeDtypeStruct((14 * PITCH, 256), F32)),
         in_specs=[vm] * len(args),
         out_specs=[vm] * 2,
-        compiler_params=pltpu.CompilerParams(vmem_limit_bytes=6 << 20),
+        compiler_params=pltpu.CompilerParams(vmem_limit_bytes=12 << 20),
         cost_estimate=pl.CostEstimate(flops=2 * 10**9, bytes_accessed=3 * 10**6, transcendentals=5 * 10**5),
         name="own_rows",
     )(*args)
@@ -214,7 +208,7 @@
 
 def inner_body(
     n_lat,
-    own_c, own_s, lat_a, lat_b, w_in, w_noisy, pool_1, open_1, pool_2, open_2,
+    own_c, own_s, lat_b, lat_a, w_in, w_noisy, pool_own, open_own,
     k_coarse, k_deeper, k_guide, k_block, k_branch, k_out,
     w_coarse, w_deeper, w_guide, w_block, w_branch, w_out, pooled, opening,
     x_c, x_s, arrived,
@@ -267,9 +261,8 @@
             for q in range(4):
                 at = (row + q) * PITCH + EDGE
                 opening[at : at + PAIRS, 128 * half : 128 * half + 128] = v[q * PAIRS : (q + 1) * PAIRS]
-    first = early()
-    pooled[5 * PITCH : 11 * PITCH, :] = jnp.where(first, pool_1[...].astype(F32), pool_2[...].astype(F32)).astype(BF16)
-    opening[4 * PITCH : 18 * PITCH, :] = jnp.where(first, open_1[...], open_2[...])
+    pooled[5 * PITCH : 11 * PITCH, :] = pool_own[...]
+    opening[4 * PITCH : 18 * PITCH, :] = open_own[...]
     for copy in copies:
         copy.wait()
 
@@ -285,14 +278,14 @@
     return pl.pallas_call(
         functools.partial(inner_body, n_lat),
         out_shape=out_shape,
-        in_specs=[vm] * 10 + [pl.BlockSpec(memory_space=pltpu.HBM)] * 6,
+        in_specs=[vm] * 8 + [pl.BlockSpec(memory_space=pltpu.HBM)] * 6,
         out_specs=[vm] * len(out_shape),
         scratch_shapes=[
             VMEM((24 * PAIRS, 256), BF16),
             VMEM((12 * PAIRS, 256), BF16),
             pltpu.SemaphoreType.DMA((6,)),
         ],
-        compiler_params=pltpu.CompilerParams(vmem_limit_bytes=10 << 20),
+        compiler_params=pltpu.CompilerParams(vmem_limit_bytes=20 << 20),
         cost_estimate=pl.CostEstimate(flops=3 * 10**9, bytes_accessed=6 * 10**6, transcendentals=10**6),
         name="inner",
     )(*args)
@@ -300,7 +293,7 @@
 
 def net_body(
     n_lat,
-    noise, sent_a, sent_b, edge_a, edge_b, state, scale, shift,
+    noise, sent_b, sent_a, edge_b, edge_a, state, scale, shift,
     w_in, w_noisy, w_coarse, w_deeper, w_guide, w_block, w_branch, w_out, pooled_in, opening,
     out, x_c, x_s, pooled, middle, guide, hidden, inner, mixed, turn,
 ):
@@ -409,7 +402,7 @@
             VMEM((18 * PITCH, 256), BF16),
             VMEM((ROWS, 2 * PITCH, 128), F32),
         ],
-        compiler_params=pltpu.CompilerParams(vmem_limit_bytes=14 << 20),
+        compiler_params=pltpu.CompilerParams(vmem_limit_bytes=24 << 20),
         name="net",
     )(*args)
 
@@ -446,20 +439,14 @@
     above, below = jnp.where(lat_even, small_b, small_a), jnp.where(lat_even, small_a, small_b)
     left, right = (jnp.concatenate([above[n], edge, below[n]]) for n, edge in enumerate((left, right)))
     sent_a, sent_b = jnp.where(lon_even, right, left), jnp.where(lon_even, left, right)
-    ahead = own_rows(True, own_c, own_s, w_in, w_noisy)
-    sent_a, sent_b, ahead, now_c, now_s = lax.optimization_barrier((sent_a, sent_b, ahead, own_c, own_s))
-    near = swap_pairs(mesh_shape, None, "A")
-    seam = lambda index: index // mesh_shape[1] % 8 < 2
-    edge_s = lax.ppermute(sent_a, AXES, [(i, j if seam(i) else i) for i, j in near])
+    sent_b, sent_a, now_c, now_s = lax.optimization_barrier((sent_b, sent_a, own_c, own_s))
     edge_b = permute(sent_b, None, "B")
-    sent_late, edge_s = lax.optimization_barrier((sent_a, edge_s))
-    edge_a = lax.ppermute(sent_late, AXES, [(i, i if seam(i) else j) for i, j in near])
-    during = own_rows(False, now_c, now_s, w_in, w_noisy)
+    edge_a = permute(sent_a, None, "A")
+    during = own_rows(now_c, now_s, w_in, w_noisy)
     weights = in_hbm(kernel_coarse, kernel_deeper, guide_weight, kernel_block, kernel_branch, kernel_output)
-    rest = inner(mesh_shape[1], own_c, own_s, lat_a, lat_b, w_in, w_noisy, *ahead, *during, *weights)
-    edge_a = jnp.where(lax.axis_index("lon") % 8 < 2, edge_s, edge_a)
+    rest = inner(mesh_shape[1], own_c, own_s, lat_b, lat_a, w_in, w_noisy, *during, *weights)
     out = net(
-        mesh_shape[1], noise_level, sent_a, sent_b, edge_a, edge_b, state,
+        mesh_shape[1], noise_level, sent_b, sent_a, edge_b, edge_a, state,
         time_scale[None], time_shift[None], w_in, w_noisy, *rest,
     )
     return out.reshape(noisy_state.shape)

time: 35.9 us -> 33.5 us (0.933)
  waiting for transfers between devices: 1.29 us -> 0.02 us
  local copies, waits for them, and re-layouts: 1.01 us -> 0.03 us
  starting transfers between devices: 17.5 us -> 17 us
    ppermute x2 -> x0, starting transfers between devices: 4.51 us -> none  [the longest x1 3.68 us: on_device(): lax.ppermute(sent_a, AXES, [(i, j if seam(i) else i) for i, j in near])]
    ppermute x5 -> x6, starting transfers between devices: 12.9 us -> 17 us  [on_device(): lax.ppermute(value, AXES, swap_pairs(mesh_shape, a, o))]
    ppermute x5 -> x6, waiting for transfers between devices: 1.29 us -> 0.02 us  [on_device(): lax.ppermute(value, AXES, swap_pairs(mesh_shape, a, o))]
    unnamed x10 -> x6, local copies, waits for them, and re-layouts: 1 us -> 0.02 us
    pallas_call x2 -> x1, Pallas kernels: 1.55 us -> 1.53 us  [own_rows(): pl.pallas_call(own_body, out_shape=(jax.ShapeDtypeStruct((6 * PITCH, 128)...]
  transfers between devices with their start and end apart: 7 -> 6, of which waited for: 1 -> 0; matrix products, arithmetic and copies ran while one was open for 0% -> 0% of each run, Pallas kernels for 12% -> 14%
where the time goes in v6:
time: 33.5 us; the launch traced here: 33.1 us
  starting transfers between devices  17 us (51%)
  Pallas kernels  15.2 us (45%)
  between operations  0.85 us (3%)
    ppermute x6, starting transfers between devices, on_device(): lax.ppermute(value, AXES, swap_pairs(mesh_shape, a, o))  17 us
    pallas_call x1, Pallas kernels, net(): pl.pallas_call(functools.partial(net_body, n_lat), out_shape=jax.ShapeDty...  8.48 us
    pallas_call x1, Pallas kernels, inner(): pl.pallas_call(functools.partial(inner_body, n_lat), out_shape=out_shape,...  2.96 us
    pallas_call x1, Pallas kernels, prep(): pl.pallas_call(prep_body, out_shape=(own, own, edge, edge, small, small,...  2.19 us
    pallas_call x1, Pallas kernels, own_rows(): pl.pallas_call(own_body, out_shape=(jax.ShapeDtypeStruct((6 * PITCH, 128)...  1.53 us
  transfers between devices with their start and end apart: 6, of which 0 were waited for; matrix products, arithmetic and copies ran while one was open for 0% of the time, Pallas kernels for 14%

profile of v6, /device:TPU:1, one launch (start us, length us, event | category | flops | bytes accessed | tf_op | source)
XLA Modules:
  0.0 33.1 jit_solution(4224778610596733873)
XLA Ops:
  0.7 2.2 %prep.1 = (bf16[1024,256]{1,0:T(8,128)(2,1)S(1)}, bf16[1024,256]{1,0:T(8,128)(2,1)S(1)}, bf16[16,8,256]{2,1,0:T(8,128)(2,1)S(1)}, bf16[16,8,256]{2,1,0:T(8,128)(...) custom-call(f32[1]{0:T(128)S(6)} %copy.14.noise, ...), custom_call_target="tpu_custom_call" | custom-call | tf_op jit(solution)/shard_map/prep/pallas_call | solution.py:119
  2.8 6.2 %collective-permute-start = (bf16[2,9,8,256]{3,2,1,0:T(8,128)(2,1)S(1)}, bf16[2,9,8,256]{3,2,1,0:T(8,128)(2,1)S(1)}, u32[]{:S(2)}, u32[]{:S(2)}) collective-permute-start(bf16[2,9,8,256]{3,2,1,0:T(8,128)(2,1)S(1)} %get-tuple-element.29), channel_id=1, source_target_pairs={{1,2},{2,1},{5,6},{6,5},{9,10},{10,9},{13,14},{14,13},{17,18},{18,... | collective-permute-start | bytes 221192 | tf_op jit(solution)/shard_map/ppermute | solution.py:434
  9.1 0.1 collective-permute-start.1
  9.2 1.9 %collective-permute-start.4 = (bf16[9,64,256]{2,1,0:T(8,128)(2,1)S(1)}, bf16[9,64,256]{2,1,0:T(8,128)(2,1)S(1)}, u32[]{:S(2)}, u32[]{:S(2)}) collective-permute-start(bf16[9,64,256]{2,1,0:T(8,128)(2,1)S(1)} %get-tuple-element.39), channel_id=1, source_target_pairs={{1,2},{2,1},{5,6},{6,5},{9,10},{10,9},{13,14},{14,13},{17,18},{18,... | collective-permute-start | bytes 884744 | tf_op jit(solution)/shard_map/ppermute | solution.py:434
  11.1 0.1 collective-permute-start.5
  11.2 0.0 collective-permute-done
  11.2 0.0 collective-permute-done.1
  11.3 8.6 %collective-permute-start.2 = (bf16[34,8,256]{2,1,0:T(8,128)(2,1)S(1)}, bf16[34,8,256]{2,1,0:T(8,128)(2,1)S(1)}, u32[]{:S(2)}, u32[]{:S(2)}) collective-permute-start(bf16[34,8,256]{2,1,0:T(8,128)(2,1)S(1)} %get-tuple-element.35.sent_b), channel_id=1, source_target_pairs={{0,252},{1,253},{2,254},{3,255},{4,8},{5,9},{6,10},{7,11},{8,4},{9... | collective-permute-start | bytes 417800 | tf_op jit(solution)/shard_map/ppermute | solution.py:434
  20.0 0.0 collective-permute-start.3
  20.0 1.5 %own_rows.1 = (bf16[432,128]{1,0:T(8,128)(2,1)S(1)}, f32[1008,256]{1,0:T(8,128)S(1)}) custom-call(bf16[1024,256]{1,0:T(8,128)(2,1)S(1)} %get-tuple-element.41.own_c, bf16[1024,256]{1,0:T(8,128)(2,1)S(1)} %get-tuple-element.42.own_s, bf16[9,128,128]{2,1,0:T(8,128)(2,1)S(1)} %get-tuple-element.37.w_in, bf16[9,128,128]{2,1,0:T(8,128)(2,1)S(1)} %get-tuple-element.38.w_noisy), custom_call_target="tpu_custom_call" | custom-call | flops 2000000000 | bytes 3000000 | tf_op jit(solution)/shard_map/own_rows/pallas_call | solution.py:198
  21.5 0.0 collective-permute-done.4.lat_b
  21.5 0.0 collective-permute-done.5.lat_a
  21.5 0.0 copy-start
  21.5 0.0 copy-start.1
  21.6 0.0 copy-start.2
  21.6 3.0 %inner.1 = (bf16[9,256,128]{2,1,0:T(8,128)(2,1)S(1)}, bf16[9,256,256]{2,1,0:T(8,128)(2,1)S(1)}, bf16[128,256]{1,0:T(8,128)(2,1)S(1)}, bf16[9,128,128]{2,1,0:T(8,...) custom-call(bf16[1024,256]{1,0:T(8,128)(2,1)S(1)} %get-tuple-element, ...), custom_call_target="tpu_custom_call" | custom-call | flops 3000000000 | bytes 6000000 | tf_op jit(solution)/shard_map/inner/pallas_call | solution.py:278
  24.5 0.0 collective-permute-done.2.edge_b
  24.5 0.0 collective-permute-done.3.edge_a
  24.6 0.0 copy-done
  24.6 0.0 copy-done.1
  24.6 0.0 copy-done.2
  24.6 8.5 %net.1 = f32[1280,128]{1,0:T(8,128)} custom-call(f32[1]{0:T(128)S(6)} %copy.14.noise, bf16[34,8,256]{2,1,0:T(8,128)(2,1)S(1)} %get-tuple-element.35.sent_b, bf16[34,8,256]{2,1,0:T(8,128)(2,1)S(1)} %get-tuple-element.36.sent_a, bf16[34,8,256]{2,1,0:T(8,128)(2,1)S(1)} %collective-permute-done.2.edge_b, bf16[34,8,256]{2,1,0:T(8,128)(2,1)S(1)} %collective-permute-done.3.edge_a, ...), custom_call_target="tpu_custom_call" | custom-call | tf_op jit(solution)/shard_map/net/pallas_call | solution.py:389
  (3 shorter events, 0.1 us)
Async XLA Ops:
  2.8 8.4 %collective-permute-start = (bf16[2,9,8,256]{3,2,1,0:T(8,128)(2,1)S(1)}, bf16[2,9,8,256]{3,2,1,0:T(8,128)(2,1)S(1)}, u32[]{:S(2)}, u32[]{:S(2)}) collective-permute-start(bf16[2,9,8,256]{3,2,1,0:T(8,128)(2,1)S(1)} %get-tuple-element.29), channel_id=1, source_target_pairs={{1,2},{2,1},{5,6},{6,5},{9,10},{10,9},{13,14},{14,13},{17,18},{18,... | collective-permute-start | bytes 221192 | tf_op jit(solution)/shard_map/ppermute | solution.py:434
  9.1 2.2 %collective-permute-start.1 = (bf16[2,9,8,256]{3,2,1,0:T(8,128)(2,1)S(1)}, bf16[2,9,8,256]{3,2,1,0:T(8,128)(2,1)S(1)}, u32[]{:S(2)}, u32[]{:S(2)}) collective-permute-start(bf16[2,9,8,256]{3,2,1,0:T(8,128)(2,1)S(1)} %get-tuple-element.30), channel_id=1, source_target_pairs={{0,1},{1,0},{2,3},{3,2},{4,5},{5,4},{6,7},{7,6},{8,9},{9,8},{10,11... | collective-permute-start | bytes 221192 | tf_op jit(solution)/shard_map/ppermute | solution.py:434
  9.2 12.3 %collective-permute-start.4 = (bf16[9,64,256]{2,1,0:T(8,128)(2,1)S(1)}, bf16[9,64,256]{2,1,0:T(8,128)(2,1)S(1)}, u32[]{:S(2)}, u32[]{:S(2)}) collective-permute-start(bf16[9,64,256]{2,1,0:T(8,128)(2,1)S(1)} %get-tuple-element.39), channel_id=1, source_target_pairs={{1,2},{2,1},{5,6},{6,5},{9,10},{10,9},{13,14},{14,13},{17,18},{18,... | collective-permute-start | bytes 884744 | tf_op jit(solution)/shard_map/ppermute | solution.py:434
  11.1 10.4 %collective-permute-start.5 = (bf16[9,64,256]{2,1,0:T(8,128)(2,1)S(1)}, bf16[9,64,256]{2,1,0:T(8,128)(2,1)S(1)}, u32[]{:S(2)}, u32[]{:S(2)}) collective-permute-start(bf16[9,64,256]{2,1,0:T(8,128)(2,1)S(1)} %get-tuple-element.40), channel_id=1, source_target_pairs={{0,1},{1,0},{2,3},{3,2},{4,5},{5,4},{6,7},{7,6},{8,9},{9,8},{10,11... | collective-permute-start | bytes 884744 | tf_op jit(solution)/shard_map/ppermute | solution.py:434
  11.3 13.2 %collective-permute-start.2 = (bf16[34,8,256]{2,1,0:T(8,128)(2,1)S(1)}, bf16[34,8,256]{2,1,0:T(8,128)(2,1)S(1)}, u32[]{:S(2)}, u32[]{:S(2)}) collective-permute-start(bf16[34,8,256]{2,1,0:T(8,128)(2,1)S(1)} %get-tuple-element.35.sent_b), channel_id=1, source_target_pairs={{0,252},{1,253},{2,254},{3,255},{4,8},{5,9},{6,10},{7,11},{8,4},{9... | collective-permute-start | bytes 417800 | tf_op jit(solution)/shard_map/ppermute | solution.py:434
  20.0 4.6 %collective-permute-start.3 = (bf16[34,8,256]{2,1,0:T(8,128)(2,1)S(1)}, bf16[34,8,256]{2,1,0:T(8,128)(2,1)S(1)}, u32[]{:S(2)}, u32[]{:S(2)}) collective-permute-start(bf16[34,8,256]{2,1,0:T(8,128)(2,1)S(1)} %get-tuple-element.36.sent_a), channel_id=1, source_target_pairs={{0,4},{1,5},{2,6},{3,7},{4,0},{5,1},{6,2},{7,3},{8,12},{9,13},{10,... | collective-permute-start | bytes 417800 | tf_op jit(solution)/shard_map/ppermute | solution.py:434
  21.5 3.0 %copy-start = (f32[1,80,16,128]{3,2,1,0:T(8,128)S(1)}, f32[1,80,16,128]{3,2,1,0:T(8,128)}, u32[]{:S(2)}) copy-start(f32[1,80,16,128]{3,2,1,0:T(8,128)} %param.14) | copy-start | bytes 1966084
  21.5 3.0 %copy-start.1 = (f32[128]{0:T(128)S(1)}, f32[128]{0:T(128)}, u32[]{:S(2)}) copy-start(f32[128]{0:T(128)} %param.20) | copy-start | bytes 1540
  21.6 3.0 %copy-start.2 = (f32[128]{0:T(128)S(1)}, f32[128]{0:T(128)}, u32[]{:S(2)}) copy-start(f32[128]{0:T(128)} %param.21) | copy-start | bytes 1540

commit v7 on v6

--- a/solution.py
+++ b/solution.py
@@ -182,7 +182,16 @@
     return (lat > 0).astype(F32), (lat < n_lat - 1).astype(F32)
 
 
-def own_body(own_c, own_s, w_in, w_noisy, pooled, opening):
+def own_body(
+    own_c, own_s, w_in, w_noisy, k_coarse, k_block, k_branch, k_out,
+    w_coarse, w_block, w_branch, w_out, pooled, opening,
+    arrived,
+):
+    moves = [(k_coarse, w_coarse), (k_block, w_block), (k_branch, w_branch), (k_out, w_out.at[:, :CH, :])]
+    copies = [pltpu.make_async_copy(src, dst, arrived.at[n]) for n, (src, dst) in enumerate(moves)]
+    for copy in copies:
+        copy.start()
+    w_out[:, CH:, :] = jnp.zeros((9, 128 - CH, 128), BF16)
     mean = pool(own_c, w_in, 2, 12, PAIRS)
     for q in range(6):
         pooled[q * PITCH + EDGE : q * PITCH + EDGE + PAIRS, :] = mean[q].astype(BF16)
@@ -191,15 +200,22 @@
             for q in range(rows):
                 at = (row + q) * PITCH + EDGE
                 opening[at : at + PAIRS, 128 * half : 128 * half + 128] = v[q * PAIRS : (q + 1) * PAIRS]
+    for copy in copies:
+        copy.wait()
 
 
 def own_rows(*args):
     vm = pl.BlockSpec(memory_space=VMEM)
+    wide = lambda n, k: jax.ShapeDtypeStruct((9, n, k), BF16)
     return pl.pallas_call(
         own_body,
-        out_shape=(jax.ShapeDtypeStruct((6 * PITCH, 128), BF16), jax.ShapeDtypeStruct((14 * PITCH, 256), F32)),
-        in_specs=[vm] * len(args),
-        out_specs=[vm] * 2,
+        out_shape=(
+            wide(256, 128), wide(128, 128), wide(128, 128), wide(128, 128),
+            jax.ShapeDtypeStruct((6 * PITCH, 128), BF16), jax.ShapeDtypeStruct((14 * PITCH, 256), F32),
+        ),
+        in_specs=[vm] * 4 + [pl.BlockSpec(memory_space=pltpu.HBM)] * 4,
+        out_specs=[vm] * 6,
+        scratch_shapes=[pltpu.SemaphoreType.DMA((4,))],
         compiler_params=pltpu.CompilerParams(vmem_limit_bytes=12 << 20),
         cost_estimate=pl.CostEstimate(flops=2 * 10**9, bytes_accessed=3 * 10**6, transcendentals=5 * 10**5),
         name="own_rows",
@@ -209,18 +225,13 @@
 def inner_body(
     n_lat,
     own_c, own_s, lat_b, lat_a, w_in, w_noisy, pool_own, open_own,
-    k_coarse, k_deeper, k_guide, k_block, k_branch, k_out,
-    w_coarse, w_deeper, w_guide, w_block, w_branch, w_out, pooled, opening,
+    k_deeper, k_guide, w_deeper, w_guide, pooled, opening,
     x_c, x_s, arrived,
 ):
-    moves = [
-        (k_coarse, w_coarse), (k_deeper, w_deeper), (k_guide, w_guide),
-        (k_block, w_block), (k_branch, w_branch), (k_out, w_out.at[:, :CH, :]),
-    ]
+    moves = [(k_deeper, w_deeper), (k_guide, w_guide)]
     copies = [pltpu.make_async_copy(src, dst, arrived.at[n]) for n, (src, dst) in enumerate(moves)]
     for copy in copies:
         copy.start()
-    w_out[:, CH:, :] = jnp.zeros((9, 128 - CH, 128), BF16)
     top, bottom = band(n_lat)
     lat_even = lax.axis_index("lat") % 2 == 0
     free = 128 - CH
@@ -271,19 +282,18 @@
     vm = pl.BlockSpec(memory_space=VMEM)
     wide = lambda n, k: jax.ShapeDtypeStruct((9, n, k), BF16)
     out_shape = (
-        wide(256, 128), wide(256, 256), jax.ShapeDtypeStruct((128, 256), BF16),
-        wide(128, 128), wide(128, 128), wide(128, 128),
+        wide(256, 256), jax.ShapeDtypeStruct((128, 256), BF16),
         jax.ShapeDtypeStruct((16 * PITCH, 128), BF16), jax.ShapeDtypeStruct((22 * PITCH, 256), F32),
     )
     return pl.pallas_call(
         functools.partial(inner_body, n_lat),
         out_shape=out_shape,
-        in_specs=[vm] * 8 + [pl.BlockSpec(memory_space=pltpu.HBM)] * 6,
+        in_specs=[vm] * 8 + [pl.BlockSpec(memory_space=pltpu.HBM)] * 2,
         out_specs=[vm] * len(out_shape),
         scratch_shapes=[
             VMEM((24 * PAIRS, 256), BF16),
             VMEM((12 * PAIRS, 256), BF16),
-            pltpu.SemaphoreType.DMA((6,)),
+            pltpu.SemaphoreType.DMA((2,)),
         ],
         compiler_params=pltpu.CompilerParams(vmem_limit_bytes=20 << 20),
         cost_estimate=pl.CostEstimate(flops=3 * 10**9, bytes_accessed=6 * 10**6, transcendentals=10**6),
@@ -294,7 +304,7 @@
 def net_body(
     n_lat,
     noise, sent_b, sent_a, edge_b, edge_a, state, scale, shift,
-    w_in, w_noisy, w_coarse, w_deeper, w_guide, w_block, w_branch, w_out, pooled_in, opening,
+    w_in, w_noisy, w_coarse, w_block, w_branch, w_out, w_deeper, w_guide, pooled_in, opening,
     out, x_c, x_s, pooled, middle, guide, hidden, inner, mixed, turn,
 ):
     top, bottom = band(n_lat)
@@ -442,12 +452,15 @@
     sent_b, sent_a, now_c, now_s = lax.optimization_barrier((sent_b, sent_a, own_c, own_s))
     edge_b = permute(sent_b, None, "B")
     edge_a = permute(sent_a, None, "A")
-    during = own_rows(now_c, now_s, w_in, w_noisy)
-    weights = in_hbm(kernel_coarse, kernel_deeper, guide_weight, kernel_block, kernel_branch, kernel_output)
-    rest = inner(mesh_shape[1], own_c, own_s, lat_b, lat_a, w_in, w_noisy, *during, *weights)
+    *fetched, pool_own, open_own = own_rows(
+        now_c, now_s, w_in, w_noisy, *in_hbm(kernel_coarse, kernel_block, kernel_branch, kernel_output)
+    )
+    rest = inner(
+        mesh_shape[1], own_c, own_s, lat_b, lat_a, w_in, w_noisy, pool_own, open_own, *in_hbm(kernel_deeper, guide_weight)
+    )
     out = net(
         mesh_shape[1], noise_level, sent_b, sent_a, edge_b, edge_a, state,
-        time_scale[None], time_shift[None], w_in, w_noisy, *rest,
+        time_scale[None], time_shift[None], w_in, w_noisy, *fetched, *rest,
     )
     return out.reshape(noisy_state.shape)
 

time: 33.5 us -> 33.4 us (level)
  Pallas kernels: 15.2 us -> 14.6 us
    pallas_call x1, Pallas kernels: 2.96 us -> 1.95 us  [inner(): pl.pallas_call(functools.partial(inner_body, n_lat), out_shape=out_shape,...]
    pallas_call x1, Pallas kernels: 1.53 us -> 2.11 us  [own_rows(): pl.pallas_call(own_body, out_shape=(wide(256, 128), wide(128, 128), wide(...]
  transfers between devices with their start and end apart: 6 -> 6, of which waited for: 0 -> 1; matrix products, arithmetic and copies ran while one was open for 0% -> 0% of each run, Pallas kernels for 14% -> 12%
where the time goes in v7:
time: 33.4 us; the launch traced here: 32.8 us
  starting transfers between devices  17 us (51%)
  Pallas kernels  14.6 us (44%)
  between operations  0.82 us (2%)
    ppermute x6, starting transfers between devices, on_device(): lax.ppermute(value, AXES, swap_pairs(mesh_shape, a, o))  17 us
    pallas_call x1, Pallas kernels, net(): pl.pallas_call(functools.partial(net_body, n_lat), out_shape=jax.ShapeDty...  8.38 us
    pallas_call x1, Pallas kernels, prep(): pl.pallas_call(prep_body, out_shape=(own, own, edge, edge, small, small,...  2.19 us
    pallas_call x1, Pallas kernels, own_rows(): pl.pallas_call(own_body, out_shape=(wide(256, 128), wide(128, 128), wide(...  2.11 us
    pallas_call x1, Pallas kernels, inner(): pl.pallas_call(functools.partial(inner_body, n_lat), out_shape=out_shape,...  1.95 us
  transfers between devices with their start and end apart: 6, of which 1 were waited for; matrix products, arithmetic and copies ran while one was open for 0% of the time, Pallas kernels for 12%

profile of v7, /device:TPU:1, one launch (start us, length us, event | category | flops | bytes accessed | tf_op | source)
XLA Modules:
  0.0 32.8 jit_solution(13019031936107071135)
XLA Ops:
  0.7 2.2 %prep.1 = (bf16[1024,256]{1,0:T(8,128)(2,1)S(1)}, bf16[1024,256]{1,0:T(8,128)(2,1)S(1)}, bf16[16,8,256]{2,1,0:T(8,128)(2,1)S(1)}, bf16[16,8,256]{2,1,0:T(8,128)(...) custom-call(f32[1]{0:T(128)S(6)} %copy.14.noise, ...), custom_call_target="tpu_custom_call" | custom-call | tf_op jit(solution)/shard_map/prep/pallas_call | solution.py:119
  2.8 6.2 %collective-permute-start = (bf16[2,9,8,256]{3,2,1,0:T(8,128)(2,1)S(1)}, bf16[2,9,8,256]{3,2,1,0:T(8,128)(2,1)S(1)}, u32[]{:S(2)}, u32[]{:S(2)}) collective-permute-start(bf16[2,9,8,256]{3,2,1,0:T(8,128)(2,1)S(1)} %get-tuple-element.29), channel_id=1, source_target_pairs={{1,2},{2,1},{5,6},{6,5},{9,10},{10,9},{13,14},{14,13},{17,18},{18,... | collective-permute-start | bytes 221192 | tf_op jit(solution)/shard_map/ppermute | solution.py:444
  9.1 0.1 collective-permute-start.1
  9.2 1.9 %collective-permute-start.4 = (bf16[9,64,256]{2,1,0:T(8,128)(2,1)S(1)}, bf16[9,64,256]{2,1,0:T(8,128)(2,1)S(1)}, u32[]{:S(2)}, u32[]{:S(2)}) collective-permute-start(bf16[9,64,256]{2,1,0:T(8,128)(2,1)S(1)} %get-tuple-element.45), channel_id=1, source_target_pairs={{1,2},{2,1},{5,6},{6,5},{9,10},{10,9},{13,14},{14,13},{17,18},{18,... | collective-permute-start | bytes 884744 | tf_op jit(solution)/shard_map/ppermute | solution.py:444
  11.1 0.1 collective-permute-start.5
  11.2 0.0 collective-permute-done
  11.2 0.0 collective-permute-done.1
  11.3 8.6 %collective-permute-start.2 = (bf16[34,8,256]{2,1,0:T(8,128)(2,1)S(1)}, bf16[34,8,256]{2,1,0:T(8,128)(2,1)S(1)}, u32[]{:S(2)}, u32[]{:S(2)}) collective-permute-start(bf16[34,8,256]{2,1,0:T(8,128)(2,1)S(1)} %get-tuple-element.35.sent_b), channel_id=1, source_target_pairs={{0,252},{1,253},{2,254},{3,255},{4,8},{5,9},{6,10},{7,11},{8,4},{9... | collective-permute-start | bytes 417800 | tf_op jit(solution)/shard_map/ppermute | solution.py:444
  20.0 0.0 collective-permute-start.3
  20.0 2.1 %own_rows.1 = (bf16[9,256,128]{2,1,0:T(8,128)(2,1)S(1)}, bf16[9,128,128]{2,1,0:T(8,128)(2,1)S(1)}, bf16[9,128,128]{2,1,0:T(8,128)(2,1)S(1)}, bf16[9,128,128]{2,1...) custom-call(bf16[1024,256]{1,0:T(8,128)(2,1)S(1)} %get-tuple-element.39.own_c, ...), custom_call_target="tpu_custom_call" | custom-call | flops 2000000000 | bytes 3000000 | tf_op jit(solution)/shard_map/own_rows/pallas_call | solution.py:210
  22.1 0.0 collective-permute-done.4.lat_b
  22.1 0.0 collective-permute-done.5.lat_a
  22.1 0.0 copy-start
  22.1 0.0 copy-start.1
  22.1 0.0 copy-start.2
  22.1 2.0 %inner.1 = (bf16[9,256,256]{2,1,0:T(8,128)(2,1)S(1)}, bf16[128,256]{1,0:T(8,128)(2,1)S(1)}, bf16[1152,128]{1,0:T(8,128)(2,1)S(1)}, f32[1584,256]{1,0:T(8,128)S(1)}) custom-call(bf16[1024,256]{1,0:T(8,128)(2,1)S(1)} %get-tuple-element.39.own_c, bf16[1024,256]{1,0:T(8,128)(2,1)S(1)} %get-tuple-element.40.own_s, ...), custom_call_target="tpu_custom_call" | custom-call | flops 3000000000 | bytes 6000000 | tf_op jit(solution)/shard_map/inner/pallas_call | solution.py:288
  24.1 0.0 collective-permute-done.2.edge_b
  24.1 0.3 collective-permute-done.3.edge_a
  24.4 0.0 copy-done
  24.4 0.0 copy-done.1
  24.4 0.0 copy-done.2
  24.4 8.4 %net.1 = f32[1280,128]{1,0:T(8,128)} custom-call(f32[1]{0:T(128)S(6)} %copy.14.noise, bf16[34,8,256]{2,1,0:T(8,128)(2,1)S(1)} %get-tuple-element.35.sent_b, bf16[34,8,256]{2,1,0:T(8,128)(2,1)S(1)} %get-tuple-element.36.sent_a, bf16[34,8,256]{2,1,0:T(8,128)(2,1)S(1)} %collective-permute-done.2.edge_b, bf16[34,8,256]{2,1,0:T(8,128)(2,1)S(1)} %collective-permute-done.3.edge_a, ...), custom_call_target="tpu_custom_call" | custom-call | tf_op jit(solution)/shard_map/net/pallas_call | solution.py:399
  (3 shorter events, 0.1 us)
Async XLA Ops:
  2.8 8.4 %collective-permute-start = (bf16[2,9,8,256]{3,2,1,0:T(8,128)(2,1)S(1)}, bf16[2,9,8,256]{3,2,1,0:T(8,128)(2,1)S(1)}, u32[]{:S(2)}, u32[]{:S(2)}) collective-permute-start(bf16[2,9,8,256]{3,2,1,0:T(8,128)(2,1)S(1)} %get-tuple-element.29), channel_id=1, source_target_pairs={{1,2},{2,1},{5,6},{6,5},{9,10},{10,9},{13,14},{14,13},{17,18},{18,... | collective-permute-start | bytes 221192 | tf_op jit(solution)/shard_map/ppermute | solution.py:444
  9.1 2.2 %collective-permute-start.1 = (bf16[2,9,8,256]{3,2,1,0:T(8,128)(2,1)S(1)}, bf16[2,9,8,256]{3,2,1,0:T(8,128)(2,1)S(1)}, u32[]{:S(2)}, u32[]{:S(2)}) collective-permute-start(bf16[2,9,8,256]{3,2,1,0:T(8,128)(2,1)S(1)} %get-tuple-element.30), channel_id=1, source_target_pairs={{0,1},{1,0},{2,3},{3,2},{4,5},{5,4},{6,7},{7,6},{8,9},{9,8},{10,11... | collective-permute-start | bytes 221192 | tf_op jit(solution)/shard_map/ppermute | solution.py:444
  9.2 12.9 %collective-permute-start.4 = (bf16[9,64,256]{2,1,0:T(8,128)(2,1)S(1)}, bf16[9,64,256]{2,1,0:T(8,128)(2,1)S(1)}, u32[]{:S(2)}, u32[]{:S(2)}) collective-permute-start(bf16[9,64,256]{2,1,0:T(8,128)(2,1)S(1)} %get-tuple-element.45), channel_id=1, source_target_pairs={{1,2},{2,1},{5,6},{6,5},{9,10},{10,9},{13,14},{14,13},{17,18},{18,... | collective-permute-start | bytes 884744 | tf_op jit(solution)/shard_map/ppermute | solution.py:444
  11.1 11.0 %collective-permute-start.5 = (bf16[9,64,256]{2,1,0:T(8,128)(2,1)S(1)}, bf16[9,64,256]{2,1,0:T(8,128)(2,1)S(1)}, u32[]{:S(2)}, u32[]{:S(2)}) collective-permute-start(bf16[9,64,256]{2,1,0:T(8,128)(2,1)S(1)} %get-tuple-element.46), channel_id=1, source_target_pairs={{0,1},{1,0},{2,3},{3,2},{4,5},{5,4},{6,7},{7,6},{8,9},{9,8},{10,11... | collective-permute-start | bytes 884744 | tf_op jit(solution)/shard_map/ppermute | solution.py:444
  11.3 12.8 %collective-permute-start.2 = (bf16[34,8,256]{2,1,0:T(8,128)(2,1)S(1)}, bf16[34,8,256]{2,1,0:T(8,128)(2,1)S(1)}, u32[]{:S(2)}, u32[]{:S(2)}) collective-permute-start(bf16[34,8,256]{2,1,0:T(8,128)(2,1)S(1)} %get-tuple-element.35.sent_b), channel_id=1, source_target_pairs={{0,252},{1,253},{2,254},{3,255},{4,8},{5,9},{6,10},{7,11},{8,4},{9... | collective-permute-start | bytes 417800 | tf_op jit(solution)/shard_map/ppermute | solution.py:444
  20.0 4.5 %collective-permute-start.3 = (bf16[34,8,256]{2,1,0:T(8,128)(2,1)S(1)}, bf16[34,8,256]{2,1,0:T(8,128)(2,1)S(1)}, u32[]{:S(2)}, u32[]{:S(2)}) collective-permute-start(bf16[34,8,256]{2,1,0:T(8,128)(2,1)S(1)} %get-tuple-element.36.sent_a), channel_id=1, source_target_pairs={{0,4},{1,5},{2,6},{3,7},{4,0},{5,1},{6,2},{7,3},{8,12},{9,13},{10,... | collective-permute-start | bytes 417800 | tf_op jit(solution)/shard_map/ppermute | solution.py:444
  22.1 2.3 %copy-start = (f32[1,80,16,128]{3,2,1,0:T(8,128)S(1)}, f32[1,80,16,128]{3,2,1,0:T(8,128)}, u32[]{:S(2)}) copy-start(f32[1,80,16,128]{3,2,1,0:T(8,128)} %param.14) | copy-start | bytes 1966084
  22.1 2.3 %copy-start.1 = (f32[128]{0:T(128)S(1)}, f32[128]{0:T(128)}, u32[]{:S(2)}) copy-start(f32[128]{0:T(128)} %param.20) | copy-start | bytes 1540
  22.1 2.3 %copy-start.2 = (f32[128]{0:T(128)S(1)}, f32[128]{0:T(128)}, u32[]{:S(2)}) copy-start(f32[128]{0:T(128)} %param.21) | copy-start | bytes 1540

commit v8 on v7

--- a/solution.py
+++ b/solution.py
@@ -354,7 +354,7 @@
         pooled[at : at + 8, :] = jnp.where(place < 5, pltpu.roll(v[:8], 7, 0), first).astype(BF16)
         last = pooled_in[at + 64 : at + 72, :].astype(F32)
         pooled[at + 64 : at + 72, :] = jnp.where(place > 2, pltpu.roll(v[8:], 1, 0), last).astype(BF16)
-    for row, rows in ((0, 14),):
+    for row, rows in ((0, 8), (8, 6)):
         put(middle, row, rows, silu(half_conv(pooled, w_coarse, row + 1, rows)), 3, 11)
     embedded = scale[...] * noise_code + shift[...]
     for row, rows in ((0, 6), (6, 6)):

time: 33.4 us -> 33.3 us (level)
  no operation moved by 1% of the time
where the time goes in v8:
time: 33.3 us; the launch traced here: 32.7 us
  starting transfers between devices  17 us (51%)
  Pallas kernels  14.5 us (44%)
  between operations  0.82 us (2%)
    ppermute x6, starting transfers between devices, on_device(): lax.ppermute(value, AXES, swap_pairs(mesh_shape, a, o))  17 us
    pallas_call x1, Pallas kernels, net(): pl.pallas_call(functools.partial(net_body, n_lat), out_shape=jax.ShapeDty...  8.29 us
    pallas_call x1, Pallas kernels, prep(): pl.pallas_call(prep_body, out_shape=(own, own, edge, edge, small, small,...  2.19 us
    pallas_call x1, Pallas kernels, own_rows(): pl.pallas_call(own_body, out_shape=(wide(256, 128), wide(128, 128), wide(...  2.11 us
    pallas_call x1, Pallas kernels, inner(): pl.pallas_call(functools.partial(inner_body, n_lat), out_shape=out_shape,...  1.95 us
  transfers between devices with their start and end apart: 6, of which 1 were waited for; matrix products, arithmetic and copies ran while one was open for 0% of the time, Pallas kernels for 12%

profile of v8, /device:TPU:1, one launch (start us, length us, event | category | flops | bytes accessed | tf_op | source)
XLA Modules:
  0.0 32.7 jit_solution(7091081809461009113)
XLA Ops:
  0.7 2.2 %prep.1 = (bf16[1024,256]{1,0:T(8,128)(2,1)S(1)}, bf16[1024,256]{1,0:T(8,128)(2,1)S(1)}, bf16[16,8,256]{2,1,0:T(8,128)(2,1)S(1)}, bf16[16,8,256]{2,1,0:T(8,128)(...) custom-call(f32[1]{0:T(128)S(6)} %copy.14.noise, ...), custom_call_target="tpu_custom_call" | custom-call | tf_op jit(solution)/shard_map/prep/pallas_call | solution.py:119
  2.8 6.2 %collective-permute-start = (bf16[2,9,8,256]{3,2,1,0:T(8,128)(2,1)S(1)}, bf16[2,9,8,256]{3,2,1,0:T(8,128)(2,1)S(1)}, u32[]{:S(2)}, u32[]{:S(2)}) collective-permute-start(bf16[2,9,8,256]{3,2,1,0:T(8,128)(2,1)S(1)} %get-tuple-element.29), channel_id=1, source_target_pairs={{1,2},{2,1},{5,6},{6,5},{9,10},{10,9},{13,14},{14,13},{17,18},{18,... | collective-permute-start | bytes 221192 | tf_op jit(solution)/shard_map/ppermute | solution.py:444
  9.1 0.1 collective-permute-start.1
  9.2 1.9 %collective-permute-start.4 = (bf16[9,64,256]{2,1,0:T(8,128)(2,1)S(1)}, bf16[9,64,256]{2,1,0:T(8,128)(2,1)S(1)}, u32[]{:S(2)}, u32[]{:S(2)}) collective-permute-start(bf16[9,64,256]{2,1,0:T(8,128)(2,1)S(1)} %get-tuple-element.45), channel_id=1, source_target_pairs={{1,2},{2,1},{5,6},{6,5},{9,10},{10,9},{13,14},{14,13},{17,18},{18,... | collective-permute-start | bytes 884744 | tf_op jit(solution)/shard_map/ppermute | solution.py:444
  11.1 0.1 collective-permute-start.5
  11.2 0.0 collective-permute-done
  11.2 0.0 collective-permute-done.1
  11.3 8.6 %collective-permute-start.2 = (bf16[34,8,256]{2,1,0:T(8,128)(2,1)S(1)}, bf16[34,8,256]{2,1,0:T(8,128)(2,1)S(1)}, u32[]{:S(2)}, u32[]{:S(2)}) collective-permute-start(bf16[34,8,256]{2,1,0:T(8,128)(2,1)S(1)} %get-tuple-element.35.sent_b), channel_id=1, source_target_pairs={{0,252},{1,253},{2,254},{3,255},{4,8},{5,9},{6,10},{7,11},{8,4},{9... | collective-permute-start | bytes 417800 | tf_op jit(solution)/shard_map/ppermute | solution.py:444
  20.0 0.0 collective-permute-start.3
  20.0 2.1 %own_rows.1 = (bf16[9,256,128]{2,1,0:T(8,128)(2,1)S(1)}, bf16[9,128,128]{2,1,0:T(8,128)(2,1)S(1)}, bf16[9,128,128]{2,1,0:T(8,128)(2,1)S(1)}, bf16[9,128,128]{2,1...) custom-call(bf16[1024,256]{1,0:T(8,128)(2,1)S(1)} %get-tuple-element.39.own_c, ...), custom_call_target="tpu_custom_call" | custom-call | flops 2000000000 | bytes 3000000 | tf_op jit(solution)/shard_map/own_rows/pallas_call | solution.py:210
  22.1 0.0 collective-permute-done.4.lat_b
  22.1 0.0 collective-permute-done.5.lat_a
  22.1 0.0 copy-start
  22.1 0.0 copy-start.1
  22.1 0.0 copy-start.2
  22.1 2.0 %inner.1 = (bf16[9,256,256]{2,1,0:T(8,128)(2,1)S(1)}, bf16[128,256]{1,0:T(8,128)(2,1)S(1)}, bf16[1152,128]{1,0:T(8,128)(2,1)S(1)}, f32[1584,256]{1,0:T(8,128)S(1)}) custom-call(bf16[1024,256]{1,0:T(8,128)(2,1)S(1)} %get-tuple-element.39.own_c, bf16[1024,256]{1,0:T(8,128)(2,1)S(1)} %get-tuple-element.40.own_s, ...), custom_call_target="tpu_custom_call" | custom-call | flops 3000000000 | bytes 6000000 | tf_op jit(solution)/shard_map/inner/pallas_call | solution.py:288
  24.1 0.0 collective-permute-done.2.edge_b
  24.1 0.3 collective-permute-done.3.edge_a
  24.4 0.0 copy-done
  24.4 0.0 copy-done.1
  24.4 0.0 copy-done.2
  24.4 8.3 %net.1 = f32[1280,128]{1,0:T(8,128)} custom-call(f32[1]{0:T(128)S(6)} %copy.14.noise, bf16[34,8,256]{2,1,0:T(8,128)(2,1)S(1)} %get-tuple-element.35.sent_b, bf16[34,8,256]{2,1,0:T(8,128)(2,1)S(1)} %get-tuple-element.36.sent_a, bf16[34,8,256]{2,1,0:T(8,128)(2,1)S(1)} %collective-permute-done.2.edge_b, bf16[34,8,256]{2,1,0:T(8,128)(2,1)S(1)} %collective-permute-done.3.edge_a, ...), custom_call_target="tpu_custom_call" | custom-call | tf_op jit(solution)/shard_map/net/pallas_call | solution.py:399
  (3 shorter events, 0.1 us)
Async XLA Ops:
  2.8 8.4 %collective-permute-start = (bf16[2,9,8,256]{3,2,1,0:T(8,128)(2,1)S(1)}, bf16[2,9,8,256]{3,2,1,0:T(8,128)(2,1)S(1)}, u32[]{:S(2)}, u32[]{:S(2)}) collective-permute-start(bf16[2,9,8,256]{3,2,1,0:T(8,128)(2,1)S(1)} %get-tuple-element.29), channel_id=1, source_target_pairs={{1,2},{2,1},{5,6},{6,5},{9,10},{10,9},{13,14},{14,13},{17,18},{18,... | collective-permute-start | bytes 221192 | tf_op jit(solution)/shard_map/ppermute | solution.py:444
  9.1 2.2 %collective-permute-start.1 = (bf16[2,9,8,256]{3,2,1,0:T(8,128)(2,1)S(1)}, bf16[2,9,8,256]{3,2,1,0:T(8,128)(2,1)S(1)}, u32[]{:S(2)}, u32[]{:S(2)}) collective-permute-start(bf16[2,9,8,256]{3,2,1,0:T(8,128)(2,1)S(1)} %get-tuple-element.30), channel_id=1, source_target_pairs={{0,1},{1,0},{2,3},{3,2},{4,5},{5,4},{6,7},{7,6},{8,9},{9,8},{10,11... | collective-permute-start | bytes 221192 | tf_op jit(solution)/shard_map/ppermute | solution.py:444
  9.2 12.9 %collective-permute-start.4 = (bf16[9,64,256]{2,1,0:T(8,128)(2,1)S(1)}, bf16[9,64,256]{2,1,0:T(8,128)(2,1)S(1)}, u32[]{:S(2)}, u32[]{:S(2)}) collective-permute-start(bf16[9,64,256]{2,1,0:T(8,128)(2,1)S(1)} %get-tuple-element.45), channel_id=1, source_target_pairs={{1,2},{2,1},{5,6},{6,5},{9,10},{10,9},{13,14},{14,13},{17,18},{18,... | collective-permute-start | bytes 884744 | tf_op jit(solution)/shard_map/ppermute | solution.py:444
  11.1 11.0 %collective-permute-start.5 = (bf16[9,64,256]{2,1,0:T(8,128)(2,1)S(1)}, bf16[9,64,256]{2,1,0:T(8,128)(2,1)S(1)}, u32[]{:S(2)}, u32[]{:S(2)}) collective-permute-start(bf16[9,64,256]{2,1,0:T(8,128)(2,1)S(1)} %get-tuple-element.46), channel_id=1, source_target_pairs={{0,1},{1,0},{2,3},{3,2},{4,5},{5,4},{6,7},{7,6},{8,9},{9,8},{10,11... | collective-permute-start | bytes 884744 | tf_op jit(solution)/shard_map/ppermute | solution.py:444
  11.3 12.8 %collective-permute-start.2 = (bf16[34,8,256]{2,1,0:T(8,128)(2,1)S(1)}, bf16[34,8,256]{2,1,0:T(8,128)(2,1)S(1)}, u32[]{:S(2)}, u32[]{:S(2)}) collective-permute-start(bf16[34,8,256]{2,1,0:T(8,128)(2,1)S(1)} %get-tuple-element.35.sent_b), channel_id=1, source_target_pairs={{0,252},{1,253},{2,254},{3,255},{4,8},{5,9},{6,10},{7,11},{8,4},{9... | collective-permute-start | bytes 417800 | tf_op jit(solution)/shard_map/ppermute | solution.py:444
  20.0 4.5 %collective-permute-start.3 = (bf16[34,8,256]{2,1,0:T(8,128)(2,1)S(1)}, bf16[34,8,256]{2,1,0:T(8,128)(2,1)S(1)}, u32[]{:S(2)}, u32[]{:S(2)}) collective-permute-start(bf16[34,8,256]{2,1,0:T(8,128)(2,1)S(1)} %get-tuple-element.36.sent_a), channel_id=1, source_target_pairs={{0,4},{1,5},{2,6},{3,7},{4,0},{5,1},{6,2},{7,3},{8,12},{9,13},{10,... | collective-permute-start | bytes 417800 | tf_op jit(solution)/shard_map/ppermute | solution.py:444
  22.1 2.3 %copy-start = (f32[1,80,16,128]{3,2,1,0:T(8,128)S(1)}, f32[1,80,16,128]{3,2,1,0:T(8,128)}, u32[]{:S(2)}) copy-start(f32[1,80,16,128]{3,2,1,0:T(8,128)} %param.14) | copy-start | bytes 1966084
  22.1 2.3 %copy-start.1 = (f32[128]{0:T(128)S(1)}, f32[128]{0:T(128)}, u32[]{:S(2)}) copy-start(f32[128]{0:T(128)} %param.20) | copy-start | bytes 1540
  22.1 2.3 %copy-start.2 = (f32[128]{0:T(128)S(1)}, f32[128]{0:T(128)}, u32[]{:S(2)}) copy-start(f32[128]{0:T(128)} %param.21) | copy-start | bytes 1540
